TPU v7x, 32 devices: a whole 2x2x4 slice. The times are simulated.
32 devices in a mesh: dp: 8 (over z, y), tensor: 4 (over x, core).
Axes of the slice: x: 2, y: 2, z: 4, core: 2. Of those that a mesh axis runs over, the one named last changes fastest.
Arguments:
- tokens: bfloat16 [8192, 2048], P('dp', 'tensor'), may hold values from -6 to 6
- segments: int32 [8, 1024], P('dp'), may hold values from 0 to 3, never falling along the last dimension, each value on 1 to 512 neighbouring positions
- cotangent: bfloat16 [8192, 2048], P('dp', 'tensor'), may hold values from -6 to 6
- w_query: bfloat16 [2048, 2048], P(None, 'tensor'), may hold values from -1 to 1
- w_key: bfloat16 [2048, 2048], P(None, 'tensor'), may hold values from -1 to 1
- w_value: bfloat16 [2048, 2048], P(None, 'tensor'), may hold values from -0.125 to 0.125
- w_out: bfloat16 [2048, 2048], P('tensor'), may hold values from -0.125 to 0.125
- w_gate: bfloat16 [2048, 8192], P(None, 'tensor'), may hold values from -0.125 to 0.125
- w_up: bfloat16 [2048, 8192], P(None, 'tensor'), may hold values from -0.125 to 0.125
- w_down: bfloat16 [8192, 2048], P('tensor'), may hold values from -0.0625 to 0.0625
- gain_query: float32 [2048], P('tensor'), may hold values from 0.1 to 1.9
- gain_key: float32 [2048], P('tensor'), may hold values from 0.1 to 1.9
- gain_attn: float32 [2048], replicated, may hold values from 0.1 to 1.9
- gain_mlp: float32 [2048], replicated, may hold values from 0.1 to 1.9
Outputs:
- output: bfloat16 [8192, 2048], P('dp', 'tensor')
- input_grad: bfloat16 [8192, 2048], P('dp', 'tensor')
- w_query_grad: float32 [2048, 2048], P(None, 'tensor')
- w_key_grad: float32 [2048, 2048], P(None, 'tensor')
- w_value_grad: float32 [2048, 2048], P(None, 'tensor')
- w_out_grad: float32 [2048, 2048], P('tensor')
- w_gate_grad: float32 [2048, 8192], P(None, 'tensor')
- w_up_grad: float32 [2048, 8192], P(None, 'tensor')
- w_down_grad: float32 [8192, 2048], P('tensor')
- gain_query_grad: float32 [2048], P('tensor')
- gain_key_grad: float32 [2048], P('tensor')
- gain_attn_grad: float32 [2048], replicated
- gain_mlp_grad: float32 [2048], replicated
Inputs may be any that keep to these rules, and one draw needn't show every extreme that they name: `segments`: along each sequence the segment numbers never fall; a document is a run of equal numbers, at most 512 tokens long, and some document has exactly that length.
All inputs are finite; a program needn't handle non-finite values.
Results may differ from a plain program's by a relative error of at most 0.025.
Values may be sent and summed in bfloat16 or wider, within the bound.
No kernel may reach another device: no remote copies, remote signals or barrier semaphores. Data moves between devices by JAX's collectives and lax.ppermute only.
A program may use at most 256 MiB of HBM per device.

v0:
```python
import jax
import jax.numpy as jnp
from jax import lax
from jax.sharding import PartitionSpec as P

HD = 128


epsilon = 1e-06
rope_base = 500000.0


def tables(segments):
    length = segments.shape[-1]
    places = jnp.broadcast_to(jnp.arange(length, dtype=jnp.int32), segments.shape)
    starts = jnp.concatenate(
        [jnp.ones(segments.shape[:-1] + (1,), dtype=bool), segments[..., 1:] != segments[..., :-1]],
        axis=-1,
    )
    firsts = lax.cummax(jnp.where(starts, places, 0), axis=segments.ndim - 1)
    offsets = (places - firsts).astype(jnp.float32)
    freqs = jnp.power(rope_base, -jnp.arange(0, HD, 2).astype(jnp.float32) / HD)
    angles = offsets[..., None] * freqs
    angles = jnp.concatenate([angles, angles], axis=-1)
    return (jnp.cos(angles), jnp.sin(angles))


def rotate(values, cosine, sine_table):
    half_dim = values.shape[-1] // 2
    turned = jnp.concatenate([-values[..., half_dim:], values[..., :half_dim]], axis=-1)
    return values * cosine + turned * sine_table


def rotate_back(gradient, cosine, sine_table):
    half_dim = gradient.shape[-1] // 2
    scaled = gradient * sine_table
    return gradient * cosine + jnp.concatenate(
        [scaled[..., half_dim:], -scaled[..., :half_dim]], axis=-1
    )


def column_sum(partial_value):
    return lax.psum_scatter(
        partial_value.astype(jnp.bfloat16), "tensor", scatter_dimension=1, tiled=True
    ).astype(jnp.float32)


def body(
    tokens,
    segments,
    cotangent,
    w_query,
    w_key,
    w_value,
    w_out,
    w_gate,
    w_up,
    w_down,
    gain_query,
    gain_key,
    gain_attn,
    gain_mlp,
):
    full_width = w_query.shape[0]
    row_count = tokens.shape[0]
    narrow = tokens.shape[1]
    local_width = w_query.shape[1]
    heads_here = local_width // HD
    tensor_rank = lax.axis_index("tensor")
    col_start = tensor_rank * narrow
    block_rows = min(512, row_count)
    block_count = row_count // block_rows
    score_scale = HD ** (-0.5)
    cosine, sine_table = tables(segments)
    cosine = cosine[0][:, None, :]
    sine_table = sine_table[0][:, None, :]
    doc_ids = segments[0]
    position = jnp.arange(row_count)
    gain_mlp_cols = lax.dynamic_slice_in_dim(gain_mlp, col_start, narrow, 0)
    whole_x, whole_dy = (
        lax.all_gather(tokens, "tensor", axis=1, tiled=True),
        lax.all_gather(cotangent, "tensor", axis=1, tiled=True),
    )
    query_proj = jnp.dot(whole_x, w_query, preferred_element_type=jnp.float32)
    key_proj = jnp.dot(whole_x, w_key, preferred_element_type=jnp.float32)
    value_proj = jnp.dot(whole_x, w_value, preferred_element_type=jnp.float32)
    query_sq, key_sq = lax.psum(
        (jnp.sum(query_proj * query_proj, 1), jnp.sum(key_proj * key_proj, 1)), "tensor"
    )
    query_scale = lax.rsqrt(query_sq / full_width + epsilon)[:, None]
    key_scale = lax.rsqrt(key_sq / full_width + epsilon)[:, None]
    query_rot = rotate(
        (query_proj * query_scale * gain_query).reshape(row_count, heads_here, HD),
        cosine,
        sine_table,
    ).astype(jnp.bfloat16)
    key_rot = rotate(
        (key_proj * key_scale * gain_key).reshape(row_count, heads_here, HD), cosine, sine_table
    ).astype(jnp.bfloat16)
    value_low = value_proj.astype(jnp.bfloat16).reshape(row_count, heads_here, HD)

    def scores_for(row_start):
        query_block = lax.dynamic_slice_in_dim(query_rot, row_start, block_rows, 0)
        ahead_rows = row_start + jnp.arange(block_rows)
        block_docs = lax.dynamic_slice_in_dim(doc_ids, row_start, block_rows, 0)
        allowed = (block_docs[:, None] == doc_ids[None, :]) & (
            ahead_rows[:, None] >= position[None, :]
        )
        scores = (
            jnp.einsum("qhd,khd->hqk", query_block, key_rot, preferred_element_type=jnp.float32)
            * score_scale
        )
        return (query_block, jnp.where(allowed[None], scores, -1e30))

    def attend_block(block_index):
        query_block, scores = scores_for(block_index * block_rows)
        row_max = jnp.max(scores, -1, keepdims=True)
        exp_terms = jnp.exp(scores - row_max)
        row_total = jnp.sum(exp_terms, -1, keepdims=True)
        weights = (exp_terms / row_total).astype(jnp.bfloat16)
        mixed_block = jnp.einsum(
            "hqk,khd->qhd", weights, value_low, preferred_element_type=jnp.float32
        )
        return (mixed_block, (row_max + jnp.log(row_total))[..., 0])

    mixed_out, log_sums = lax.map(attend_block, jnp.arange(block_count))
    mixed_low = mixed_out.reshape(row_count, local_width).astype(jnp.bfloat16)
    attn_part = jnp.dot(mixed_low, w_out, preferred_element_type=jnp.float32)
    attn_total = lax.psum(attn_part.astype(jnp.bfloat16), "tensor").astype(jnp.float32)
    attn_scale = lax.rsqrt(
        jnp.sum(attn_total * attn_total, 1, keepdims=True) / full_width + epsilon
    )
    hidden = whole_x.astype(jnp.float32) + attn_total * attn_scale * gain_attn
    hidden_low = hidden.astype(jnp.bfloat16)
    hidden_cols = lax.dynamic_slice_in_dim(hidden, col_start, narrow, 1)
    gate_proj = jnp.dot(hidden_low, w_gate, preferred_element_type=jnp.float32)
    up_proj = jnp.dot(hidden_low, w_up, preferred_element_type=jnp.float32)
    gate_silu = jax.nn.silu(gate_proj)
    act_low = (gate_silu * up_proj).astype(jnp.bfloat16)
    branch_part = jnp.dot(act_low, w_down, preferred_element_type=jnp.float32)
    branch = lax.psum(branch_part.astype(jnp.bfloat16), "tensor").astype(jnp.float32)
    branch_scale = lax.rsqrt(jnp.sum(branch * branch, 1, keepdims=True) / full_width + epsilon)
    branch_own = lax.dynamic_slice_in_dim(branch, col_start, narrow, 1)
    output = (hidden_cols + branch_own * branch_scale * gain_mlp_cols).astype(jnp.bfloat16)
    dy_full = whole_dy.astype(jnp.float32)
    gained = gain_mlp * dy_full
    row_inner = jnp.sum(gained * branch, 1, keepdims=True)
    branch_low = (
        branch_scale * gained - branch * branch_scale**3 / full_width * row_inner
    ).astype(jnp.bfloat16)
    owner_mask = jnp.arange(full_width) // narrow == tensor_rank
    gain_mlp_part = jnp.where(owner_mask, jnp.sum(dy_full * branch * branch_scale, 0), 0.0)
    down_wgrad = jnp.einsum("tf,td->fd", act_low, branch_low, preferred_element_type=jnp.float32)
    act_grad = jnp.einsum("td,fd->tf", branch_low, w_down, preferred_element_type=jnp.float32)
    sigma = jax.nn.sigmoid(gate_proj)
    gate_low = (act_grad * up_proj * sigma * (1.0 + gate_proj * (1.0 - sigma))).astype(jnp.bfloat16)
    up_low = (act_grad * gate_silu).astype(jnp.bfloat16)
    gate_wgrad = jnp.einsum("td,tf->df", hidden_low, gate_low, preferred_element_type=jnp.float32)
    up_wgrad = jnp.einsum("td,tf->df", hidden_low, up_low, preferred_element_type=jnp.float32)
    hidden_part = jnp.einsum(
        "tf,df->td", gate_low, w_gate, preferred_element_type=jnp.float32
    ) + jnp.einsum("tf,df->td", up_low, w_up, preferred_element_type=jnp.float32)
    hidden_sum, gain_mlp_grad = (
        lax.psum(hidden_part.astype(jnp.bfloat16), "tensor").astype(jnp.float32),
        lax.psum(gain_mlp_part.astype(jnp.bfloat16), "tensor").astype(jnp.float32),
    )
    hidden_grad = dy_full + hidden_sum
    gained_attn = gain_attn * hidden_grad
    attn_inner = jnp.sum(gained_attn * attn_total, 1, keepdims=True)
    attn_low = (
        attn_scale * gained_attn - attn_total * attn_scale**3 / full_width * attn_inner
    ).astype(jnp.bfloat16)
    gain_attn_grad = jnp.sum(hidden_grad * attn_total * attn_scale, 0)
    grad_own = lax.dynamic_slice_in_dim(hidden_grad, col_start, narrow, 1)
    out_wgrad = jnp.einsum("tc,td->cd", mixed_low, attn_low, preferred_element_type=jnp.float32)
    mixed_grad = (
        jnp.einsum("td,cd->tc", attn_low, w_out, preferred_element_type=jnp.float32)
        .astype(jnp.bfloat16)
        .reshape(row_count, heads_here, HD)
    )

    def attend_back(carry, block_index):
        key_acc, value_acc = carry
        row_start = block_index * block_rows
        query_block, scores = scores_for(row_start)
        grad_block = lax.dynamic_slice_in_dim(mixed_grad, row_start, block_rows, 0)
        probs = jnp.exp(scores - log_sums[block_index][..., None])
        probs_low = probs.astype(jnp.bfloat16)
        prob_grad = jnp.einsum(
            "qhd,khd->hqk", grad_block, value_low, preferred_element_type=jnp.float32
        )
        row_dot = jnp.sum(probs * prob_grad, -1, keepdims=True)
        score_low = (probs * (prob_grad - row_dot)).astype(jnp.bfloat16)
        query_part = (
            jnp.einsum("hqk,khd->qhd", score_low, key_rot, preferred_element_type=jnp.float32)
            * score_scale
        )
        key_acc = (
            key_acc
            + jnp.einsum("hqk,qhd->khd", score_low, query_block, preferred_element_type=jnp.float32)
            * score_scale
        )
        value_acc = value_acc + jnp.einsum(
            "hqk,qhd->khd", probs_low, grad_block, preferred_element_type=jnp.float32
        )
        return ((key_acc, value_acc), query_part)

    zero_acc = jnp.zeros((row_count, heads_here, HD), jnp.float32)
    (key_grad, value_grad), query_grad = lax.scan(
        attend_back, (zero_acc, zero_acc), jnp.arange(block_count)
    )
    query_grad = query_grad.reshape(row_count, heads_here, HD)
    query_normed_grad = rotate_back(query_grad, cosine, sine_table).reshape(row_count, local_width)
    key_normed_grad = rotate_back(key_grad, cosine, sine_table).reshape(row_count, local_width)
    gain_query_grad = jnp.sum(query_normed_grad * query_proj * query_scale, 0)
    gain_key_grad = jnp.sum(key_normed_grad * key_proj * key_scale, 0)
    query_gained = gain_query * query_normed_grad
    key_gained = gain_key * key_normed_grad
    query_dot, key_dot = lax.psum(
        (jnp.sum(query_gained * query_proj, 1), jnp.sum(key_gained * key_proj, 1)), "tensor"
    )
    query_low = (
        query_scale * query_gained - query_proj * query_scale**3 / full_width * query_dot[:, None]
    ).astype(jnp.bfloat16)
    key_low = (
        key_scale * key_gained - key_proj * key_scale**3 / full_width * key_dot[:, None]
    ).astype(jnp.bfloat16)
    value_grad_low = value_grad.reshape(row_count, local_width).astype(jnp.bfloat16)
    query_wgrad = jnp.einsum("td,tc->dc", whole_x, query_low, preferred_element_type=jnp.float32)
    key_wgrad = jnp.einsum("td,tc->dc", whole_x, key_low, preferred_element_type=jnp.float32)
    value_wgrad = jnp.einsum(
        "td,tc->dc", whole_x, value_grad_low, preferred_element_type=jnp.float32
    )
    input_part = jnp.einsum("tc,dc->td", query_low, w_query, preferred_element_type=jnp.float32)
    input_part = input_part + jnp.einsum(
        "tc,dc->td", key_low, w_key, preferred_element_type=jnp.float32
    )
    input_part = input_part + jnp.einsum(
        "tc,dc->td", value_grad_low, w_value, preferred_element_type=jnp.float32
    )
    input_grad = (column_sum(input_part) + grad_own).astype(jnp.bfloat16)
    pieces = (
        lax.psum_scatter(
            query_wgrad.astype(jnp.bfloat16), "dp", scatter_dimension=0, tiled=True
        ).astype(jnp.float32),
        lax.psum_scatter(
            key_wgrad.astype(jnp.bfloat16), "dp", scatter_dimension=0, tiled=True
        ).astype(jnp.float32),
        lax.psum_scatter(
            value_wgrad.astype(jnp.bfloat16), "dp", scatter_dimension=0, tiled=True
        ).astype(jnp.float32),
        lax.psum_scatter(
            out_wgrad.astype(jnp.bfloat16), "dp", scatter_dimension=1, tiled=True
        ).astype(jnp.float32),
        lax.psum_scatter(
            gate_wgrad.astype(jnp.bfloat16), "dp", scatter_dimension=0, tiled=True
        ).astype(jnp.float32),
        lax.psum_scatter(
            up_wgrad.astype(jnp.bfloat16), "dp", scatter_dimension=0, tiled=True
        ).astype(jnp.float32),
        lax.psum_scatter(
            down_wgrad.astype(jnp.bfloat16), "dp", scatter_dimension=1, tiled=True
        ).astype(jnp.float32),
        lax.psum_scatter(
            gain_query_grad.astype(jnp.bfloat16), "dp", scatter_dimension=0, tiled=True
        ).astype(jnp.float32),
        lax.psum_scatter(
            gain_key_grad.astype(jnp.bfloat16), "dp", scatter_dimension=0, tiled=True
        ).astype(jnp.float32),
        lax.psum_scatter(
            gain_attn_grad.astype(jnp.bfloat16), "dp", scatter_dimension=0, tiled=True
        ).astype(jnp.float32),
        lax.psum_scatter(
            gain_mlp_grad.astype(jnp.bfloat16), "dp", scatter_dimension=0, tiled=True
        ).astype(jnp.float32),
    )
    summed = (
        lax.all_gather(pieces[0].astype(jnp.bfloat16), "dp", axis=0, tiled=True).astype(
            jnp.float32
        ),
        lax.all_gather(pieces[1].astype(jnp.bfloat16), "dp", axis=0, tiled=True).astype(
            jnp.float32
        ),
        lax.all_gather(pieces[2].astype(jnp.bfloat16), "dp", axis=0, tiled=True).astype(
            jnp.float32
        ),
        lax.all_gather(pieces[3].astype(jnp.bfloat16), "dp", axis=1, tiled=True).astype(
            jnp.float32
        ),
        lax.all_gather(pieces[4].astype(jnp.bfloat16), "dp", axis=0, tiled=True).astype(
            jnp.float32
        ),
        lax.all_gather(pieces[5].astype(jnp.bfloat16), "dp", axis=0, tiled=True).astype(
            jnp.float32
        ),
        lax.all_gather(pieces[6].astype(jnp.bfloat16), "dp", axis=1, tiled=True).astype(
            jnp.float32
        ),
        lax.all_gather(pieces[7].astype(jnp.bfloat16), "dp", axis=0, tiled=True).astype(
            jnp.float32
        ),
        lax.all_gather(pieces[8].astype(jnp.bfloat16), "dp", axis=0, tiled=True).astype(
            jnp.float32
        ),
        lax.all_gather(pieces[9].astype(jnp.bfloat16), "dp", axis=0, tiled=True).astype(
            jnp.float32
        ),
        lax.all_gather(pieces[10].astype(jnp.bfloat16), "dp", axis=0, tiled=True).astype(
            jnp.float32
        ),
    )
    return (
        output,
        input_grad,
        summed[0],
        summed[1],
        summed[2],
        summed[3],
        summed[4],
        summed[5],
        summed[6],
        summed[7],
        summed[8],
        summed[9],
        summed[10],
    )


def solution(mesh):
    in_specs = (
        P("dp", "tensor"),
        P("dp", None),
        P("dp", "tensor"),
        P(None, "tensor"),
        P(None, "tensor"),
        P(None, "tensor"),
        P("tensor", None),
        P(None, "tensor"),
        P(None, "tensor"),
        P("tensor", None),
        P("tensor"),
        P("tensor"),
        P(),
        P(),
    )
    out_specs = (
        P("dp", "tensor"),
        P("dp", "tensor"),
        P(None, "tensor"),
        P(None, "tensor"),
        P(None, "tensor"),
        P("tensor", None),
        P(None, "tensor"),
        P(None, "tensor"),
        P("tensor", None),
        P("tensor"),
        P("tensor"),
        P(),
        P(),
    )
    return jax.shard_map(body, mesh=mesh, in_specs=in_specs, out_specs=out_specs, check_vma=False)
```

profile of v0, /device:TPU:0, one launch (start us, length us, event | category | flops | bytes accessed | tf_op | source)
XLA Modules:
  0.0 2042.8 jit_solution(538331763269702420)
XLA Ops:
  14.0 32.8 %all-gather.12.cloned.1.call-done = bf16[1024,2048]{1,0:T(8,128)(2,1)} async-done(((bf16[1024,512]{1,0:T(8,128)(2,1)}), bf16[1024,2048]{1,0:T(8,128)(2,1)}) %all-gather.12.cloned.1.call-update) | async-done | bytes 4194320 | tf_op jit(solution)/shard_map/all_gather | solution.py:81
  95.6 23.1 %while.30 = (s32[]{:T(128)}, bf16[2,512,4,128]{3,1,2,0:T(8,128)(2,1)}, f32[2,4,512]{2,1,0:T(4,128)S(1)}, s32[2]{0:T(128)S(1)}, s32[1024]{0:T(1024)S(1)}, /*index...) while((s32[]{:T(128)}, ...), condition=%wide.region_9.10_spmd.clone.clone, body=%wide.region_6.9_spmd.clone.sunk.clone | while | flops 1100478976 | bytes 43596048 | solution.py:126
  128.2 86.7 %all-reduce.14.cloned.1.call-done = bf16[1024,2048]{1,0:T(8,128)(2,1)} async-done(((bf16[1024,2048]{1,0:T(8,128)(2,1)}), bf16[1024,2048]{1,0:T(8,128)(2,1)}) %all-reduce.14.cloned.1.call-update) | async-done | bytes 4194320 | tf_op jit(solution)/shard_map/psum | solution.py:129
  225.4 14.8 fusion.85
  240.2 15.2 multiply_convert_fusion.3
  268.7 85.0 %all-reduce.16.cloned.1.call-done = bf16[1024,2048]{1,0:T(8,128)(2,1)} async-done(((bf16[1024,2048]{1,0:T(8,128)(2,1)}), bf16[1024,2048]{1,0:T(8,128)(2,1)}) %all-reduce.16.cloned.1.call-update) | async-done | bytes 4194320 | tf_op jit(solution)/shard_map/psum | solution.py:141
  356.8 32.9 %all-gather.14.cloned.1.call-done = bf16[1024,2048]{1,0:T(8,128)(2,1)} async-done(((bf16[1024,512]{1,0:T(8,128)(2,1)}), bf16[1024,2048]{1,0:T(8,128)(2,1)}) %all-gather.14.cloned.1.call-update) | async-done | bytes 4194320 | tf_op jit(solution)/shard_map/all_gather | solution.py:82
  396.0 20.0 multiply_convert_fusion.1
  416.0 12.7 fusion.86
  428.7 13.0 add_convert_fusion.1
  443.8 83.6 %all-reduce.18.cloned.1.call-done = bf16[1024,2048]{1,0:T(8,128)(2,1)} async-done(((bf16[1024,2048]{1,0:T(8,128)(2,1)}), bf16[1024,2048]{1,0:T(8,128)(2,1)}) %all-reduce.18.cloned.1.call-update) | async-done | bytes 4194320 | tf_op jit(solution)/shard_map/psum | solution.py:164
  544.1 68.4 %while.31 = (s32[]{:T(128)}, f32[1024,4,128]{0,2,1:T(8,128)}, f32[1024,4,128]{0,2,1:T(8,128)}, f32[2,512,4,128]{3,1,2,0:T(8,128)}, s32[2]{0:T(128)S(1)}, /*index...) while((s32[]{:T(128)}, f32[1024,4,128]{0,2,1:T(8,128)}, ...), condition=%wide.region_19.20_spmd.clone.clone, body=%wide.region_17.19_spmd.clone.sunk.clone | while | flops 2720266752 | bytes 163650096 | solution.py:209
  686.0 14.0 convolution_convert_fusion.2
  700.1 14.2 convolution_convert_fusion.1
  715.0 15.7 convolution_convert_fusion
  733.0 71.5 %reduce-scatter.13.cloned.1.call-done = bf16[256,512]{0,1:T(8,128)(2,1)} async-done(((bf16[2048,512]{0,1:T(8,128)(2,1)}), bf16[256,512]{0,1:T(8,128)(2,1)}) %reduce-scatter.13.cloned.1.call-update) | async-done | bytes 262160 | tf_op jit(solution)/shard_map/reduce_scatter | solution.py:246
  804.5 71.7 %reduce-scatter.15.cloned.1.call-done = bf16[256,512]{0,1:T(8,128)(2,1)} async-done(((bf16[2048,512]{0,1:T(8,128)(2,1)}), bf16[256,512]{0,1:T(8,128)(2,1)}) %reduce-scatter.15.cloned.1.call-update) | async-done | bytes 262160 | tf_op jit(solution)/shard_map/reduce_scatter | solution.py:249
  876.2 71.6 %reduce-scatter.17.cloned.1.call-done = bf16[512,256]{1,0:T(8,128)(2,1)} async-done(((bf16[512,2048]{1,0:T(8,128)(2,1)}), bf16[512,256]{1,0:T(8,128)(2,1)}) %reduce-scatter.17.cloned.1.call-update) | async-done | bytes 262160 | tf_op jit(solution)/shard_map/reduce_scatter | solution.py:252
  959.3 139.1 %reduce-scatter.19.cloned.1.call-done = bf16[256,2048]{1,0:T(8,128)(2,1)} async-done(((bf16[2048,2048]{1,0:T(8,128)(2,1)}), bf16[256,2048]{1,0:T(8,128)(2,1)}) %reduce-scatter.19.cloned.1.call-update) | async-done | bytes 1048592 | tf_op jit(solution)/shard_map/reduce_scatter | solution.py:255
  1098.4 150.2 %reduce-scatter.21.cloned.1.call-done = bf16[256,2048]{1,0:T(8,128)(2,1)} async-done(((bf16[2048,2048]{1,0:T(8,128)(2,1)}), bf16[256,2048]{1,0:T(8,128)(2,1)}) %reduce-scatter.21.cloned.1.call-update) | async-done | bytes 1048592 | tf_op jit(solution)/shard_map/reduce_scatter | solution.py:258
  1248.7 150.4 %reduce-scatter.23.cloned.1.call-done = bf16[2048,256]{1,0:T(8,128)(2,1)} async-done(((bf16[2048,2048]{1,0:T(8,128)(2,1)}), bf16[2048,256]{1,0:T(8,128)(2,1)}) %reduce-scatter.23.cloned.1.call-update) | async-done | bytes 1048592 | tf_op jit(solution)/shard_map/reduce_scatter | solution.py:261
  1408.0 19.5 all-reduce.9
  1428.0 33.9 %all-reduce.8 = (bf16[512]{0:T(512)(128)(2,1)S(1)}, bf16[512]{0:T(512)(128)(2,1)S(1)}, bf16[2048]{0:T(1024)(128)(2,1)S(1)}, bf16[2048]{0:T(1024)(128)(2,1)S(1)}) all-reduce(bf16[512]{0:T(512)(128)(2,1)S(1)} %dynamic-update-slice, bf16[512]{0:T(512)(128)(2,1)S(1)} %dynamic-update-slice.1, ...), channel_id=1, replica_groups=mesh['dp'=8,'tensor'=4] {'dp'}, use_global_device_ids=true, to_apply=%add | all-reduce | flops 5120 | bytes 20480
  1463.2 16.3 all-gather
  1486.2 18.7 all-gather.1
  1513.8 38.5 %all-gather.20.cloned.1.call-done = bf16[2048,512]{0,1:T(8,128)(2,1)} async-done(((bf16[256,512]{0,1:T(8,128)(2,1)}), bf16[2048,512]{0,1:T(8,128)(2,1)}) %all-gather.20.cloned.1.call-update) | async-done | bytes 2097168 | tf_op jit(solution)/shard_map/all_gather | solution.py:284
  1556.4 46.3 %all-gather.22.cloned.1.call-done = bf16[512,2048]{1,0:T(8,128)(2,1)} async-done(((bf16[512,256]{1,0:T(8,128)(2,1)}), bf16[512,2048]{1,0:T(8,128)(2,1)}) %all-gather.22.cloned.1.call-update) | async-done | bytes 2097168 | tf_op jit(solution)/shard_map/all_gather | solution.py:287
  1606.9 40.9 %reduce-scatter.9.cloned.1.call-done = bf16[1024,512]{1,0:T(8,128)(2,1)} async-done(((bf16[1024,2048]{1,0:T(8,128)(2,1)}), bf16[1024,512]{1,0:T(8,128)(2,1)}) %reduce-scatter.9.cloned.1.call-update) | async-done | bytes 1048592 | tf_op jit(solution)/shard_map/reduce_scatter | solution.py:43
  1650.9 123.3 %all-gather.24.cloned.1.call-done = bf16[2048,2048]{1,0:T(8,128)(2,1)} async-done(((bf16[256,2048]{1,0:T(8,128)(2,1)}), bf16[2048,2048]{1,0:T(8,128)(2,1)}) %all-gather.24.cloned.1.call-update) | async-done | bytes 8388624 | tf_op jit(solution)/shard_map/all_gather | solution.py:290
  1774.3 12.1 convert_element_type.250
  1786.4 112.7 %all-gather.26.cloned.1.call-done = bf16[2048,2048]{1,0:T(8,128)(2,1)} async-done(((bf16[256,2048]{1,0:T(8,128)(2,1)}), bf16[2048,2048]{1,0:T(8,128)(2,1)}) %all-gather.26.cloned.1.call-update) | async-done | bytes 8388624 | tf_op jit(solution)/shard_map/all_gather | solution.py:293
  1911.2 112.9 %all-gather.28.cloned.1.call-done = bf16[2048,2048]{1,0:T(8,128)(2,1)} async-done(((bf16[2048,256]{1,0:T(8,128)(2,1)}), bf16[2048,2048]{1,0:T(8,128)(2,1)}) %all-gather.28.cloned.1.call-update) | async-done | bytes 8388624 | tf_op jit(solution)/shard_map/all_gather | solution.py:296
  (368 shorter events, 348.2 us)
Async XLA Ops:
  7.2 46.3 %copy-start = (bf16[2048,512]{1,0:T(8,128)(2,1)S(1)}, bf16[2048,512]{1,0:T(8,128)(2,1)}, u32[]{:S(2)}) copy-start(bf16[2048,512]{1,0:T(8,128)(2,1)} %param.21) | copy-start | bytes 6291460
  7.2 39.6 %all-gather.12.cloned.1.call-start = ((), (), s32[]{:S(2)}) async-start(), calls=%async_computation.8 | async-start | bytes 5242880 | tf_op jit(solution)/shard_map/all_gather | solution.py:81
  7.9 206.9 %all-reduce.14.cloned.1.call-start = ((), (), s32[]{:S(2)}) async-start(), calls=%async_computation.9 | async-start | bytes 8388608 | tf_op jit(solution)/shard_map/psum | solution.py:129
  128.1 90.6 %copy-start.45 = (f32[2048]{0:T(1024)S(1)}, f32[2048]{0:T(1024)}, u32[]{:S(2)}) copy-start(f32[2048]{0:T(1024)} %param.30) | copy-start | bytes 24580
  128.1 225.6 %all-reduce.16.cloned.1.call-start = ((), (), s32[]{:S(2)}) async-start(), calls=%async_computation.10 | async-start | bytes 8388608 | tf_op jit(solution)/shard_map/psum | solution.py:141
  225.4 32.1 %slice-start.2 = ((s8[8388608]{0:T(1024)(128)(4,1)}), s8[4194304]{0:T(1024)(128)(4,1)S(1)}, s32[]{:S(2)}) async-start(s8[8388608]{0:T(1024)(128)(4,1)} %bitcast.205), calls=%async_computation.30 | async-start | bytes 8388608
  267.9 121.9 %copy-start.64 = (f32[2048]{0:T(1024)S(1)}, f32[2048]{0:T(1024)}, u32[]{:S(2)}) copy-start(f32[2048]{0:T(1024)} %param.31) | copy-start | bytes 24580
  267.9 121.8 %all-gather.14.cloned.1.call-start = ((), (), s32[]{:S(2)}) async-start(), calls=%async_computation.11 | async-start | bytes 5242880 | tf_op jit(solution)/shard_map/all_gather | solution.py:82
  268.5 258.9 %all-reduce.18.cloned.1.call-start = ((), (), s32[]{:S(2)}) async-start(), calls=%async_computation.12 | async-start | bytes 8388608 | tf_op jit(solution)/shard_map/psum | solution.py:164
  356.8 39.2 %copy-start.53 = (f32[1024]{0:T(1024)}, f32[1024]{0:T(1024)S(1)}, u32[]{:S(2)}) copy-start(f32[1024]{0:T(1024)S(1)} %get-tuple-element.395) | copy-start | bytes 12292
  356.8 39.2 %copy-start.66 = (f32[1024]{0:T(1024)}, f32[1024]{0:T(1024)S(1)}, u32[]{:S(2)}) copy-start(f32[1024]{0:T(1024)S(1)} %get-tuple-element.394) | copy-start | bytes 12292
  441.7 85.7 %copy-start.46 = (f32[2048]{0:T(1024)S(1)}, f32[2048]{0:T(1024)}, u32[]{:S(2)}) copy-start(f32[2048]{0:T(1024)} %param.30) | copy-start | bytes 24580
  441.7 85.7 %copy-start.52 = (f32[1024]{0:T(1024)S(1)}, f32[1024]{0:T(1024)}, u32[]{:S(2)}) copy-start(f32[1024]{0:T(1024)} %copy-done.51) | copy-start | bytes 12292
  441.8 291.1 %reduce-scatter.11.cloned.1.call-start = ((), (), s32[]{:S(2)}) async-start(), calls=%async_computation.14 | async-start | bytes 2359296 | tf_op jit(solution)/shard_map/reduce_scatter | solution.py:243
  443.8 90.8 %copy-start.59 = (f32[1024]{0:T(1024)S(1)}, f32[1024]{0:T(1024)}, u32[]{:S(2)}) copy-start(f32[1024]{0:T(1024)} %get-tuple-element.392) | copy-start | bytes 12292
  663.2 141.3 %reduce-scatter.13.cloned.1.call-start = ((), (), s32[]{:S(2)}) async-start(), calls=%async_computation.16 | async-start | bytes 2359296 | tf_op jit(solution)/shard_map/reduce_scatter | solution.py:246
  670.7 205.4 %reduce-scatter.15.cloned.1.call-start = ((), (), s32[]{:S(2)}) async-start(), calls=%async_computation.18 | async-start | bytes 2359296 | tf_op jit(solution)/shard_map/reduce_scatter | solution.py:249
  679.5 268.3 %reduce-scatter.17.cloned.1.call-start = ((), (), s32[]{:S(2)}) async-start(), calls=%async_computation.20 | async-start | bytes 2359296 | tf_op jit(solution)/shard_map/reduce_scatter | solution.py:252
  685.9 412.4 %reduce-scatter.19.cloned.1.call-start = ((), (), s32[]{:S(2)}) async-start(), calls=%async_computation.22 | async-start | bytes 9437184 | tf_op jit(solution)/shard_map/reduce_scatter | solution.py:255
  700.1 548.6 %reduce-scatter.21.cloned.1.call-start = ((), (), s32[]{:S(2)}) async-start(), calls=%async_computation.24 | async-start | bytes 9437184 | tf_op jit(solution)/shard_map/reduce_scatter | solution.py:258
  714.3 684.7 %reduce-scatter.23.cloned.1.call-start = ((), (), s32[]{:S(2)}) async-start(), calls=%async_computation.26 | async-start | bytes 9437184 | tf_op jit(solution)/shard_map/reduce_scatter | solution.py:261
  730.7 217.1 %copy-start.40 = (bf16[1024,512]{0,1:T(8,128)(2,1)S(1)}, bf16[1024,512]{0,1:T(8,128)(2,1)}, u32[]{:S(2)}) copy-start(bf16[1024,512]{0,1:T(8,128)(2,1)} %copy-done.39) | copy-start | bytes 3145732
  730.8 774.8 %all-gather.16.cloned.1.call-start = ((), (), s32[]{:S(2)}) async-start(), calls=%async_computation.15 | async-start | bytes 2359296 | tf_op jit(solution)/shard_map/all_gather | solution.py:278
  732.9 776.7 %all-gather.18.cloned.1.call-start = ((), (), s32[]{:S(2)}) async-start(), calls=%async_computation.17 | async-start | bytes 2359296 | tf_op jit(solution)/shard_map/all_gather | solution.py:281
  804.5 747.8 %all-gather.20.cloned.1.call-start = ((), (), s32[]{:S(2)}) async-start(), calls=%async_computation.19 | async-start | bytes 2359296 | tf_op jit(solution)/shard_map/all_gather | solution.py:284
  876.2 726.6 %all-gather.22.cloned.1.call-start = ((), (), s32[]{:S(2)}) async-start(), calls=%async_computation.21 | async-start | bytes 2359296 | tf_op jit(solution)/shard_map/all_gather | solution.py:287
  947.8 699.9 %reduce-scatter.9.cloned.1.call-start = ((), (), s32[]{:S(2)}) async-start(), calls=%async_computation.13 | async-start | bytes 5242880 | tf_op jit(solution)/shard_map/reduce_scatter | solution.py:43
  959.2 440.0 %copy-start.70 = (u32[32]{0:T(128)S(1)}, u32[32]{0:T(128)}, u32[]{:S(2)}) copy-start(u32[32]{0:T(128)} %constant.112) | copy-start | bytes 388
  959.3 815.0 %all-gather.24.cloned.1.call-start = ((), (), s32[]{:S(2)}) async-start(), calls=%async_computation.23 | async-start | bytes 9437184 | tf_op jit(solution)/shard_map/all_gather | solution.py:290
  1098.4 800.7 %all-gather.26.cloned.1.call-start = ((), (), s32[]{:S(2)}) async-start(), calls=%async_computation.25 | async-start | bytes 9437184 | tf_op jit(solution)/shard_map/all_gather | solution.py:293
  1248.6 775.5 %all-gather.28.cloned.1.call-start = ((), (), s32[]{:S(2)}) async-start(), calls=%async_computation.27 | async-start | bytes 9437184 | tf_op jit(solution)/shard_map/all_gather | solution.py:296
  1405.0 23.0 %copy-start.60 = (bf16[2048]{0:T(1024)(128)(2,1)S(1)}, bf16[2048]{0:T(1024)(128)(2,1)}, u32[]{:S(2)}) copy-start(bf16[2048]{0:T(1024)(128)(2,1)} %get-tuple-element.303) | copy-start | bytes 12292
  (80 other events, 401.6 us)
Sparse Core Ops, SparseCore 0:
  9.6 37.1 all-gather.11
  128.2 86.5 all-reduce.13
  268.1 85.6 all-reduce.15
  355.1 34.5 all-gather.13
  441.9 85.4 all-reduce.17
  663.3 69.5 reduce-scatter.10
  736.4 67.9 reduce-scatter.12
  808.0 68.1 reduce-scatter.14
  879.7 68.0 reduce-scatter.16
  951.8 146.4 reduce-scatter.18
  1102.0 146.5 reduce-scatter.20
  1252.1 146.9 reduce-scatter.22
  1401.1 50.0 all-gather.15
  1453.1 48.6 all-gather.17
  1503.7 48.5 all-gather.19
  1554.2 48.5 all-gather.21
  1605.1 42.5 reduce-scatter.8
  1649.7 124.4 all-gather.23
  1776.4 122.6 all-gather.25
  1901.0 123.1 all-gather.27
where the time goes:
time: 2050 us; the launch traced here: 2040 us
  waiting for transfers between devices  1450 us (71%)
  matrix products  245 us (12%)
  other arithmetic  150 us (7%)
  blocking collectives  107 us (5%)
  local copies, waits for them, and re-layouts  61.7 us (3%)
    reduce_scatter x1, waiting for transfers between devices, body(): lax.psum_scatter(down_wgrad.astype(jnp.bfloat16), 'dp', scatter_dimension...  150 us
    reduce_scatter x1, waiting for transfers between devices, body(): lax.psum_scatter(up_wgrad.astype(jnp.bfloat16), 'dp', scatter_dimension=0...  150 us
    reduce_scatter x1, waiting for transfers between devices, body(): lax.psum_scatter(gate_wgrad.astype(jnp.bfloat16), 'dp', scatter_dimension...  139 us
    all_gather x1, waiting for transfers between devices, body(): lax.all_gather(pieces[4].astype(jnp.bfloat16), 'dp', axis=0, tiled=True)  123 us
    all_gather x1, waiting for transfers between devices, body(): lax.all_gather(pieces[6].astype(jnp.bfloat16), 'dp', axis=1, tiled=True)  113 us
    all_gather x1, waiting for transfers between devices, body(): lax.all_gather(pieces[5].astype(jnp.bfloat16), 'dp', axis=0, tiled=True)  113 us
    psum x1, waiting for transfers between devices, body(): lax.psum(attn_part.astype(jnp.bfloat16), 'tensor').astype(jnp.float32)  86.7 us
    psum x1, waiting for transfers between devices, body(): lax.psum(branch_part.astype(jnp.bfloat16), 'tensor').astype(jnp.float32)  85 us
  transfers between devices with their start and end apart: 20, of which 18 were waited for; matrix products, arithmetic and copies ran while one was open for 7% of the time, Pallas kernels for 0%

commit v1 on v0

--- a/solution.py
+++ b/solution.py
@@ -1,7 +1,12 @@
+import math
+
 import jax
 import jax.numpy as jnp
 from jax import lax
+from jax.experimental import pallas as pl
+from jax.experimental.pallas import tpu as pltpu
 from jax.sharding import PartitionSpec as P
+
 
 HD = 128
 
@@ -45,7 +50,7 @@
     ).astype(jnp.float32)
 
 
-def body(
+def general_body(
     tokens,
     segments,
     cotangent,
@@ -113,7 +118,7 @@
         return (query_block, jnp.where(allowed[None], scores, -1e30))
 
     def attend_block(block_index):
-        query_block, scores = scores_for(block_index * block_rows)
+        _, scores = scores_for(block_index * block_rows)
         row_max = jnp.max(scores, -1, keepdims=True)
         exp_terms = jnp.exp(scores - row_max)
         row_total = jnp.sum(exp_terms, -1, keepdims=True)
@@ -326,6 +331,1117 @@
     )
 
 
+f32 = jnp.float32
+bf16 = jnp.bfloat16
+
+SWAP_Y = [(d, d ^ 1) for d in range(8)]
+SWAP_Y_MIDDLE = [(d, d ^ 1) for d in range(2, 6)]
+SWAP_Y_END = [(d, d ^ 1) for d in (0, 1, 6, 7)]
+Z_IN = [(2 * a + y, 2 * b + y) for a, b in ((0, 1), (3, 2)) for y in (0, 1)]
+Z_MID = [(2 * a + y, 2 * b + y) for a, b in ((1, 2), (2, 1)) for y in (0, 1)]
+Z_OUT = [(2 * a + y, 2 * b + y) for a, b in ((1, 0), (2, 3)) for y in (0, 1)]
+SWAP_CORE = [(t, t ^ 1) for t in range(4)]
+SWAP_X = [(t, t ^ 2) for t in range(4)]
+
+
+def over_dp(value, pairs):
+    return lax.ppermute(value, "dp", pairs)
+
+
+def to_core(value):
+    return lax.ppermute(value, "tensor", SWAP_CORE)
+
+
+def to_x(value):
+    return lax.ppermute(value, "tensor", SWAP_X)
+
+
+def low_add(left, right):
+    return (left.astype(f32) + right.astype(f32)).astype(bf16)
+
+
+def dot(left, right, left_axis=1, right_axis=0):
+    return lax.dot_general(
+        left, right, (((left_axis,), (right_axis,)), ((), ())), preferred_element_type=f32
+    )
+
+
+def part(value, index, size, axis):
+    return lax.dynamic_slice_in_dim(value, index * size, size, axis)
+
+
+def place_one(target, shape, use_first, first, second, row_block, col_block):
+    rows, cols = second.shape
+    steps = 4
+    tile = rows // steps
+
+    def kernel(spot_ref, first_ref, second_ref, *refs):
+        @pl.when(spot_ref[2] == 1)
+        def _():
+            refs[-1][...] = first_ref[...].astype(f32)
+
+        @pl.when(spot_ref[2] != 1)
+        def _():
+            refs[-1][...] = second_ref[...].astype(f32)
+
+    spots = jnp.stack(
+        [jnp.int32(row_block) * steps, jnp.int32(col_block), use_first.astype(jnp.int32)]
+    )
+    in_specs = [
+        pl.BlockSpec((tile, cols), lambda i, spot: (i * spot[2], 0)),
+        pl.BlockSpec((tile, cols), lambda i, spot: (i * (1 - spot[2]), 0)),
+    ]
+    operands = [spots, first, second]
+    aliases = {}
+    if target is not None:
+        in_specs.append(pl.BlockSpec(memory_space=pl.ANY))
+        operands.append(target)
+        aliases = {3: 0}
+    return pl.pallas_call(
+        kernel,
+        out_shape=jax.ShapeDtypeStruct(shape, f32),
+        grid_spec=pltpu.PrefetchScalarGridSpec(
+            num_scalar_prefetch=1,
+            grid=(steps,),
+            in_specs=in_specs,
+            out_specs=pl.BlockSpec((tile, cols), lambda i, spot: (spot[0] + i, spot[1])),
+        ),
+        input_output_aliases=aliases,
+        compiler_params=pltpu.CompilerParams(vmem_limit_bytes=16 << 20),
+        cost_estimate=pl.CostEstimate(
+            flops=rows * cols, bytes_accessed=6 * rows * cols, transcendentals=0
+        ),
+        name="place",
+    )(*operands)
+
+
+def place(target, shape, block, row_block, col_block):
+    rows, cols = block.shape
+    steps = 4
+    tile = rows // steps
+
+    def kernel(spot_ref, block_ref, target_ref, out_ref):
+        out_ref[...] = block_ref[...].astype(f32)
+
+    spots = jnp.stack([jnp.int32(row_block) * steps, jnp.int32(col_block)])
+    return pl.pallas_call(
+        kernel,
+        out_shape=jax.ShapeDtypeStruct(shape, f32),
+        grid_spec=pltpu.PrefetchScalarGridSpec(
+            num_scalar_prefetch=1,
+            grid=(steps,),
+            in_specs=[
+                pl.BlockSpec((tile, cols), lambda i, spot: (i, 0)),
+                pl.BlockSpec(memory_space=pl.ANY),
+            ],
+            out_specs=pl.BlockSpec((tile, cols), lambda i, spot: (spot[0] + i, spot[1])),
+        ),
+        input_output_aliases={2: 0},
+        compiler_params=pltpu.CompilerParams(vmem_limit_bytes=16 << 20),
+        cost_estimate=pl.CostEstimate(
+            flops=rows * cols, bytes_accessed=6 * rows * cols, transcendentals=0
+        ),
+        name="place",
+    )(spots, block, target)
+
+
+def matmul_call(kernel, steps, ins, outs, scratch=(), flops=0, mib=24):
+    moved = sum(a.size * a.dtype.itemsize for a, _, _ in ins)
+    moved += sum(math.prod(s) * jnp.dtype(d).itemsize for s, d, _, _ in outs)
+    return pl.pallas_call(
+        kernel,
+        out_shape=[jax.ShapeDtypeStruct(s, d) for s, d, _, _ in outs],
+        grid=(steps,),
+        in_specs=[pl.BlockSpec(b, m) for _, b, m in ins],
+        out_specs=[pl.BlockSpec(b, m) for _, _, b, m in outs],
+        scratch_shapes=list(scratch),
+        compiler_params=pltpu.CompilerParams(vmem_limit_bytes=mib << 20),
+        cost_estimate=pl.CostEstimate(flops=flops, bytes_accessed=moved, transcendentals=0),
+    )(*[a for a, _, _ in ins])
+
+
+def feed(low, w_gate, w_up):
+    rows, width = low.shape
+    units = w_gate.shape[1]
+    tile = min(512, units)
+
+    def kernel(low_ref, gate_w, up_w, gate_ref, up_ref, act_ref):
+        gate = dot(low_ref[...], gate_w[...])
+        up = dot(low_ref[...], up_w[...])
+        gate_ref[...] = gate.astype(bf16)
+        up_ref[...] = up.astype(bf16)
+        act_ref[...] = (gate * jax.nn.sigmoid(gate) * up).astype(bf16)
+
+    column = lambda n: (0, n)
+    return matmul_call(
+        kernel,
+        units // tile,
+        [
+            (low, (rows, width), lambda n: (0, 0)),
+            (w_gate, (width, tile), column),
+            (w_up, (width, tile), column),
+        ],
+        [((rows, units), bf16, (rows, tile), column)] * 3,
+        flops=4 * rows * width * units,
+        mib=56,
+    )
+
+
+def unfeed(low, w_down, gate, up):
+    rows, width = low.shape
+    units = w_down.shape[0]
+    tile = min(512, units)
+
+    def kernel(low_ref, down_w, gate_ref, up_ref, dgate_ref, dup_ref):
+        grad = dot(low_ref[...], down_w[...], 1, 1)
+        gate = gate_ref[...].astype(f32)
+        sigma = jax.nn.sigmoid(gate)
+        dup_ref[...] = (grad * (gate * sigma)).astype(bf16)
+        dgate_ref[...] = (
+            grad * up_ref[...].astype(f32) * sigma * (1.0 + gate * (1.0 - sigma))
+        ).astype(bf16)
+
+    column = lambda n: (0, n)
+    return matmul_call(
+        kernel,
+        units // tile,
+        [
+            (low, (rows, width), lambda n: (0, 0)),
+            (w_down, (tile, width), lambda n: (n, 0)),
+            (gate, (rows, tile), column),
+            (up, (rows, tile), column),
+        ],
+        [((rows, units), bf16, (rows, tile), column)] * 2,
+        flops=2 * rows * width * units,
+        mib=56,
+    )
+
+
+def unwide(dgate, dup, w_gate, w_up):
+    rows, units = dgate.shape
+    width = w_gate.shape[0]
+    tile = min(512, width)
+
+    def kernel(dgate_ref, dup_ref, gate_w, up_w, upper_ref, lower_ref):
+        total = dot(dgate_ref[...], gate_w[...], 1, 1) + dot(dup_ref[...], up_w[...], 1, 1)
+        upper_ref[...] = total[: rows // 2].astype(bf16)
+        lower_ref[...] = total[rows // 2 :].astype(bf16)
+
+    whole = lambda n: (0, 0)
+    row = lambda n: (n, 0)
+    column = lambda n: (0, n)
+    return matmul_call(
+        kernel,
+        width // tile,
+        [
+            (dgate, (rows, units), whole),
+            (dup, (rows, units), whole),
+            (w_gate, (tile, units), row),
+            (w_up, (tile, units), row),
+        ],
+        [((rows // 2, width), bf16, (rows // 2, tile), column)] * 2,
+        flops=4 * rows * width * units,
+        mib=56,
+    )
+
+
+def half_turned(values):
+    lanes = lax.broadcasted_iota(jnp.int32, values.shape, 1)
+    rolled = pltpu.roll(values, HD // 2, 1)
+    return jnp.where(lanes < HD // 2, -rolled, rolled)
+
+
+def as_column(row):
+    return jnp.broadcast_to(row, (HD, row.shape[1])).T
+
+
+def as_row(values):
+    return jnp.sum(values.T, 0, keepdims=True)
+
+
+def project(x, w_query, w_key, w_value):
+    rows, width = x.shape
+    cols = w_query.shape[1]
+    tile = rows // 4
+
+    def kernel(x_ref, q_w, k_w, v_w, q_ref, k_ref, v_ref, sum_ref):
+        for which, (weight, result) in enumerate(((q_w, q_ref), (k_w, k_ref))):
+            value = dot(x_ref[...], weight[...])
+            result[...] = value
+            square = value * value
+            total = square[:, :HD]
+            for start in range(HD, cols, HD):
+                total = total + square[:, start : start + HD]
+            sum_ref[which : which + 1] = as_row(total)
+        v_ref[...] = dot(x_ref[...], v_w[...]).astype(bf16)
+
+    row = lambda i: (i, 0)
+    whole = lambda i: (0, 0)
+    return matmul_call(
+        kernel,
+        rows // tile,
+        [
+            (x, (tile, width), row),
+            (w_query, (width, cols), whole),
+            (w_key, (width, cols), whole),
+            (w_value, (width, cols), whole),
+        ],
+        [
+            ((rows, cols), f32, (tile, cols), row),
+            ((rows, cols), f32, (tile, cols), row),
+            ((rows, cols), bf16, (tile, cols), row),
+            ((2, rows), f32, (2, tile), lambda i: (0, i)),
+        ],
+        flops=6 * rows * width * cols,
+    )
+
+
+def turn_heads(query, key, squares, full_width, gain_query, gain_key, cosine, sine):
+    rows, width = query.shape
+
+    def kernel(q_ref, k_ref, sum_ref, gq_ref, gk_ref, cos_ref, sin_ref, qr_ref, kr_ref):
+        scales = lax.rsqrt(sum_ref[...] / full_width + epsilon)
+        for value, col, gain, result in ((q_ref, 0, gq_ref, qr_ref), (k_ref, 1, gk_ref, kr_ref)):
+            normed = value[...] * as_column(scales[col : col + 1]) * gain[...]
+            result[...] = (normed * cos_ref[...] + half_turned(normed) * sin_ref[...]).astype(bf16)
+
+    head = lambda h: (0, h)
+    whole = lambda h: (0, 0)
+    return matmul_call(
+        kernel,
+        width // HD,
+        [
+            (query, (rows, HD), head),
+            (key, (rows, HD), head),
+            (squares, (2, rows), whole),
+            (gain_query[None], (1, HD), head),
+            (gain_key[None], (1, HD), head),
+            (cosine, (rows, HD), whole),
+            (sine, (rows, HD), whole),
+        ],
+        [((rows, width), bf16, (rows, HD), head)] * 2,
+        flops=10 * rows * width,
+    )
+
+
+BLOCK = 256
+
+
+def key_span(block):
+    first = max(0, block - 512 // BLOCK) * BLOCK
+    return first, (block + 1) * BLOCK
+
+
+def attend_heads(query, key, value, docs, blocks):
+    width = query.shape[1]
+    rows = len(blocks) * BLOCK
+    last = blocks[-1] * BLOCK + BLOCK
+
+    def kernel(q_ref, k_ref, v_ref, doc_ref, out_ref):
+        for n, block in enumerate(blocks):
+            begin, end = key_span(block)
+            span = end - begin
+            mine = slice(n * BLOCK, (n + 1) * BLOCK)
+            own = slice(block * BLOCK, (block + 1) * BLOCK)
+            scores = dot(q_ref[mine], k_ref[begin:end], 1, 1) * HD ** (-0.5)
+            at_row = block * BLOCK + lax.broadcasted_iota(jnp.int32, (BLOCK, span), 0)
+            at_col = begin + lax.broadcasted_iota(jnp.int32, (BLOCK, span), 1)
+            doc = jnp.concatenate([as_column(doc_ref[:, own])] * (span // HD), 1)
+            allowed = (doc == doc_ref[:, begin:end]) & (at_row >= at_col)
+            scores = jnp.where(allowed, scores, -1e30)
+            terms = jnp.exp(scores - jnp.max(scores, 1, keepdims=True))
+            weights = (terms * (1.0 / jnp.sum(terms, 1, keepdims=True))).astype(bf16)
+            out_ref[mine] = dot(weights, v_ref[begin:end]).astype(bf16)
+
+    head = lambda h: (0, h)
+    return matmul_call(
+        kernel,
+        width // HD,
+        [
+            (query, (rows, HD), lambda h: (blocks[0] // len(blocks), h)),
+            (key, (last, HD), head),
+            (value, (last, HD), head),
+            (docs, docs.shape, lambda h: (0, 0)),
+        ],
+        [((rows, width), bf16, (rows, HD), head)],
+        flops=4 * rows * last * width,
+        mib=16,
+    )[0]
+
+
+def unattend_heads(query, key, value, grad, docs, q_proj, k_proj, squares, full_width, gain_query, gain_key, cosine, sine):
+    rows, width = query.shape
+
+    def kernel(
+        q_ref, k_ref, v_ref, do_ref, doc_ref, qp_ref, kp_ref, sum_ref, gq_ref, gk_ref, cos_ref, sin_ref,
+        dq_ref, dk_ref, dv_ref, dots_ref, gain_ref, q_acc, k_acc, v_acc,
+    ):
+        k_acc[...] = jnp.zeros_like(k_acc)
+        v_acc[...] = jnp.zeros_like(v_acc)
+        for block in range(rows // BLOCK):
+            begin, end = key_span(block)
+            span = end - begin
+            mine = slice(block * BLOCK, (block + 1) * BLOCK)
+            keys = k_ref[begin:end]
+            do = do_ref[mine]
+            scores = dot(keys, q_ref[mine], 1, 1) * HD ** (-0.5)
+            at_key = begin + lax.broadcasted_iota(jnp.int32, (span, BLOCK), 0)
+            at_query = block * BLOCK + lax.broadcasted_iota(jnp.int32, (span, BLOCK), 1)
+            doc = jnp.concatenate([as_column(doc_ref[:, begin:end])] * (BLOCK // HD), 1)
+            allowed = (doc == doc_ref[:, mine]) & (at_query >= at_key)
+            scores = jnp.where(allowed, scores, -1e30)
+            terms = jnp.exp(scores - jnp.max(scores, 0, keepdims=True))
+            probs = terms * (1.0 / jnp.sum(terms, 0, keepdims=True))
+            prob_grad = dot(v_ref[begin:end], do, 1, 1)
+            inner = jnp.sum(probs * prob_grad, 0, keepdims=True)
+            low = (probs * (prob_grad - inner)).astype(bf16)
+            q_acc[mine] = dot(low, keys, 0, 0)
+            k_acc[begin:end] += dot(low, q_ref[mine])
+            v_acc[begin:end] += dot(probs.astype(bf16), do)
+        dv_ref[...] = v_acc[...].astype(bf16)
+        scales = lax.rsqrt(sum_ref[...] / full_width + epsilon)
+        for which, (acc, proj, gain, result) in enumerate(
+            ((q_acc, qp_ref, gq_ref, dq_ref), (k_acc, kp_ref, gk_ref, dk_ref))
+        ):
+            turned = acc[...] * HD ** (-0.5)
+            normed = turned * cos_ref[...] - half_turned(turned * sin_ref[...])
+            gained = normed * gain[...]
+            result[...] = gained
+            projected = proj[...]
+            gain_ref[which : which + 1] = jnp.sum(
+                normed * projected * as_column(scales[which : which + 1]), 0, keepdims=True
+            )
+            inner = as_row(gained * projected)
+
+            @pl.when(pl.program_id(0) == 0)
+            def _():
+                dots_ref[which : which + 1] = inner
+
+            @pl.when(pl.program_id(0) > 0)
+            def _():
+                dots_ref[which : which + 1] += inner
+
+    head = lambda h: (0, h)
+    whole = lambda h: (0, 0)
+    column = (rows, HD)
+    return matmul_call(
+        kernel,
+        width // HD,
+        [
+            (query, column, head),
+            (key, column, head),
+            (value, column, head),
+            (grad, column, head),
+            (docs, (1, rows), whole),
+            (q_proj, column, head),
+            (k_proj, column, head),
+            (squares, (2, rows), whole),
+            (gain_query[None], (1, HD), head),
+            (gain_key[None], (1, HD), head),
+            (cosine, column, whole),
+            (sine, column, whole),
+        ],
+        [
+            ((rows, width), f32, column, head),
+            ((rows, width), f32, column, head),
+            ((rows, width), bf16, column, head),
+            ((2, rows), f32, (2, rows), whole),
+            ((2, width), f32, (2, HD), head),
+        ],
+        scratch=[pltpu.VMEM((rows, HD), f32)] * 3,
+        flops=10 * rows * rows * width,
+        mib=56,
+    )
+
+
+def unscale(gained, projected, squares, dots, which, full_width):
+    rows, cols = gained.shape
+    tile = rows // 2
+
+    def kernel(gained_ref, proj_ref, sum_ref, dot_ref, out_ref):
+        scale = lax.rsqrt(sum_ref[which : which + 1] / full_width + epsilon)
+        inner = scale**3 / full_width * dot_ref[which : which + 1]
+        scale, inner = as_column(scale), as_column(inner)
+        for start in range(0, cols, HD):
+            lanes = slice(start, start + HD)
+            out_ref[:, lanes] = (
+                scale * gained_ref[:, lanes] - proj_ref[:, lanes] * inner
+            ).astype(bf16)
+
+    row = lambda i: (i, 0)
+    column = lambda i: (0, i)
+    return matmul_call(
+        kernel,
+        rows // tile,
+        [
+            (gained, (tile, cols), row),
+            (projected, (tile, cols), row),
+            (squares, (2, tile), column),
+            (dots, (2, tile), column),
+        ],
+        [((rows, cols), bf16, (tile, cols), row)],
+    )[0]
+
+
+def fast_add(left, right):
+    rows, cols = left.shape
+    tile = rows // 2
+
+    def kernel(left_ref, right_ref, out_ref):
+        out_ref[...] = (left_ref[...].astype(f32) + right_ref[...].astype(f32)).astype(bf16)
+
+    row = lambda i: (i, 0)
+    return matmul_call(
+        kernel,
+        rows // tile,
+        [(left, (tile, cols), row), (right, (tile, cols), row)],
+        [((rows, cols), bf16, (tile, cols), row)],
+        mib=12,
+    )[0]
+
+
+def pick_and_place(target, shape, use_first, first, second, row_block, col_block):
+    rows, cols = first.shape
+    tile = rows // 4
+    steps = 4
+
+    def kernel(spot_ref, first_ref, second_ref, *refs):
+        low_ref, wide_ref = refs[-2:]
+
+        @pl.when(spot_ref[2] == 1)
+        def _():
+            low_ref[...] = first_ref[...]
+            wide_ref[...] = first_ref[...].astype(f32)
+
+        @pl.when(spot_ref[2] != 1)
+        def _():
+            low_ref[...] = second_ref[...]
+            wide_ref[...] = second_ref[...].astype(f32)
+
+    spots = jnp.stack(
+        [jnp.int32(row_block) * steps, jnp.int32(col_block), use_first.astype(jnp.int32)]
+    )
+    in_specs = [
+        pl.BlockSpec((tile, cols), lambda i, spot: (i * spot[2], 0)),
+        pl.BlockSpec((tile, cols), lambda i, spot: (i * (1 - spot[2]), 0)),
+    ]
+    operands = [spots, first, second]
+    aliases = {}
+    if target is not None:
+        in_specs.append(pl.BlockSpec(memory_space=pl.ANY))
+        operands.append(target)
+        aliases = {3: 1}
+    return pl.pallas_call(
+        kernel,
+        out_shape=[jax.ShapeDtypeStruct(first.shape, bf16), jax.ShapeDtypeStruct(shape, f32)],
+        grid_spec=pltpu.PrefetchScalarGridSpec(
+            num_scalar_prefetch=1,
+            grid=(steps,),
+            in_specs=in_specs,
+            out_specs=[
+                pl.BlockSpec((tile, cols), lambda i, spot: (i, 0)),
+                pl.BlockSpec((tile, cols), lambda i, spot: (spot[0] + i, spot[1])),
+            ],
+        ),
+        input_output_aliases=aliases,
+        cost_estimate=pl.CostEstimate(
+            flops=rows * cols, bytes_accessed=8 * rows * cols, transcendentals=0
+        ),
+        name="pick_and_place",
+    )(*operands)
+
+
+ORDER = [
+    -3, -2, 1, -4, 6, -8, -7, 5, 11, -12, 206, -207, 13, -14, -9, 15, 16, 17, 18, -19,
+    10, 20, -21, 25, 26, -27, 194, -208, 28, -29, 209, 22, -23, -117, 24, 33, 34, -35, -119, 30,
+    -31, -118, 36, -37, 32, 41, 42, -43, -120, 54, 38, -39, 44, -45, 121, 40, 114, 166, -167, 46,
+    -47, 116, 48, 55, 72, -73, 115, 144, -145, 56, 57, -58, 85, 86, 122, -123, 173, -87, -174, 74,
+    -76, 75, 146, -147, 59, -60, 124, 77, -78, 155, -125, -156, 175, -176, 88, -89, 90, 133, 61, 62,
+    -63, -134, 168, -169, 79, -80, -81, 51, -52, 177, -178, 91, -92, 157, -158, 148, -149, 179, -82, 170,
+    -171, 180, -181, 64, -65, 135, -136, 126, -127, 93, -94, 172, 185, 150, -151, 195, -196, 186, 187, -188,
+    159, -160, 210, -211, 128, -129, 152, -153, 189, -190, 197, -198, 95, -96, 137, -138, 191, 193, 232, -233,
+    192, 161, -162, 199, -200, 130, -131, 154, 66, -67, 212, -213, 101, 234, -97, 139, -140, -235, 49, -50,
+    163, -164, 243, -68, -102, -245, -246, 201, -202, 132, 214, -215, 53, 221, -222, 182, -98, -183, 236, 141,
+    184, -237, 244, -69, -142, 165, 203, -204, 223, -224, 216, -217, 103, -105, 104, 247, -248, 250, -251, 70,
+    238, 252, -253, -239, 225, -226, 71, 83, 84, 99, 100, 106, -107, 254, 218, -219, 143, 205, 227, -228,
+    249, 240, -241, 108, -109, -110, 229, -255, 220, -111, 112, -230, 242, 256, -257, 258, -259, 260, -261, 113,
+    262, 231,
+]
+
+
+class Handle:
+    def __init__(self, task, index=None):
+        self.task, self.index = task, index
+
+
+class Task:
+    def __init__(self, function, inputs, link):
+        self.function, self.inputs, self.link, self.values = function, inputs, link, None
+        self.handle = Handle(self, 0)
+
+
+class Plan:
+    window = 2
+
+    def __init__(self):
+        self.tasks = []
+
+    def add(self, function, inputs, link):
+        task = Task(function, inputs, link)
+        self.tasks.append(task)
+        return task
+
+    def step(self, cost, function, *inputs, outs=1):
+        task = self.add(function, inputs, ())
+        if outs == 1:
+            return task.handle
+        return (task.handle, *[Handle(task, k) for k in range(1, outs)])
+
+    def move(self, link, function, value):
+        links = {"y": ("y_middle", "y_end")}.get(link, (link,))
+        return self.add(function, (value,), links).handle
+
+    def run(self):
+        last, sent = None, {}
+
+        def fence(task, extra):
+            handles = list(task.inputs) + [h for h in extra if h not in task.inputs]
+            values = [h.task.values[h.index] if isinstance(h, Handle) else h for h in handles]
+            if extra:
+                values = lax.optimization_barrier(tuple(values))
+                for handle, fresh in zip(handles, values):
+                    if isinstance(handle, Handle):
+                        handle.task.values[handle.index] = fresh
+            return values[: len(task.inputs)]
+
+        for number in ORDER:
+            task = self.tasks[abs(number) - 1]
+            extra = [last] if last is not None else []
+            for link in task.link:
+                earlier = sent.setdefault(link, [])
+                if len(earlier) >= self.window and earlier[-self.window] not in extra:
+                    extra.append(earlier[-self.window])
+                earlier.append(task.handle)
+            fenced = fence(task, extra)
+            result = task.function(*fenced)
+            task.values = list(result) if isinstance(result, (tuple, list)) else [result]
+            if number > 0:
+                last = task.handle
+
+
+def in_order(rank, *pieces):
+    rows, cols = pieces[0].shape
+    tile = rows // 4
+
+    def kernel(rank_ref, *refs):
+        for k in range(4):
+            start = pl.multiple_of((rank_ref[0] ^ k) * cols, cols)
+            refs[4][:, pl.ds(start, cols)] = refs[k][...]
+
+    return pl.pallas_call(
+        kernel,
+        out_shape=jax.ShapeDtypeStruct((rows, 4 * cols), pieces[0].dtype),
+        grid_spec=pltpu.PrefetchScalarGridSpec(
+            num_scalar_prefetch=1,
+            grid=(rows // tile,),
+            in_specs=[pl.BlockSpec((tile, cols), lambda i, rank: (i, 0))] * 4,
+            out_specs=pl.BlockSpec((tile, 4 * cols), lambda i, rank: (i, 0)),
+        ),
+        cost_estimate=pl.CostEstimate(
+            flops=rows * cols, bytes_accessed=16 * rows * cols, transcendentals=0
+        ),
+        name="in_order",
+    )(rank[None], *pieces)
+
+
+def fast_body(
+    tokens,
+    segments,
+    cotangent,
+    w_query,
+    w_key,
+    w_value,
+    w_out,
+    w_gate,
+    w_up,
+    w_down,
+    gain_query,
+    gain_key,
+    gain_attn,
+    gain_mlp,
+):
+    full_width = w_query.shape[0]
+    row_count, narrow = tokens.shape
+    local_width = w_query.shape[1]
+    units = w_gate.shape[1]
+    rank = lax.axis_index("tensor")
+    core = rank % 2
+    dp_rank = lax.axis_index("dp")
+    y = dp_rank % 2
+    z = dp_rank // 2
+    z_side = z // 2
+    outer = (z == 0) | (z == 3)
+    chunks = 2
+    chunk = row_count // chunks
+    half = chunk // 2
+
+    plan = Plan()
+    step = plan.step
+
+    def core_move(value):
+        return plan.move("core", to_core, value)
+
+    def x_move(value):
+        return plan.move("x", to_x, value)
+
+    def y_move(value):
+        return plan.move("y", lambda v: over_dp(v, SWAP_Y), value)
+
+    def y_move_at(where, value):
+        pairs = {"middle": SWAP_Y_MIDDLE, "end": SWAP_Y_END}[where]
+        return plan.move("y_" + where, lambda v: over_dp(v, pairs), value)
+
+    def z_move(which, value):
+        pairs = {"in": Z_IN, "mid": Z_MID, "out": Z_OUT}[which]
+        return plan.move(which, lambda v: over_dp(v, pairs), value)
+
+    def gathered(value):
+        across = x_move(value)
+        pieces = (value, core_move(value), across, core_move(across))
+        return across, step(5.0, lambda *p: in_order(rank, *p), *pieces)
+
+    def prepare(value):
+        cosine, sine = tables(segments)
+        return value, cosine[0], sine[0]
+
+    _, cosine, sine = step(6.0, prepare, tokens, outs=3)
+    across, whole_x = gathered(tokens)
+    held_dy = step(0.0, lambda v, _: v, cotangent, across)
+    _, whole_dy = gathered(held_dy)
+
+    def small_sum(value):
+        value = step(0.6, lambda a, b: a + b, value, core_move(value))
+        return step(0.6, lambda a, b: a + b, value, x_move(value))
+
+    query_proj, key_proj, value_low, squares = step(
+        11.0, lambda x: project(x, w_query, w_key, w_value), whole_x, outs=4
+    )
+    squares = small_sum(squares)
+
+    query_rot, key_rot = step(
+        6.0,
+        lambda q, k, s, cos, sin: turn_heads(q, k, s, full_width, gain_query, gain_key, cos, sin),
+        query_proj,
+        key_proj,
+        squares,
+        cosine,
+        sine,
+        outs=2,
+    )
+
+    def attend(query, key, value, j):
+        per = chunk // BLOCK
+        blocks = list(range(j * per, (j + 1) * per))
+        block = attend_heads(query, key, value, segments, blocks)
+        return jnp.concatenate([part(block, core, half, 0), part(block, 1 - core, half, 0)], 0)
+
+    def own_rows(value, j):
+        return lax.dynamic_slice_in_dim(value, j * chunk + core * half, half, 0)
+
+    def halves(value):
+        value = value.astype(bf16)
+        return value[:half], value[half:]
+
+    def chip_sum(keep, give):
+        chip = step(1.8, fast_add, keep, core_move(give))
+        return chip, x_move(chip)
+
+    def both(value):
+        return step(2.0, lambda a, b: jnp.concatenate([a, b], 0), value, core_move(value))
+
+    mixed, attn_total, attn_scale, hid, own_low, hid_low = [], [], [], [], [], []
+    for j in range(chunks):
+        block = step(
+            8.0 + j,
+            lambda q, k, v, j=j: attend(q, k, v, j),
+            query_rot,
+            key_rot,
+            value_low,
+        )
+        mixed.append(block)
+        keep, give = step(3.0, lambda m: halves(dot(m, w_out)), block, outs=2)
+        chip, away = chip_sum(keep, give)
+
+        def join(chip, away, x, j=j):
+            total = chip.astype(f32) + away.astype(f32)
+            scale = lax.rsqrt(jnp.sum(total * total, 1, keepdims=True) / full_width + epsilon)
+            hidden = own_rows(x, j).astype(f32) + total * scale * gain_attn
+            return total, scale, hidden, hidden.astype(bf16)
+
+        total, scale, hidden, low = step(5.0, join, chip, away, whole_x, outs=4)
+        attn_total.append(total)
+        attn_scale.append(scale)
+        hid.append(hidden)
+        own_low.append(low)
+        hid_low.append(both(low))
+
+    gate, up, act, out_rows, branch_low, mlp_gains = [], [], [], [], [], []
+    for j in range(chunks):
+        g, u, a = step(14.5, lambda low: feed(low, w_gate, w_up), hid_low[j], outs=3)
+        gate.append(g)
+        up.append(u)
+        act.append(a)
+        keep, give = step(5.0, lambda a: halves(dot(a, w_down)), a, outs=2)
+        chip, away = chip_sum(keep, give)
+
+        def finish(chip, away, hidden, dy, j=j):
+            branch = chip.astype(f32) + away.astype(f32)
+            scale = lax.rsqrt(jnp.sum(branch * branch, 1, keepdims=True) / full_width + epsilon)
+            normed = branch * scale
+            dy_rows = own_rows(dy, j).astype(f32)
+            gained = gain_mlp * dy_rows
+            inner = jnp.sum(gained * branch, 1, keepdims=True)
+            low = (scale * gained - branch * scale**3 / full_width * inner).astype(bf16)
+            return low, (hidden + normed * gain_mlp).astype(bf16), jnp.sum(dy_rows * normed, 0)
+
+        low, rows, gains = step(8.0, finish, chip, away, hid[j], whole_dy, outs=3)
+        branch_low.append(both(low))
+        out_rows.append(rows)
+        mlp_gains.append(gains)
+
+    def own_columns(blocks):
+        keeps, comes = [], []
+        for block in blocks:
+            keep, give = step(
+                1.5,
+                lambda b: (
+                    lax.dynamic_slice_in_dim(b, rank * narrow, narrow, 1),
+                    lax.dynamic_slice_in_dim(b, (rank ^ 1) * narrow, narrow, 1),
+                ),
+                block,
+                outs=2,
+            )
+            keeps.append(keep)
+            comes.append(core_move(give))
+
+        def merge(*values):
+            pieces = []
+            for keep, came in zip(values[:chunks], values[chunks:]):
+                pieces += [jnp.where(core == 0, keep, came), jnp.where(core == 0, came, keep)]
+            return jnp.concatenate(pieces, 0)
+
+        return step(2.0, merge, *keeps, *comes)
+
+    output = own_columns(out_rows)
+
+    def joined(*values):
+        return jnp.concatenate(values, 0)
+
+    def chosen(which):
+        return lambda own, came: low_add(
+            part(own, which, own.shape[0] // 2, 0), part(came, which, came.shape[0] // 2, 0)
+        )
+
+    def half_of(which):
+        return lambda own: part(own, which, own.shape[0] // 2, 0)
+
+    def line_sum(own, mib):
+        near = step(0.6 + 1.6 * mib, fast_add, own, z_move("in", own))
+        total = step(0.6 + 1.6 * mib, fast_add, near, z_move("mid", near))
+        return z_move("out", total), total
+
+    def put(target, shape, spots, first, second, mib):
+        if target is None:
+            run = lambda a, b: pick_and_place(None, shape, outer, a, b, *spots)
+            return step(1.0 + 2.2 * mib, run, first, second, outs=2)
+        run = lambda a, b, t: pick_and_place(t, shape, outer, a, b, *spots)
+        return step(1.0 + 2.2 * mib, run, first, second, target, outs=2)
+
+    def set_down(target, shape, spots, value, mib):
+        run = lambda v, t: place(t, shape, v, *spots)
+        return step(0.8 + 1.7 * mib, run, value, target)
+
+    def put_only(target, shape, spots, first, second, mib):
+        run = lambda a, b, *t: place_one(*(t or (None,)), shape, outer, a, b, *spots)
+        rest = () if target is None else (target,)
+        return step(0.8 + 1.7 * mib, run, first, second, *rest)
+
+    def sum_middle(own, mib):
+        came = z_move("in", own)
+        send = step(0.8 * mib, chosen(1 - z_side), own, came)
+        keep = step(0.8 * mib, chosen(z_side), own, came)
+        keep = step(0.8 * mib, fast_add, keep, z_move("mid", send))
+        keep = step(0.8 * mib, fast_add, keep, y_move_at("middle", keep))
+        other = z_move("mid", keep)
+        return (z_move("out", keep), keep), (z_move("out", other), other)
+
+    def sum_ends(own, mib):
+        far = step(0.5 * mib, half_of(1 - z_side), own)
+        came = z_move("in", far)
+        came = z_move("mid", step(0.8 * mib, fast_add, far, came))
+        near = step(0.5 * mib, half_of(z_side), own)
+        came = z_move("out", step(0.8 * mib, fast_add, near, came))
+        root = step(0.8 * mib, fast_add, near, came)
+        root = step(0.8 * mib, fast_add, root, y_move_at("end", root))
+        first = z_move("in", root)
+        second = z_move("mid", first)
+        third = z_move("out", second)
+        return (root, first), (third, second)
+
+    quarter = units // 4
+    whole_act = step(3.0, joined, *act)
+    whole_branch_low = step(3.0, joined, *branch_low)
+    down_grad = None
+    for k in range(4):
+        block = step(
+            5.0,
+            lambda a, b, k=k: dot(a[:, k * quarter : (k + 1) * quarter], b, 0, 0).astype(bf16),
+            whole_act,
+            whole_branch_low,
+        )
+        summed = (sum_middle if k % 2 else sum_ends)(block, 2.0)
+        for side, pair in ((z_side, summed[0]), (1 - z_side, summed[1])):
+            spot = (2 * k + side, 0)
+            down_grad = put_only(down_grad, (units, full_width), spot, *pair, 1.0)
+
+    gate_low, up_low = [], []
+    for j in range(chunks):
+        g, u = step(
+            12.0,
+            lambda low, gate, up: unfeed(low, w_down, gate, up),
+            branch_low[j],
+            gate[j],
+            up[j],
+            outs=2,
+        )
+        gate_low.append(g)
+        up_low.append(u)
+
+    whole_hid = step(3.0, joined, *hid_low)
+    came = [y_move(low) for low in own_low]
+    beside = [core_move(c) for c in came]
+    neighbour_hid = step(
+        3.0, lambda a0, a1, b0, b1: joined(a0, b0, a1, b1), *came, *beside
+    )
+    mid = units // 2
+    piece_cols = mid // 2
+
+    wide = []
+    for lows in (gate_low, up_low):
+        result = None
+        for q in range(2):
+            def cut(g0, g1, q=q):
+                def columns(which):
+                    start = which * mid + q * piece_cols
+                    return joined(
+                        *[lax.dynamic_slice_in_dim(g, start, piece_cols, 1) for g in (g0, g1)]
+                    )
+
+                return columns(y), columns(1 - y)
+
+            keep, give = step(2.5, cut, *lows, outs=2)
+            own = step(
+                10.0,
+                lambda h, k, n, c: (dot(h, k, 0, 0) + dot(n, c, 0, 0)).astype(bf16),
+                whole_hid,
+                keep,
+                neighbour_hid,
+                y_move(give),
+            )
+            shape = (full_width, units)
+            piece, result = put(result, shape, (0, 2 * y + q), *line_sum(own, 2.0), 2.0)
+            result = set_down(result, shape, (0, 2 * (1 - y) + q), y_move(piece), 2.0)
+        wide.append(result)
+    gate_grad, up_grad = wide
+
+    hidden_grad, attn_low, attn_gains = [], [], []
+    for j in range(chunks):
+        keep, give = step(
+            14.0,
+            lambda g, u: unwide(g, u, w_gate, w_up),
+            gate_low[j],
+            up_low[j],
+            outs=2,
+        )
+        chip, away = chip_sum(keep, give)
+
+        def unjoin(chip, away, dy, total, scale, j=j):
+            grad = own_rows(dy, j).astype(f32) + (chip.astype(f32) + away.astype(f32))
+            gained = gain_attn * grad
+            inner = jnp.sum(gained * total, 1, keepdims=True)
+            low = (scale * gained - total * scale**3 / full_width * inner).astype(bf16)
+            return low, grad, jnp.sum(grad * total * scale, 0)
+
+        low, grad, gains = step(
+            8.0, unjoin, chip, away, whole_dy, attn_total[j], attn_scale[j], outs=3
+        )
+        hidden_grad.append(grad)
+        attn_gains.append(gains)
+        attn_low.append(both(low))
+    grad_own = own_columns(hidden_grad)
+    whole_attn_low = step(3.0, joined, *attn_low)
+
+    def unmix(low):
+        grad = dot(low, w_out, 1, 1).astype(bf16)
+        ordered = []
+        for j in range(chunks):
+            block = grad[j * chunk : (j + 1) * chunk]
+            ordered += [part(block, core, half, 0), part(block, 1 - core, half, 0)]
+        return jnp.concatenate(ordered, 0)
+
+    mixed_grad = step(6.0, unmix, whole_attn_low)
+
+    query_gained, key_gained, value_grad_low, dots, head_gains = step(
+        21.0,
+        lambda q, k, v, m, qp, kp, s, cos, sin: unattend_heads(
+            q, k, v, m, segments, qp, kp, s, full_width, gain_query, gain_key, cos, sin
+        ),
+        query_rot,
+        key_rot,
+        value_low,
+        mixed_grad,
+        query_proj,
+        key_proj,
+        squares,
+        cosine,
+        sine,
+        outs=5,
+    )
+    dots = small_sum(dots)
+
+    def scaled_back(which, gained, projected):
+        run = lambda g, p, s, d: unscale(g, p, s, d, which, full_width)
+        return step(4.5, run, gained, projected, squares, dots)
+
+    query_low = scaled_back(0, query_gained, query_proj)
+    key_low = scaled_back(1, key_gained, key_proj)
+
+    def pair_grad(left, right, shape):
+        rows = shape[0] // 2
+        give = step(
+            3.0, lambda a, b: dot(part(a, 1 - y, rows, 1), b, 0, 0).astype(bf16), left, right
+        )
+        own = step(
+            3.5,
+            lambda a, b, c: (dot(part(a, y, rows, 1), b, 0, 0) + c.astype(f32)).astype(bf16),
+            left,
+            right,
+            y_move(give),
+        )
+        piece, result = put(None, shape, (y, 0), *line_sum(own, 1.0), 1.0)
+        return set_down(result, shape, (1 - y, 0), y_move(piece), 1.0)
+
+    whole_mixed = step(1.5, joined, *mixed)
+    out_grad = pair_grad(whole_mixed, whole_attn_low, (local_width, full_width))
+
+    x_own = step(2.5, lambda x: part(x, core, row_count // 2, 0), whole_x)
+    x_came = y_move(x_own)
+    neighbour_x = step(3.0, joined, x_came, core_move(x_came))
+
+    def core_first(value):
+        rows = row_count // 2
+        return joined(part(value, core, rows, 0), part(value, 1 - core, rows, 0))
+
+    def narrow_grad(low):
+        columns = local_width // 2
+        keep, give = step(
+            1.5, lambda v: (part(v, y, columns, 1), part(v, 1 - y, columns, 1)), low, outs=2
+        )
+        own = step(
+            5.0,
+            lambda x, k, n, c: (dot(x, k, 0, 0) + dot(n, core_first(c), 0, 0)).astype(bf16),
+            whole_x,
+            keep,
+            neighbour_x,
+            y_move(give),
+        )
+        shape = (full_width, local_width)
+        piece, result = put(None, shape, (0, y), *line_sum(own, 1.0), 1.0)
+        return set_down(result, shape, (0, 1 - y), y_move(piece), 1.0)
+
+    value_wgrad = narrow_grad(value_grad_low)
+    query_wgrad = narrow_grad(query_low)
+    key_wgrad = narrow_grad(key_low)
+
+    def column_part(which):
+        def run(query_low, key_low, value_low):
+            pieces = []
+            for x in (0, 1):
+                rows = (2 * x + which) * narrow
+                total = 0.0
+                for low, weight in ((query_low, w_query), (key_low, w_key), (value_low, w_value)):
+                    total = total + dot(
+                        low, lax.dynamic_slice_in_dim(weight, rows, narrow, 0), 1, 1
+                    )
+                pieces.append(total.astype(bf16))
+            return pieces
+
+        return run
+
+    lows = (query_low, key_low, value_grad_low)
+    give0, give1 = step(7.0, column_part(1 - core), *lows, outs=2)
+    keep0, keep1 = step(7.0, column_part(core), *lows, outs=2)
+    x_here = rank // 2
+
+    def chip_columns(k0, k1, g0, g1):
+        k0, k1 = low_add(k0, g0), low_add(k1, g1)
+        first = x_here == 0
+        return jnp.where(first, k0, k1), jnp.where(first, k1, k0)
+
+    here, there = step(3.0, chip_columns, keep0, keep1, core_move(give0), core_move(give1), outs=2)
+    input_grad = step(
+        2.0,
+        lambda a, b, c: (a.astype(f32) + b.astype(f32) + c).astype(bf16),
+        here,
+        x_move(there),
+        grad_own,
+    )
+
+    wide_gains = step(
+        1.0, lambda a, b, c, d: jnp.stack([a + b, c + d]), *mlp_gains, *attn_gains
+    )
+
+    def masked(a, b):
+        mine = jnp.arange(full_width) // (full_width // 2) == rank // 2
+        return jnp.where(mine, a + b, 0.0)
+
+    wide_gains = step(1.0, masked, wide_gains, core_move(wide_gains))
+    gains = step(
+        1.0,
+        lambda a, b, h: jnp.concatenate([(a + b).reshape(-1), h.reshape(-1)]),
+        wide_gains,
+        x_move(wide_gains),
+        head_gains,
+    )
+    gains = step(0.6, lambda a, b: a + b, gains, y_move(gains))
+    gains = step(0.6, lambda a, b: a + b, gains, z_move("in", gains))
+    gains = step(0.6, lambda a, b: a + b, gains, z_move("mid", gains))
+    gains = step(0.6, lambda a, b: jnp.where(outer, a, b), z_move("out", gains), gains)
+
+    plan.run()
+    results = (
+        output,
+        input_grad,
+        query_wgrad,
+        key_wgrad,
+        value_wgrad,
+        out_grad,
+        gate_grad,
+        up_grad,
+        down_grad,
+        gains,
+    )
+    values = [r.task.values[r.index] for r in results]
+    gains = values.pop()
+    return (
+        *values,
+        gains[2 * full_width : 2 * full_width + local_width],
+        gains[2 * full_width + local_width :],
+        gains[full_width : 2 * full_width],
+        gains[:full_width],
+    )
+
+
 def solution(mesh):
     in_specs = (
         P("dp", "tensor"),
@@ -358,4 +1474,5 @@
         P(),
         P(),
     )
+    body = fast_body if dict(mesh.shape) == {"dp": 8, "tensor": 4} else general_body
     return jax.shard_map(body, mesh=mesh, in_specs=in_specs, out_specs=out_specs, check_vma=False)

time: 2050 us -> 1090 us (0.53)
  waiting for transfers between devices: 1450 us -> 379 us
  Pallas kernels: 0 us -> 277 us
  starting transfers between devices: 1.55 us -> 165 us
  matrix products: 245 us -> 104 us
  blocking collectives: 107 us -> 0 us
  other arithmetic: 150 us -> 94.9 us
    reduce_scatter x8 -> x0, waiting for transfers between devices: 697 us -> none  [the longest x1 150 us: body(): lax.psum_scatter(down_wgrad.astype(jnp.bfloat16), 'dp', scatter_dimension...]
    all_gather x9 -> x0, waiting for transfers between devices: 500 us -> none  [the longest x1 123 us: body(): lax.all_gather(pieces[4].astype(jnp.bfloat16), 'dp', axis=0, tiled=True)]
    ppermute x0 -> x113, waiting for transfers between devices: none -> 379 us  [the longest x73 320 us: over_dp(): return lax.ppermute(value, 'dp', pairs)]
    pallas_call x0 -> x73, Pallas kernels: none -> 277 us  [the longest x47 164 us: matmul_call(): pl.pallas_call(kernel, out_shape=[jax.ShapeDtypeStruct(s, d) for s, d, _,...]
    psum x3 -> x0, waiting for transfers between devices: 255 us -> none  [the longest x1 86.7 us: body(): lax.psum(attn_part.astype(jnp.bfloat16), 'tensor').astype(jnp.float32)]
    ppermute x0 -> x113, starting transfers between devices: none -> 165 us  [the longest x73 146 us: over_dp(): return lax.ppermute(value, 'dp', pairs)]
    dot_general x35 -> x37, matrix products: 245 us -> 104 us  [dot(): lax.dot_general(left, right, (((left_axis,), (right_axis,)), ((), ())), p...]
    convert_element_type x20 -> x11, other arithmetic: 85.2 us -> 27.6 us  [the longest x4 9.75 us: low_add(): return (left.astype(f32) + right.astype(f32)).astype(bf16)]
  transfers between devices with their start and end apart: 20 -> 113, of which waited for: 18 -> 37; matrix products, arithmetic and copies ran while one was open for 7% -> 18% of each run, Pallas kernels for 0% -> 25%
where the time goes in v1:
time: 1090 us; the launch traced here: 1080 us
  waiting for transfers between devices  379 us (35%)
  Pallas kernels  277 us (25%)
  starting transfers between devices  165 us (15%)
  matrix products  104 us (10%)
  other arithmetic  94.9 us (9%)
  local copies, waits for them, and re-layouts  56.8 us (5%)
    ppermute x73, waiting for transfers between devices, over_dp(): return lax.ppermute(value, 'dp', pairs)  320 us
    pallas_call x47, Pallas kernels, matmul_call(): pl.pallas_call(kernel, out_shape=[jax.ShapeDtypeStruct(s, d) for s, d, _,...  164 us
    ppermute x73, starting transfers between devices, over_dp(): return lax.ppermute(value, 'dp', pairs)  146 us
    dot_general x37, matrix products, dot(): lax.dot_general(left, right, (((left_axis,), (right_axis,)), ((), ())), p...  104 us
    ppermute x12, waiting for transfers between devices, to_x(): return lax.ppermute(value, 'tensor', SWAP_X)  52 us
    pallas_call x8, Pallas kernels, pick_and_place(): pl.pallas_call(kernel, out_shape=[jax.ShapeDtypeStruct(first.shape, bf16)...  40.8 us
    unnamed x278, local copies, waits for them, and re-layouts  39.3 us
    pallas_call x8, Pallas kernels, place(): pl.pallas_call(kernel, out_shape=jax.ShapeDtypeStruct(shape, f32), grid_s...  34.1 us
  transfers between devices with their start and end apart: 113, of which 37 were waited for; matrix products, arithmetic and copies ran while one was open for 18% of the time, Pallas kernels for 25%

profile of v1, /device:TPU:0, one launch (start us, length us, event | category | flops | bytes accessed | tf_op | source)
XLA Modules:
  0.0 1079.2 jit_solution(17655282081348301996)
XLA Ops:
  4.6 22.4 %collective-permute-done.refs_2_ = bf16[1024,512]{1,0:T(8,128)(2,1)S(1)} collective-permute-done((bf16[1024,512]{1,0:T(8,128)(2,1)}, bf16[1024,512]{1,0:T(8,128)(2,1)S(1)}, u32[]{:S(2)}, u32[]{:S(2)}) %collective-permute-start) | collective-permute-done | bytes 1048608 | tf_op jit(solution)/shard_map/ppermute | solution.py:356
  42.8 7.2 shard_map.237
  89.7 29.9 %collective-permute-done.10 = bf16[512,2048]{1,0:T(8,128)(2,1)} collective-permute-done((bf16[512,2048]{1,0:T(8,128)(2,1)}, bf16[512,2048]{1,0:T(8,128)(2,1)}, u32[]{:S(2)}, u32[]{:S(2)}) %collective-permute-start.10) | collective-permute-done | bytes 2097184 | tf_op jit(solution)/shard_map/ppermute | solution.py:348
  134.1 11.5 %collective-permute-done.11 = bf16[256,2048]{1,0:T(8,128)(2,1)} collective-permute-done((bf16[256,2048]{1,0:T(8,128)(2,1)}, bf16[256,2048]{1,0:T(8,128)(2,1)}, u32[]{:S(2)}, u32[]{:S(2)}) %collective-permute-start.11) | collective-permute-done | bytes 1048608 | tf_op jit(solution)/shard_map/ppermute | solution.py:356
  159.2 13.9 %shard_map.243 = (bf16[512,2048]{1,0:T(8,128)(2,1)}, bf16[512,2048]{1,0:T(8,128)(2,1)}, bf16[512,2048]{1,0:T(8,128)(2,1)}) custom-call(bf16[512,2048]{1,0:T(8,128)(2,1)} %pad_maximum_fusion.6.low_ref, bf16[2048,2048]{1,0:T(8,128)(2,1)} %gate_w.7, bf16[2048,2048]{1,0:T(8,128)(2,1)} %up_w.7), custom_call_target="tpu_custom_call" | custom-call | flops 8589934592 | bytes 25165824 | tf_op jit(solution)/shard_map/pallas_call | solution.py:451
  173.1 8.5 convolution_convert_fusion.5
  191.8 13.7 %shard_map.245 = (bf16[512,2048]{1,0:T(8,128)(2,1)}, bf16[512,2048]{1,0:T(8,128)(2,1)}, bf16[512,2048]{1,0:T(8,128)(2,1)}) custom-call(bf16[512,2048]{1,0:T(8,128)(2,1)} %pad_maximum_fusion.7.low_ref, bf16[2048,2048]{1,0:T(8,128)(2,1)} %gate_w.7, bf16[2048,2048]{1,0:T(8,128)(2,1)} %up_w.7), custom_call_target="tpu_custom_call" | custom-call | flops 8589934592 | bytes 25165824 | tf_op jit(solution)/shard_map/pallas_call | solution.py:451
  205.6 8.5 convolution_convert_fusion.4
  234.0 11.4 %shard_map.247 = (bf16[512,2048]{1,0:T(8,128)(2,1)}, bf16[512,2048]{1,0:T(8,128)(2,1)}) custom-call(bf16[512,2048]{1,0:T(8,128)(2,1)} %pad_maximum_fusion.8.low_ref, bf16[2048,2048]{1,0:T(8,128)(2,1)} %down_w.3, bf16[512,2048]{1,0:T(8,128)(2,1)} %get-tuple-element.814.gate_ref, bf16[512,2048]{1,0:T(8,128)(2,1)} %get-tuple-element.815.up_ref), custom_call_target="tpu_custom_call" | custom-call | flops 4294967296 | bytes 18874368 | tf_op jit(solution)/shard_map/pallas_call | solution.py:451
  245.5 14.2 %shard_map.248 = (bf16[256,2048]{1,0:T(8,128)(2,1)}, bf16[256,2048]{1,0:T(8,128)(2,1)}) custom-call(bf16[512,2048]{1,0:T(8,128)(2,1)} %get-tuple-element.912.dgate_ref, bf16[512,2048]{1,0:T(8,128)(2,1)} %get-tuple-element.893.dup_ref, bf16[2048,2048]{1,0:T(8,128)(2,1)} %gate_w.7, bf16[2048,2048]{1,0:T(8,128)(2,1)} %up_w.7), custom_call_target="tpu_custom_call" | custom-call | flops 8589934592 | bytes 23068672 | tf_op jit(solution)/shard_map/pallas_call | solution.py:451
  287.5 11.6 %shard_map.249 = (bf16[512,2048]{1,0:T(8,128)(2,1)}, bf16[512,2048]{1,0:T(8,128)(2,1)}) custom-call(bf16[512,2048]{1,0:T(8,128)(2,1)} %copy-done.77, bf16[2048,2048]{1,0:T(8,128)(2,1)} %down_w.3, bf16[512,2048]{1,0:T(8,128)(2,1)} %get-tuple-element.839.gate_ref, bf16[512,2048]{1,0:T(8,128)(2,1)} %get-tuple-element.840.up_ref), custom_call_target="tpu_custom_call" | custom-call | flops 4294967296 | bytes 18874368 | tf_op jit(solution)/shard_map/pallas_call | solution.py:451
  316.7 13.8 %shard_map.250 = (bf16[256,2048]{1,0:T(8,128)(2,1)}, bf16[256,2048]{1,0:T(8,128)(2,1)}) custom-call(bf16[512,2048]{1,0:T(8,128)(2,1)} %get-tuple-element.913.dgate_ref, bf16[512,2048]{1,0:T(8,128)(2,1)} %get-tuple-element.894.dup_ref, bf16[2048,2048]{1,0:T(8,128)(2,1)} %gate_w.7, bf16[2048,2048]{1,0:T(8,128)(2,1)} %up_w.7), custom_call_target="tpu_custom_call" | custom-call | flops 8589934592 | bytes 23068672 | tf_op jit(solution)/shard_map/pallas_call | solution.py:451
  372.5 52.9 %collective-permute-done.32.right_ref = bf16[256,2048]{1,0:T(8,128)(2,1)S(1)} collective-permute-done((bf16[256,2048]{1,0:T(8,128)(2,1)S(1)}, bf16[256,2048]{1,0:T(8,128)(2,1)S(1)}, u32[]{:S(2)}, u32[]{:S(2)}) %collective-permute-start.32) | collective-permute-done | bytes 1048608 | tf_op jit(solution)/shard_map/ppermute | solution.py:348
  435.7 14.6 %collective-permute-done.35 = bf16[256,2048]{1,0:T(8,128)(2,1)S(1)} collective-permute-done((bf16[256,2048]{1,0:T(8,128)(2,1)S(1)}, bf16[256,2048]{1,0:T(8,128)(2,1)S(1)}, u32[]{:S(2)}, u32[]{:S(2)}) %collective-permute-start.35) | collective-permute-done | bytes 1048608 | tf_op jit(solution)/shard_map/ppermute | solution.py:356
  454.2 21.6 %collective-permute-done.40.right_ref = bf16[256,2048]{1,0:T(8,128)(2,1)S(1)} collective-permute-done((bf16[256,2048]{1,0:T(8,128)(2,1)S(1)}, bf16[256,2048]{1,0:T(8,128)(2,1)S(1)}, u32[]{:S(2)}, u32[]{:S(2)}) %collective-permute-start.40) | collective-permute-done | bytes 1048608 | tf_op jit(solution)/shard_map/ppermute | solution.py:348
  495.0 9.4 collective-permute-done.45.first_ref
  510.6 19.6 %collective-permute-done.49 = bf16[1024,512]{1,0:T(8,128)(2,1)S(1)} collective-permute-done((bf16[1024,512]{1,0:T(8,128)(2,1)}, bf16[1024,512]{1,0:T(8,128)(2,1)S(1)}, u32[]{:S(2)}, u32[]{:S(2)}) %collective-permute-start.49) | collective-permute-done | bytes 1048608 | tf_op jit(solution)/shard_map/ppermute | solution.py:348
  569.4 9.3 collective-permute-done.52.right_ref
  581.0 7.2 collective-permute-done.56.right_ref
  591.9 19.1 %shard_map.264 = (f32[1024,512]{1,0:T(8,128)}, f32[1024,512]{1,0:T(8,128)}, bf16[1024,512]{1,0:T(8,128)(2,1)}, f32[2,1024]{1,0:T(2,128)}, f32[2,512]{1,0:T(2,128)}) custom-call(bf16[1024,512]{1,0:T(8,128)(2,1)} %copy-done.57, bf16[1024,512]{1,0:T(8,128)(2,1)} %copy-done.59, bf16[1024,512]{1,0:T(8,128)(2,1)} %copy-done.54, ...), custom_call_target="tpu_custom_call" | custom-call | flops 5368709120 | bytes 14708736 | tf_op jit(solution)/shard_map/pallas_call | solution.py:451
  638.6 6.8 collective-permute-start.64
  657.0 30.1 %collective-permute-done.62 = bf16[1024,256]{1,0:T(8,128)(2,1)} collective-permute-done((bf16[1024,256]{1,0:T(8,128)(2,1)}, bf16[1024,256]{1,0:T(8,128)(2,1)}, u32[]{:S(2)}, u32[]{:S(2)}) %collective-permute-start.62) | collective-permute-done | bytes 524320 | tf_op jit(solution)/shard_map/ppermute | solution.py:348
  687.8 6.6 collective-permute-start.67
  728.4 9.0 collective-permute-start.70
  746.5 11.6 %collective-permute-done.70.second_ref = bf16[256,2048]{1,0:T(8,128)(2,1)} collective-permute-done((bf16[256,2048]{1,0:T(8,128)(2,1)S(1)}, bf16[256,2048]{1,0:T(8,128)(2,1)}, u32[]{:S(2)}, u32[]{:S(2)}) %collective-permute-start.70) | collective-permute-done | bytes 1048608 | tf_op jit(solution)/shard_map/ppermute | solution.py:348
  777.4 6.5 collective-permute-done.73.right_ref
  847.6 17.2 %collective-permute-done.83.block_ref = bf16[2048,512]{1,0:T(8,128)(2,1)} collective-permute-done((bf16[2048,512]{1,0:T(8,128)(2,1)}, bf16[2048,512]{1,0:T(8,128)(2,1)}, u32[]{:S(2)}, u32[]{:S(2)}) %collective-permute-start.83) | collective-permute-done | bytes 2097184 | tf_op jit(solution)/shard_map/ppermute | solution.py:348
  917.3 12.5 %collective-permute-done.94.right_ref = bf16[2048,256]{1,0:T(8,128)(2,1)} collective-permute-done((bf16[2048,256]{1,0:T(8,128)(2,1)}, bf16[2048,256]{1,0:T(8,128)(2,1)}, u32[]{:S(2)}, u32[]{:S(2)}) %collective-permute-start.94) | collective-permute-done | bytes 1048608 | tf_op jit(solution)/shard_map/ppermute | solution.py:348
  994.2 12.3 %collective-permute-done.101.first_ref = bf16[2048,256]{1,0:T(8,128)(2,1)} collective-permute-done((bf16[2048,256]{1,0:T(8,128)(2,1)S(1)}, bf16[2048,256]{1,0:T(8,128)(2,1)}, u32[]{:S(2)}, u32[]{:S(2)}) %collective-permute-start.101) | collective-permute-done | bytes 1048608 | tf_op jit(solution)/shard_map/ppermute | solution.py:348
  1016.5 12.4 %collective-permute-done.104.first_ref = bf16[256,2048]{1,0:T(8,128)(2,1)} collective-permute-done((bf16[256,2048]{1,0:T(8,128)(2,1)}, bf16[256,2048]{1,0:T(8,128)(2,1)}, u32[]{:S(2)}, u32[]{:S(2)}) %collective-permute-start.104) | collective-permute-done | bytes 1048608 | tf_op jit(solution)/shard_map/ppermute | solution.py:348
  1039.3 15.6 %collective-permute-done.108 = f32[5120]{0:T(1024)S(1)} collective-permute-done((f32[5120]{0:T(1024)S(1)}, f32[5120]{0:T(1024)S(1)}, u32[]{:S(2)}, u32[]{:S(2)}) %collective-permute-start.108) | collective-permute-done | bytes 20512 | tf_op jit(solution)/shard_map/ppermute | solution.py:348
  1054.8 6.3 collective-permute-start.109
  (716 shorter events, 608.8 us)
Async XLA Ops:
  71.3 48.4 %collective-permute-start.10 = (bf16[512,2048]{1,0:T(8,128)(2,1)}, bf16[512,2048]{1,0:T(8,128)(2,1)}, u32[]{:S(2)}, u32[]{:S(2)}) collective-permute-start(bf16[512,2048]{1,0:T(8,128)(2,1)} %constant_dynamic-slice_fusion.48), channel_id=1, source_target_pairs={{0,4},{4,0},{8,12},{12,8},{16,20},{20,16},{24,28},{28,24},{1,5},{5... | collective-permute-start | bytes 6291464 | tf_op jit(solution)/shard_map/ppermute | solution.py:348
  268.6 63.9 %collective-permute-start.28 = (bf16[256,2048]{1,0:T(8,128)(2,1)}, bf16[256,2048]{1,0:T(8,128)(2,1)S(1)}, u32[]{:S(2)}, u32[]{:S(2)}) collective-permute-start(bf16[256,2048]{1,0:T(8,128)(2,1)} %get-tuple-element.867), channel_id=1, source_target_pairs={{0,1},{1,0},{2,3},{3,2},{4,5},{5,4},{6,7},{7,6},{8,9},{9,8},{10,11... | collective-permute-start | bytes 3145736 | tf_op jit(solution)/shard_map/ppermute | solution.py:352
  282.8 49.8 %collective-permute-start.26 = (bf16[512,2048]{1,0:T(8,128)(2,1)}, bf16[512,2048]{1,0:T(8,128)(2,1)}, u32[]{:S(2)}, u32[]{:S(2)}) collective-permute-start(bf16[512,2048]{1,0:T(8,128)(2,1)} %convolution_convert_fusion.3), channel_id=1, source_target_pairs={{0,8},{4,12},{24,16},{28,20},{1,9},{5,13},{25,17},{29,21},{2,10},{... | collective-permute-start | bytes 6291464 | tf_op jit(solution)/shard_map/ppermute | solution.py:348
  306.4 47.7 %collective-permute-start.31 = (bf16[256,2048]{1,0:T(8,128)(2,1)S(1)}, bf16[256,2048]{1,0:T(8,128)(2,1)S(1)}, u32[]{:S(2)}, u32[]{:S(2)}) collective-permute-start(bf16[256,2048]{1,0:T(8,128)(2,1)S(1)} %constant_dynamic-slice_fusion.39.left_ref), channel_id=1, source_target_pairs={{0,8},{4,12},{24,16},{28,20},{1,9},{5,13},{25,17},{29,21},{2,10},{... | collective-permute-start | bytes 3145736 | tf_op jit(solution)/shard_map/ppermute | solution.py:348
  354.1 133.1 %collective-permute-start.41 = (bf16[2048,512]{1,0:T(8,128)(2,1)S(1)}, bf16[2048,512]{1,0:T(8,128)(2,1)S(1)}, u32[]{:S(2)}, u32[]{:S(2)}) collective-permute-start(bf16[2048,512]{1,0:T(8,128)(2,1)S(1)} %add_convert_fusion.3.left_ref), channel_id=1, source_target_pairs={{0,8},{4,12},{24,16},{28,20},{1,9},{5,13},{25,17},{29,21},{2,10},{... | collective-permute-start | bytes 6291464 | tf_op jit(solution)/shard_map/ppermute | solution.py:348
  358.9 72.6 %collective-permute-start.36 = (bf16[256,2048]{1,0:T(8,128)(2,1)S(1)}, bf16[256,2048]{1,0:T(8,128)(2,1)S(1)}, u32[]{:S(2)}, u32[]{:S(2)}) collective-permute-start(bf16[256,2048]{1,0:T(8,128)(2,1)S(1)} %shard_map.251), channel_id=1, source_target_pairs={{8,16},{12,20},{16,8},{20,12},{9,17},{13,21},{17,9},{21,13},{10,18... | collective-permute-start | bytes 3145736 | tf_op jit(solution)/shard_map/ppermute | solution.py:348
  362.4 63.0 %collective-permute-start.32 = (bf16[256,2048]{1,0:T(8,128)(2,1)S(1)}, bf16[256,2048]{1,0:T(8,128)(2,1)S(1)}, u32[]{:S(2)}, u32[]{:S(2)}) collective-permute-start(bf16[256,2048]{1,0:T(8,128)(2,1)S(1)} %constant_dynamic-slice_fusion.38.left_ref), channel_id=1, source_target_pairs={{0,8},{4,12},{24,16},{28,20},{1,9},{5,13},{25,17},{29,21},{2,10},{... | collective-permute-start | bytes 3145736 | tf_op jit(solution)/shard_map/ppermute | solution.py:348
  364.0 62.2 %collective-permute-start.33 = (bf16[256,2048]{1,0:T(8,128)(2,1)S(1)}, bf16[256,2048]{1,0:T(8,128)(2,1)S(1)}, u32[]{:S(2)}, u32[]{:S(2)}) collective-permute-start(bf16[256,2048]{1,0:T(8,128)(2,1)S(1)} %copy-done.137), channel_id=1, source_target_pairs={{0,1},{1,0},{2,3},{3,2},{4,5},{5,4},{6,7},{7,6},{8,9},{9,8},{10,11... | collective-permute-start | bytes 3145736 | tf_op jit(solution)/shard_map/ppermute | solution.py:352
  370.1 134.3 %collective-permute-start.43 = (bf16[256,2048]{1,0:T(8,128)(2,1)S(1)}, bf16[256,2048]{1,0:T(8,128)(2,1)}, u32[]{:S(2)}, u32[]{:S(2)}) collective-permute-start(bf16[256,2048]{1,0:T(8,128)(2,1)S(1)} %shard_map.256), channel_id=1, source_target_pairs={{0,2},{1,3},{2,0},{3,1},{4,6},{5,7},{6,4},{7,5},{8,10},{9,11},{10,... | collective-permute-start | bytes 3145736 | tf_op jit(solution)/shard_map/ppermute | solution.py:356
  487.2 50.6 %collective-permute-start.50 = (bf16[2048,512]{1,0:T(8,128)(2,1)S(1)}, bf16[2048,512]{1,0:T(8,128)(2,1)S(1)}, u32[]{:S(2)}, u32[]{:S(2)}) collective-permute-start(bf16[2048,512]{1,0:T(8,128)(2,1)S(1)} %add_convert_fusion.2.left_ref), channel_id=1, source_target_pairs={{0,8},{4,12},{24,16},{28,20},{1,9},{5,13},{25,17},{29,21},{2,10},{... | collective-permute-start | bytes 6291464 | tf_op jit(solution)/shard_map/ppermute | solution.py:348
  492.5 54.1 %collective-permute-start.48 = (bf16[256,2048]{1,0:T(8,128)(2,1)S(1)}, bf16[256,2048]{1,0:T(8,128)(2,1)S(1)}, u32[]{:S(2)}, u32[]{:S(2)}) collective-permute-start(bf16[256,2048]{1,0:T(8,128)(2,1)S(1)} %shard_map.258), channel_id=1, source_target_pairs={{8,0},{12,4},{16,24},{20,28},{9,1},{13,5},{17,25},{21,29},{10,2},{... | collective-permute-start | bytes 3145736 | tf_op jit(solution)/shard_map/ppermute | solution.py:348
  494.2 61.2 %collective-permute-start.42 = (bf16[2048,512]{1,0:T(8,128)(2,1)S(1)}, bf16[2048,512]{1,0:T(8,128)(2,1)S(1)}, u32[]{:S(2)}, u32[]{:S(2)}) collective-permute-start(bf16[2048,512]{1,0:T(8,128)(2,1)S(1)} %shard_map.259.left_ref), channel_id=1, source_target_pairs={{8,16},{12,20},{16,8},{20,12},{9,17},{13,21},{17,9},{21,13},{10,18... | collective-permute-start | bytes 6291464 | tf_op jit(solution)/shard_map/ppermute | solution.py:348
  507.6 71.0 %collective-permute-start.52 = (bf16[2048,512]{1,0:T(8,128)(2,1)S(1)}, bf16[2048,512]{1,0:T(8,128)(2,1)S(1)}, u32[]{:S(2)}, u32[]{:S(2)}) collective-permute-start(bf16[2048,512]{1,0:T(8,128)(2,1)S(1)} %add_convert_fusion.1.left_ref), channel_id=1, source_target_pairs={{0,8},{4,12},{24,16},{28,20},{1,9},{5,13},{25,17},{29,21},{2,10},{... | collective-permute-start | bytes 6291464 | tf_op jit(solution)/shard_map/ppermute | solution.py:348
  546.7 68.6 %collective-permute-start.55 = (bf16[2048,512]{1,0:T(8,128)(2,1)S(1)}, bf16[2048,512]{1,0:T(8,128)(2,1)}, u32[]{:S(2)}, u32[]{:S(2)}) collective-permute-start(bf16[2048,512]{1,0:T(8,128)(2,1)S(1)} %shard_map.261.left_ref), channel_id=1, source_target_pairs={{8,16},{12,20},{16,8},{20,12},{9,17},{13,21},{17,9},{21,13},{10,18... | collective-permute-start | bytes 6291464 | tf_op jit(solution)/shard_map/ppermute | solution.py:348
  555.9 70.5 %collective-permute-start.54 = (bf16[2048,512]{1,0:T(8,128)(2,1)S(1)}, bf16[2048,512]{1,0:T(8,128)(2,1)}, u32[]{:S(2)}, u32[]{:S(2)}) collective-permute-start(bf16[2048,512]{1,0:T(8,128)(2,1)S(1)} %shard_map.263.second_ref), channel_id=1, source_target_pairs={{8,0},{12,4},{16,24},{20,28},{9,1},{13,5},{17,25},{21,29},{10,2},{... | collective-permute-start | bytes 6291464 | tf_op jit(solution)/shard_map/ppermute | solution.py:348
  565.7 59.2 %collective-permute-start.57 = (bf16[256,2048]{1,0:T(8,128)(2,1)S(1)}, bf16[256,2048]{1,0:T(8,128)(2,1)}, u32[]{:S(2)}, u32[]{:S(2)}) collective-permute-start(bf16[256,2048]{1,0:T(8,128)(2,1)S(1)} %collective-permute-done.44.second_ref), channel_id=1, source_target_pairs={{8,0},{12,4},{16,24},{20,28},{9,1},{13,5},{17,25},{21,29},{10,2},{... | collective-permute-start | bytes 3145736 | tf_op jit(solution)/shard_map/ppermute | solution.py:348
  578.7 53.5 %collective-permute-start.58 = (bf16[256,2048]{1,0:T(8,128)(2,1)}, bf16[256,2048]{1,0:T(8,128)(2,1)}, u32[]{:S(2)}, u32[]{:S(2)}) collective-permute-start(bf16[256,2048]{1,0:T(8,128)(2,1)} %convolution_convert_fusion.8), channel_id=1, source_target_pairs={{0,4},{4,0},{8,12},{12,8},{16,20},{20,16},{24,28},{28,24},{1,5},{5... | collective-permute-start | bytes 3145736 | tf_op jit(solution)/shard_map/ppermute | solution.py:348
  589.2 56.2 %collective-permute-start.61 = (bf16[2048,512]{1,0:T(8,128)(2,1)}, bf16[2048,512]{1,0:T(8,128)(2,1)}, u32[]{:S(2)}, u32[]{:S(2)}) collective-permute-start(bf16[2048,512]{1,0:T(8,128)(2,1)} %add_convert_fusion.left_ref), channel_id=1, source_target_pairs={{0,8},{4,12},{24,16},{28,20},{1,9},{5,13},{25,17},{29,21},{2,10},{... | collective-permute-start | bytes 6291464 | tf_op jit(solution)/shard_map/ppermute | solution.py:348
  615.2 72.5 %collective-permute-start.53 = (bf16[2048,512]{1,0:T(8,128)(2,1)}, bf16[2048,512]{1,0:T(8,128)(2,1)}, u32[]{:S(2)}, u32[]{:S(2)}) collective-permute-start(bf16[2048,512]{1,0:T(8,128)(2,1)} %shard_map.265.left_ref), channel_id=1, source_target_pairs={{8,16},{12,20},{16,8},{20,12},{9,17},{13,21},{17,9},{21,13},{10,18... | collective-permute-start | bytes 6291464 | tf_op jit(solution)/shard_map/ppermute | solution.py:348
  624.9 77.3 %collective-permute-start.65 = (bf16[2048,512]{1,0:T(8,128)(2,1)}, bf16[2048,512]{1,0:T(8,128)(2,1)}, u32[]{:S(2)}, u32[]{:S(2)}) collective-permute-start(bf16[2048,512]{1,0:T(8,128)(2,1)} %shard_map.266.second_ref), channel_id=1, source_target_pairs={{8,0},{12,4},{16,24},{20,28},{9,1},{13,5},{17,25},{21,29},{10,2},{... | collective-permute-start | bytes 6291464 | tf_op jit(solution)/shard_map/ppermute | solution.py:348
  632.1 76.9 %collective-permute-start.66 = (bf16[2048,512]{1,0:T(8,128)(2,1)}, bf16[2048,512]{1,0:T(8,128)(2,1)}, u32[]{:S(2)}, u32[]{:S(2)}) collective-permute-start(bf16[2048,512]{1,0:T(8,128)(2,1)} %get-tuple-element.1031), channel_id=1, source_target_pairs={{0,4},{4,0},{8,12},{12,8},{16,20},{20,16},{24,28},{28,24},{1,5},{5... | collective-permute-start | bytes 6291464 | tf_op jit(solution)/shard_map/ppermute | solution.py:348
  638.6 59.1 %collective-permute-start.64 = (bf16[256,2048]{1,0:T(8,128)(2,1)}, bf16[256,2048]{1,0:T(8,128)(2,1)}, u32[]{:S(2)}, u32[]{:S(2)}) collective-permute-start(bf16[256,2048]{1,0:T(8,128)(2,1)} %fusion.left_ref), channel_id=1, source_target_pairs={{0,8},{4,12},{24,16},{28,20},{1,9},{5,13},{25,17},{29,21},{2,10},{... | collective-permute-start | bytes 3145736 | tf_op jit(solution)/shard_map/ppermute | solution.py:348
  687.1 77.2 %collective-permute-start.71 = (f32[256,512]{1,0:T(8,128)}, f32[256,512]{1,0:T(8,128)}, u32[]{:S(2)}, u32[]{:S(2)}) collective-permute-start(f32[256,512]{1,0:T(8,128)} %get-tuple-element.1113), channel_id=1, source_target_pairs={{0,1},{1,0},{2,3},{3,2},{4,5},{5,4},{6,7},{7,6},{8,9},{9,8},{10,11... | collective-permute-start | bytes 1572872 | tf_op jit(solution)/shard_map/ppermute | solution.py:352
  702.2 63.4 %collective-permute-start.63 = (bf16[2048,512]{1,0:T(8,128)(2,1)}, bf16[2048,512]{1,0:T(8,128)(2,1)}, u32[]{:S(2)}, u32[]{:S(2)}) collective-permute-start(bf16[2048,512]{1,0:T(8,128)(2,1)} %shard_map.271.second_ref), channel_id=1, source_target_pairs={{8,0},{12,4},{16,24},{20,28},{9,1},{13,5},{17,25},{21,29},{10,2},{... | collective-permute-start | bytes 6291464 | tf_op jit(solution)/shard_map/ppermute | solution.py:348
  721.7 55.7 %collective-permute-start.72 = (bf16[256,2048]{1,0:T(8,128)(2,1)}, bf16[256,2048]{1,0:T(8,128)(2,1)}, u32[]{:S(2)}, u32[]{:S(2)}) collective-permute-start(bf16[256,2048]{1,0:T(8,128)(2,1)} %shard_map.272.left_ref), channel_id=1, source_target_pairs={{8,16},{12,20},{16,8},{20,12},{9,17},{13,21},{17,9},{21,13},{10,18... | collective-permute-start | bytes 3145736 | tf_op jit(solution)/shard_map/ppermute | solution.py:348
  741.3 55.3 %collective-permute-start.75 = (bf16[2048,512]{1,0:T(8,128)(2,1)}, bf16[2048,512]{1,0:T(8,128)(2,1)}, u32[]{:S(2)}, u32[]{:S(2)}) collective-permute-start(bf16[2048,512]{1,0:T(8,128)(2,1)} %get-tuple-element.1079), channel_id=1, source_target_pairs={{0,4},{4,0},{8,12},{12,8},{16,20},{20,16},{24,28},{28,24},{1,5},{5... | collective-permute-start | bytes 6291464 | tf_op jit(solution)/shard_map/ppermute | solution.py:348
  764.3 48.0 %collective-permute-start.78 = (bf16[2048,512]{1,0:T(8,128)(2,1)}, bf16[2048,512]{1,0:T(8,128)(2,1)}, u32[]{:S(2)}, u32[]{:S(2)}) collective-permute-start(bf16[2048,512]{1,0:T(8,128)(2,1)} %shard_map.274.second_ref), channel_id=1, source_target_pairs={{8,0},{12,4},{16,24},{20,28},{9,1},{13,5},{17,25},{21,29},{10,2},{... | collective-permute-start | bytes 6291464 | tf_op jit(solution)/shard_map/ppermute | solution.py:348
  816.0 48.9 %collective-permute-start.83 = (bf16[2048,512]{1,0:T(8,128)(2,1)}, bf16[2048,512]{1,0:T(8,128)(2,1)}, u32[]{:S(2)}, u32[]{:S(2)}) collective-permute-start(bf16[2048,512]{1,0:T(8,128)(2,1)} %get-tuple-element.1119), channel_id=1, source_target_pairs={{0,4},{4,0},{8,12},{12,8},{16,20},{20,16},{24,28},{28,24},{1,5},{5... | collective-permute-start | bytes 6291464 | tf_op jit(solution)/shard_map/ppermute | solution.py:348
  818.6 75.1 %collective-permute-start.85 = (bf16[512,2048]{1,0:T(8,128)(2,1)}, bf16[512,2048]{1,0:T(8,128)(2,1)}, u32[]{:S(2)}, u32[]{:S(2)}) collective-permute-start(bf16[512,2048]{1,0:T(8,128)(2,1)} %convolution_convert_fusion), channel_id=1, source_target_pairs={{0,8},{4,12},{24,16},{28,20},{1,9},{5,13},{25,17},{29,21},{2,10},{... | collective-permute-start | bytes 6291464 | tf_op jit(solution)/shard_map/ppermute | solution.py:348
  832.6 66.8 %collective-permute-start.84 = (bf16[1024,512]{1,0:T(8,128)(2,1)}, bf16[1024,512]{1,0:T(8,128)(2,1)}, u32[]{:S(2)}, u32[]{:S(2)}) collective-permute-start(bf16[1024,512]{1,0:T(8,128)(2,1)} %add_convert_fusion.12), channel_id=1, source_target_pairs={{0,1},{1,0},{2,3},{3,2},{4,5},{5,4},{6,7},{7,6},{8,9},{9,8},{10,11... | collective-permute-start | bytes 3145736 | tf_op jit(solution)/shard_map/ppermute | solution.py:352
  899.4 53.8 %collective-permute-start.99 = (bf16[2048,512]{1,0:T(8,128)(2,1)}, bf16[2048,512]{1,0:T(8,128)(2,1)}, u32[]{:S(2)}, u32[]{:S(2)}) collective-permute-start(bf16[2048,512]{1,0:T(8,128)(2,1)} %get-tuple-element.1279), channel_id=1, source_target_pairs={{0,4},{4,0},{8,12},{12,8},{16,20},{20,16},{24,28},{28,24},{1,5},{5... | collective-permute-start | bytes 6291464 | tf_op jit(solution)/shard_map/ppermute | solution.py:348
  1015.1 49.6 %collective-permute-start.112 = (bf16[256,2048]{1,0:T(8,128)(2,1)S(1)}, bf16[256,2048]{1,0:T(8,128)(2,1)}, u32[]{:S(2)}, u32[]{:S(2)}) collective-permute-start(bf16[256,2048]{1,0:T(8,128)(2,1)S(1)} %collective-permute-done.105.second_ref), channel_id=1, source_target_pairs={{8,0},{12,4},{16,24},{20,28},{9,1},{13,5},{17,25},{21,29},{10,2},{... | collective-permute-start | bytes 3145736 | tf_op jit(solution)/shard_map/ppermute | solution.py:348
  (219 other events, 2962.4 us)

commit v2 on v1

--- a/solution.py
+++ b/solution.py
@@ -372,7 +372,7 @@
 
 def place_one(target, shape, use_first, first, second, row_block, col_block):
     rows, cols = second.shape
-    steps = 4
+    steps = 2
     tile = rows // steps
 
     def kernel(spot_ref, first_ref, second_ref, *refs):
@@ -417,7 +417,7 @@
 
 def place(target, shape, block, row_block, col_block):
     rows, cols = block.shape
-    steps = 4
+    steps = 2
     tile = rows // steps
 
     def kernel(spot_ref, block_ref, target_ref, out_ref):
@@ -445,19 +445,23 @@
     )(spots, block, target)
 
 
-def matmul_call(kernel, steps, ins, outs, scratch=(), flops=0, mib=24):
+def matmul_call(kernel, steps, ins, outs, scratch=(), flops=0, mib=24, scalars=None):
     moved = sum(a.size * a.dtype.itemsize for a, _, _ in ins)
     moved += sum(math.prod(s) * jnp.dtype(d).itemsize for s, d, _, _ in outs)
+    ahead = () if scalars is None else (scalars,)
     return pl.pallas_call(
         kernel,
         out_shape=[jax.ShapeDtypeStruct(s, d) for s, d, _, _ in outs],
-        grid=(steps,),
-        in_specs=[pl.BlockSpec(b, m) for _, b, m in ins],
-        out_specs=[pl.BlockSpec(b, m) for _, _, b, m in outs],
-        scratch_shapes=list(scratch),
+        grid_spec=pltpu.PrefetchScalarGridSpec(
+            num_scalar_prefetch=len(ahead),
+            grid=(steps,),
+            in_specs=[pl.BlockSpec(b, m) for _, b, m in ins],
+            out_specs=[pl.BlockSpec(b, m) for _, _, b, m in outs],
+            scratch_shapes=list(scratch),
+        ),
         compiler_params=pltpu.CompilerParams(vmem_limit_bytes=mib << 20),
         cost_estimate=pl.CostEstimate(flops=flops, bytes_accessed=moved, transcendentals=0),
-    )(*[a for a, _, _ in ins])
+    )(*ahead, *[a for a, _, _ in ins])
 
 
 def feed(low, w_gate, w_up):
@@ -487,61 +491,273 @@
     )
 
 
-def unfeed(low, w_down, gate, up):
+def unfeed(low, w_down, gate, up, y):
     rows, width = low.shape
     units = w_down.shape[0]
-    tile = min(512, units)
-
-    def kernel(low_ref, down_w, gate_ref, up_ref, dgate_ref, dup_ref):
+    tile = units // 4
+
+    def kernel(_, low_ref, down_w, gate_ref, up_ref, *outs):
         grad = dot(low_ref[...], down_w[...], 1, 1)
         gate = gate_ref[...].astype(f32)
         sigma = jax.nn.sigmoid(gate)
-        dup_ref[...] = (grad * (gate * sigma)).astype(bf16)
-        dgate_ref[...] = (
-            grad * up_ref[...].astype(f32) * sigma * (1.0 + gate * (1.0 - sigma))
-        ).astype(bf16)
-
-    column = lambda n: (0, n)
+        dup = (grad * (gate * sigma)).astype(bf16)
+        dgate = (grad * up_ref[...].astype(f32) * sigma * (1.0 + gate * (1.0 - sigma))).astype(bf16)
+
+        @pl.when(pl.program_id(0) < 2)
+        def _():
+            outs[0][...], outs[1][...] = dgate, dup
+
+        @pl.when(pl.program_id(0) >= 2)
+        def _():
+            outs[2][...], outs[3][...] = dgate, dup
+
+    def unit(n, y):
+        return jnp.where(n < 2, 2 * (1 - y[0]) + n, 2 * y[0] + n - 2)
+
+    column = lambda n, y: (0, unit(n, y))
+    give = ((rows, units // 2), bf16, (rows, tile), lambda n, y: (0, jnp.minimum(n, 1)))
+    keep = ((rows, units // 2), bf16, (rows, tile), lambda n, y: (0, jnp.maximum(n - 2, 0)))
     return matmul_call(
         kernel,
-        units // tile,
+        4,
         [
-            (low, (rows, width), lambda n: (0, 0)),
-            (w_down, (tile, width), lambda n: (n, 0)),
+            (low, (rows, width), lambda n, y: (0, 0)),
+            (w_down, (tile, width), lambda n, y: (unit(n, y), 0)),
             (gate, (rows, tile), column),
             (up, (rows, tile), column),
         ],
-        [((rows, units), bf16, (rows, tile), column)] * 2,
+        [give, give, keep, keep],
         flops=2 * rows * width * units,
         mib=56,
-    )
-
-
-def unwide(dgate, dup, w_gate, w_up):
-    rows, units = dgate.shape
-    width = w_gate.shape[0]
+        scalars=y[None],
+    )
+
+
+def unwide(give_gate, give_up, keep_gate, keep_up, w_gate, w_up, y):
+    rows, part_units = keep_gate.shape
+    width, units = w_gate.shape
     tile = min(512, width)
 
-    def kernel(dgate_ref, dup_ref, gate_w, up_w, upper_ref, lower_ref):
-        total = dot(dgate_ref[...], gate_w[...], 1, 1) + dot(dup_ref[...], up_w[...], 1, 1)
+    def kernel(_, give_g, give_u, keep_g, keep_u, give_gw, give_uw, keep_gw, keep_uw, upper_ref, lower_ref):
+        total = dot(give_g[...], give_gw[...], 1, 1) + dot(give_u[...], give_uw[...], 1, 1)
+        total += dot(keep_g[...], keep_gw[...], 1, 1) + dot(keep_u[...], keep_uw[...], 1, 1)
         upper_ref[...] = total[: rows // 2].astype(bf16)
         lower_ref[...] = total[rows // 2 :].astype(bf16)
 
-    whole = lambda n: (0, 0)
-    row = lambda n: (n, 0)
-    column = lambda n: (0, n)
+    whole = lambda n, y: (0, 0)
+    column = lambda n, y: (0, n)
+    other = lambda n, y: (n, 1 - y[0])
+    mine = lambda n, y: (n, y[0])
+    lows = [(v, (rows, part_units), whole) for v in (give_gate, give_up, keep_gate, keep_up)]
+    weights = [(w, (tile, part_units), m) for m in (other, mine) for w in (w_gate, w_up)]
     return matmul_call(
         kernel,
         width // tile,
-        [
-            (dgate, (rows, units), whole),
-            (dup, (rows, units), whole),
-            (w_gate, (tile, units), row),
-            (w_up, (tile, units), row),
-        ],
+        lows + weights,
         [((rows // 2, width), bf16, (rows // 2, tile), column)] * 2,
         flops=4 * rows * width * units,
         mib=56,
+        scalars=y[None],
+    )
+
+
+def wide_grad(hid0, hid1, near0, next0, near1, next1, own0, own1, came0, came1):
+    rows, cols = own0.shape
+    width = hid0.shape[1]
+    tile = min(512, width)
+    half = rows // 2
+
+    def kernel(h0, h1, n0, x0, n1, x1, o0, o1, c0, c1, left_ref, right_ref):
+        total = dot(h0[...], o0[...], 0, 0) + dot(h1[...], o1[...], 0, 0)
+        total += dot(n0[...], c0[:half], 0, 0) + dot(x0[...], c0[half:], 0, 0)
+        total += dot(n1[...], c1[:half], 0, 0) + dot(x1[...], c1[half:], 0, 0)
+        left_ref[...] = total[:, : cols // 2].astype(bf16)
+        right_ref[...] = total[:, cols // 2 :].astype(bf16)
+
+    lefts = (hid0, hid1, near0, next0, near1, next1)
+    return matmul_call(
+        kernel,
+        width // tile,
+        [(v, (v.shape[0], tile), lambda n: (0, n)) for v in lefts]
+        + [(v, v.shape, lambda n: (0, 0)) for v in (own0, own1, came0, came1)],
+        [((width, cols // 2), bf16, (tile, cols // 2), lambda n: (n, 0))] * 2,
+        flops=8 * rows * width * cols,
+        mib=56,
+    )
+
+
+def down_grad_rows(act0, act1, low0, low1, which):
+    rows, units = act0.shape
+    width = low0.shape[1]
+    tile = units // 8
+
+    def kernel(_, a0, a1, b0, b1, *outs):
+        total = (dot(a0[...], b0[...], 0, 0) + dot(a1[...], b1[...], 0, 0)).astype(bf16)
+        for n, out in enumerate(outs):
+            @pl.when(pl.program_id(0) == n)
+            def _(out=out):
+                out[...] = total
+
+    whole = lambda n, which: (0, 0)
+    return matmul_call(
+        kernel,
+        4,
+        [(a, (rows, tile), lambda n, which: (0, which[n])) for a in (act0, act1)]
+        + [(b, (rows, width), whole) for b in (low0, low1)],
+        [((tile, width), bf16, (tile, width), whole)] * 4,
+        flops=4 * rows * width * units,
+        mib=56,
+        scalars=which,
+    )
+
+
+def input_columns(lows, weights, core):
+    rows, cols = lows[0].shape
+    narrow = weights[0].shape[0] // 4
+
+    def kernel(_, a0, a1, a2, w0, w1, w2, give_ref, keep_ref):
+        total = dot(a0[...], w0[...], 1, 1) + dot(a1[...], w1[...], 1, 1) + dot(a2[...], w2[...], 1, 1)
+        total = total.astype(bf16)
+
+        @pl.when(pl.program_id(0) < 2)
+        def _():
+            give_ref[0] = total
+
+        @pl.when(pl.program_id(0) >= 2)
+        def _():
+            keep_ref[0] = total
+
+    def block(n, core):
+        return (jnp.where(n < 2, 2 * n + 1 - core[0], 2 * (n - 2) + core[0]), 0)
+
+    return matmul_call(
+        kernel,
+        4,
+        [(a, (rows, cols), lambda n, core: (0, 0)) for a in lows]
+        + [(w, (narrow, cols), block) for w in weights],
+        [
+            ((2, rows, narrow), bf16, (1, rows, narrow), lambda n, core: (jnp.minimum(n, 1), 0, 0)),
+            ((2, rows, narrow), bf16, (1, rows, narrow), lambda n, core: (jnp.maximum(n - 2, 0), 0, 0)),
+        ],
+        flops=24 * rows * cols * narrow,
+        mib=56,
+        scalars=core[None],
+    )
+
+
+def join_rows(chip, away, x, block, gain):
+    rows, width = chip.shape
+    tile = rows // 2
+
+    def kernel(_, chip_ref, away_ref, x_ref, gain_ref, low_ref):
+        total = chip_ref[...].astype(f32) + away_ref[...].astype(f32)
+        scale = lax.rsqrt(jnp.sum(total * total, 1, keepdims=True) / width + epsilon)
+        low_ref[...] = (x_ref[...].astype(f32) + total * scale * gain_ref[...]).astype(bf16)
+
+    row = lambda i, b: (i, 0)
+    return matmul_call(
+        kernel,
+        2,
+        [
+            (chip, (tile, width), row),
+            (away, (tile, width), row),
+            (x, (tile, width), lambda i, b: (2 * b[0] + i, 0)),
+            (gain[None], (1, width), lambda i, b: (0, 0)),
+        ],
+        [((rows, width), bf16, (tile, width), row)],
+        scalars=block[None],
+    )[0]
+
+
+def norm_back_rows(sums, grads, columns, base, block, rank, gain):
+    rows, width = sums[0].shape
+    narrow = columns[0].shape[1]
+    tile = rows // 2
+    kind = f32 if base is None else bf16
+    extra = grads if base is None else (base,)
+
+    def kernel(spot, *refs):
+        first, second = refs[:2]
+        more = refs[2 : 2 + len(extra)]
+        pieces = refs[2 + len(extra) : 6 + len(extra)]
+        gain_ref, low_ref, own_ref, give_ref, grad_ref = refs[6 + len(extra) :]
+        lanes = [pl.ds(pl.multiple_of((spot[1] ^ k) * narrow, narrow), narrow) for k in range(4)]
+        square = jnp.zeros((tile, 1), f32)
+        inner = jnp.zeros((tile, 1), f32)
+
+        def terms(k):
+            total = first[:, lanes[k]].astype(f32) + second[:, lanes[k]].astype(f32)
+            grad = pieces[k][...].astype(f32)
+            if base is None:
+                grad += more[0][:, lanes[k]].astype(f32) + more[1][:, lanes[k]].astype(f32)
+            return total, grad
+
+        for k in range(4):
+            total, grad = terms(k)
+            square += jnp.sum(total * total, 1, keepdims=True)
+            inner += jnp.sum(grad * gain_ref[:, lanes[k]] * total, 1, keepdims=True)
+        scale = lax.rsqrt(square / width + epsilon)
+        back = scale * scale * scale / width * inner
+        for k in range(4):
+            total, grad = terms(k)
+            gained = grad * gain_ref[:, lanes[k]]
+            low_ref[:, lanes[k]] = (scale * gained - total * back).astype(bf16)
+            normed = total * scale
+            if k < 2:
+                if base is None:
+                    value = grad
+                else:
+                    value = more[0][:, lanes[k]].astype(f32) + normed * gain_ref[:, lanes[k]]
+                (own_ref, give_ref)[k][...] = value.astype(kind)
+            part_sum = jnp.sum(grad * normed, 0, keepdims=True)
+
+            @pl.when(pl.program_id(0) == 0)
+            def _():
+                grad_ref[:, lanes[k]] = part_sum
+
+            @pl.when(pl.program_id(0) > 0)
+            def _():
+                grad_ref[:, lanes[k]] += part_sum
+
+    row = lambda i, s: (i, 0)
+    whole = lambda i, s: (0, 0)
+    return matmul_call(
+        kernel,
+        2,
+        [(v, (tile, width), row) for v in (*sums, *extra)]
+        + [(v, (tile, narrow), lambda i, s: (2 * s[0] + i, 0)) for v in columns]
+        + [(gain[None], (1, width), whole)],
+        [
+            ((rows, width), bf16, (tile, width), row),
+            ((rows, narrow), kind, (tile, narrow), row),
+            ((rows, narrow), kind, (tile, narrow), row),
+            ((1, width), f32, (1, width), whole),
+        ],
+        scalars=jnp.stack([block, rank]),
+    )
+
+
+def narrow_grads(x, beside, lows, came, y):
+    rows, width = x.shape
+    cols = came[0].shape[1]
+    tile = min(512, width)
+
+    def kernel(_, x_ref, beside_ref, *refs):
+        for low, other, out in zip(refs[:3], refs[3:6], refs[6:]):
+            total = dot(x_ref[...], low[...], 0, 0) + dot(beside_ref[...], other[...], 0, 0)
+            out[...] = total.astype(bf16)
+
+    column = lambda n, y: (0, n)
+    return matmul_call(
+        kernel,
+        width // tile,
+        [(v, (rows, tile), column) for v in (x, beside)]
+        + [(v, (rows, cols), lambda n, y: (0, y[0])) for v in lows]
+        + [(v, (rows, cols), lambda n, y: (0, 0)) for v in came],
+        [((width, cols), bf16, (tile, cols), lambda n, y: (n, 0))] * 3,
+        flops=12 * rows * width * cols,
+        mib=56,
+        scalars=y[None],
     )
 
 
@@ -593,6 +809,7 @@
             ((2, rows), f32, (2, tile), lambda i: (0, i)),
         ],
         flops=6 * rows * width * cols,
+        mib=56,
     )
 
 
@@ -754,11 +971,11 @@
     )
 
 
-def unscale(gained, projected, squares, dots, which, full_width):
+def unscale(gained, projected, squares, dots, which, full_width, y):
     rows, cols = gained.shape
     tile = rows // 2
 
-    def kernel(gained_ref, proj_ref, sum_ref, dot_ref, out_ref):
+    def kernel(y_ref, gained_ref, proj_ref, sum_ref, dot_ref, out_ref, give_ref):
         scale = lax.rsqrt(sum_ref[which : which + 1] / full_width + epsilon)
         inner = scale**3 / full_width * dot_ref[which : which + 1]
         scale, inner = as_column(scale), as_column(inner)
@@ -767,9 +984,11 @@
             out_ref[:, lanes] = (
                 scale * gained_ref[:, lanes] - proj_ref[:, lanes] * inner
             ).astype(bf16)
-
-    row = lambda i: (i, 0)
-    column = lambda i: (0, i)
+        other = pl.multiple_of((1 - y_ref[0]) * (cols // 2), cols // 2)
+        give_ref[...] = out_ref[:, pl.ds(other, cols // 2)]
+
+    row = lambda i, y: (i, 0)
+    column = lambda i, y: (0, i)
     return matmul_call(
         kernel,
         rows // tile,
@@ -779,8 +998,12 @@
             (squares, (2, tile), column),
             (dots, (2, tile), column),
         ],
-        [((rows, cols), bf16, (tile, cols), row)],
-    )[0]
+        [
+            ((rows, cols), bf16, (tile, cols), row),
+            ((rows, cols // 2), bf16, (tile, cols // 2), row),
+        ],
+        scalars=y[None],
+    )
 
 
 def fast_add(left, right):
@@ -802,8 +1025,8 @@
 
 def pick_and_place(target, shape, use_first, first, second, row_block, col_block):
     rows, cols = first.shape
-    tile = rows // 4
-    steps = 4
+    tile = rows // 2
+    steps = 2
 
     def kernel(spot_ref, first_ref, second_ref, *refs):
         low_ref, wide_ref = refs[-2:]
@@ -852,20 +1075,18 @@
 
 
 ORDER = [
-    -3, -2, 1, -4, 6, -8, -7, 5, 11, -12, 206, -207, 13, -14, -9, 15, 16, 17, 18, -19,
-    10, 20, -21, 25, 26, -27, 194, -208, 28, -29, 209, 22, -23, -117, 24, 33, 34, -35, -119, 30,
-    -31, -118, 36, -37, 32, 41, 42, -43, -120, 54, 38, -39, 44, -45, 121, 40, 114, 166, -167, 46,
-    -47, 116, 48, 55, 72, -73, 115, 144, -145, 56, 57, -58, 85, 86, 122, -123, 173, -87, -174, 74,
-    -76, 75, 146, -147, 59, -60, 124, 77, -78, 155, -125, -156, 175, -176, 88, -89, 90, 133, 61, 62,
-    -63, -134, 168, -169, 79, -80, -81, 51, -52, 177, -178, 91, -92, 157, -158, 148, -149, 179, -82, 170,
-    -171, 180, -181, 64, -65, 135, -136, 126, -127, 93, -94, 172, 185, 150, -151, 195, -196, 186, 187, -188,
-    159, -160, 210, -211, 128, -129, 152, -153, 189, -190, 197, -198, 95, -96, 137, -138, 191, 193, 232, -233,
-    192, 161, -162, 199, -200, 130, -131, 154, 66, -67, 212, -213, 101, 234, -97, 139, -140, -235, 49, -50,
-    163, -164, 243, -68, -102, -245, -246, 201, -202, 132, 214, -215, 53, 221, -222, 182, -98, -183, 236, 141,
-    184, -237, 244, -69, -142, 165, 203, -204, 223, -224, 216, -217, 103, -105, 104, 247, -248, 250, -251, 70,
-    238, 252, -253, -239, 225, -226, 71, 83, 84, 99, 100, 106, -107, 254, 218, -219, 143, 205, 227, -228,
-    249, 240, -241, 108, -109, -110, 229, -255, 220, -111, 112, -230, 242, 256, -257, 258, -259, 260, -261, 113,
-    262, 231,
+    -2, -3, -6, 1, -4, -12, -11, 7, -9, 5, 15, -16, 17, -18, -8, 19, 20, 21, 22, -23,
+    -13, 24, -25, 29, -10, 30, 14, -31, 175, 32, -33, 26, -27, -106, 28, 37, 38, -39, -108, 34,
+    -35, -107, 40, -41, 36, 46, 47, -48, -109, 42, -43, -45, 49, -50, 44, 104, -129, 148, -110, -149,
+    51, -52, -54, 150, -151, 53, 105, -130, 56, -57, 156, -157, -111, 80, -81, 58, -59, 131, -132, -94,
+    158, -159, -70, 82, 60, -61, 152, -154, -153, -83, 155, 112, -113, 62, 160, -162, -161, 84, 133, -134,
+    163, 165, 166, -63, -85, -140, 167, 114, -115, 174, -187, 135, -168, -136, 86, -87, 169, -170, 71, 220,
+    -221, 171, 176, -121, 222, -223, 164, -177, 224, 141, -142, 172, -188, 116, -117, 88, 137, -138, 178, -179,
+    173, 215, 122, -123, -216, 143, -72, -144, 118, -225, 64, 180, -181, -119, 95, -96, -189, 139, 73, 217,
+    -218, 226, -227, 124, -125, -65, 145, 97, 228, -229, -74, 230, 182, -183, 219, -89, -146, 120, -66, 68,
+    190, -207, -98, 75, 126, -67, -191, -127, -76, 55, -199, 208, -209, 184, -185, -90, 99, 69, 147, 192,
+    210, -211, 77, -78, 200, 128, -193, -201, -91, 212, -213, 186, 194, -195, 79, 92, 202, -203, 196, -197,
+    93, -100, 214, 204, -205, -231, 198, 101, -102, 206, 232, 103,
 ]
 
 
@@ -931,7 +1152,7 @@
 
 def in_order(rank, *pieces):
     rows, cols = pieces[0].shape
-    tile = rows // 4
+    tile = rows // 2
 
     def kernel(rank_ref, *refs):
         for k in range(4):
@@ -947,6 +1168,7 @@
             in_specs=[pl.BlockSpec((tile, cols), lambda i, rank: (i, 0))] * 4,
             out_specs=pl.BlockSpec((tile, 4 * cols), lambda i, rank: (i, 0)),
         ),
+        compiler_params=pltpu.CompilerParams(vmem_limit_bytes=24 << 20),
         cost_estimate=pl.CostEstimate(
             flops=rows * cols, bytes_accessed=16 * rows * cols, transcendentals=0
         ),
@@ -971,7 +1193,7 @@
     gain_mlp,
 ):
     full_width = w_query.shape[0]
-    row_count, narrow = tokens.shape
+    row_count, _ = tokens.shape
     local_width = w_query.shape[1]
     units = w_gate.shape[1]
     rank = lax.axis_index("tensor")
@@ -1007,21 +1229,25 @@
 
     def gathered(value):
         across = x_move(value)
-        pieces = (value, core_move(value), across, core_move(across))
-        return across, step(5.0, lambda *p: in_order(rank, *p), *pieces)
+        return value, core_move(value), across, core_move(across)
+
+    def ordered(pieces):
+        return step(4.9, lambda *p: in_order(rank, *p), *pieces)
 
     def prepare(value):
         cosine, sine = tables(segments)
         return value, cosine[0], sine[0]
 
     _, cosine, sine = step(6.0, prepare, tokens, outs=3)
-    across, whole_x = gathered(tokens)
-    held_dy = step(0.0, lambda v, _: v, cotangent, across)
-    _, whole_dy = gathered(held_dy)
+    x_pieces = gathered(tokens)
+    whole_x = ordered(x_pieces)
+    near_tokens = y_move(tokens)
+    dy_pieces = gathered(step(0.0, lambda v, _: v, cotangent, x_pieces[2]))
+    neighbour_x = ordered(gathered(near_tokens))
 
     def small_sum(value):
-        value = step(0.6, lambda a, b: a + b, value, core_move(value))
-        return step(0.6, lambda a, b: a + b, value, x_move(value))
+        value = step(0.2, lambda a, b: a + b, value, core_move(value))
+        return step(0.2, lambda a, b: a + b, value, x_move(value))
 
     query_proj, key_proj, value_low, squares = step(
         11.0, lambda x: project(x, w_query, w_key, w_value), whole_x, outs=4
@@ -1029,7 +1255,7 @@
     squares = small_sum(squares)
 
     query_rot, key_rot = step(
-        6.0,
+        5.5,
         lambda q, k, s, cos, sin: turn_heads(q, k, s, full_width, gain_query, gain_key, cos, sin),
         query_proj,
         key_proj,
@@ -1045,9 +1271,6 @@
         block = attend_heads(query, key, value, segments, blocks)
         return jnp.concatenate([part(block, core, half, 0), part(block, 1 - core, half, 0)], 0)
 
-    def own_rows(value, j):
-        return lax.dynamic_slice_in_dim(value, j * chunk + core * half, half, 0)
-
     def halves(value):
         value = value.astype(bf16)
         return value[:half], value[half:]
@@ -1057,93 +1280,67 @@
         return chip, x_move(chip)
 
     def both(value):
-        return step(2.0, lambda a, b: jnp.concatenate([a, b], 0), value, core_move(value))
-
-    mixed, attn_total, attn_scale, hid, own_low, hid_low = [], [], [], [], [], []
+        return step(1.7, lambda a, b: jnp.concatenate([a, b], 0), value, core_move(value))
+
+    mixed, attn_sums, own_low, hid_low = [], [], [], []
     for j in range(chunks):
         block = step(
-            8.0 + j,
+            5.5 + j,
             lambda q, k, v, j=j: attend(q, k, v, j),
             query_rot,
             key_rot,
             value_low,
         )
         mixed.append(block)
-        keep, give = step(3.0, lambda m: halves(dot(m, w_out)), block, outs=2)
+        keep, give = step(2.6, lambda m: halves(dot(m, w_out)), block, outs=2)
         chip, away = chip_sum(keep, give)
 
-        def join(chip, away, x, j=j):
-            total = chip.astype(f32) + away.astype(f32)
-            scale = lax.rsqrt(jnp.sum(total * total, 1, keepdims=True) / full_width + epsilon)
-            hidden = own_rows(x, j).astype(f32) + total * scale * gain_attn
-            return total, scale, hidden, hidden.astype(bf16)
-
-        total, scale, hidden, low = step(5.0, join, chip, away, whole_x, outs=4)
-        attn_total.append(total)
-        attn_scale.append(scale)
-        hid.append(hidden)
+        low = step(
+            3.6,
+            lambda a, b, x, j=j: join_rows(a, b, x, 2 * j + core, gain_attn),
+            chip,
+            away,
+            whole_x,
+        )
+        attn_sums.append((chip, away))
         own_low.append(low)
         hid_low.append(both(low))
 
-    gate, up, act, out_rows, branch_low, mlp_gains = [], [], [], [], [], []
+    gate, up, act, outs, branch_low, mlp_gains = [], [], [], [], [], []
     for j in range(chunks):
         g, u, a = step(14.5, lambda low: feed(low, w_gate, w_up), hid_low[j], outs=3)
         gate.append(g)
         up.append(u)
         act.append(a)
-        keep, give = step(5.0, lambda a: halves(dot(a, w_down)), a, outs=2)
+        keep, give = step(9.3, lambda a: halves(dot(a, w_down)), a, outs=2)
         chip, away = chip_sum(keep, give)
 
-        def finish(chip, away, hidden, dy, j=j):
-            branch = chip.astype(f32) + away.astype(f32)
-            scale = lax.rsqrt(jnp.sum(branch * branch, 1, keepdims=True) / full_width + epsilon)
-            normed = branch * scale
-            dy_rows = own_rows(dy, j).astype(f32)
-            gained = gain_mlp * dy_rows
-            inner = jnp.sum(gained * branch, 1, keepdims=True)
-            low = (scale * gained - branch * scale**3 / full_width * inner).astype(bf16)
-            return low, (hidden + normed * gain_mlp).astype(bf16), jnp.sum(dy_rows * normed, 0)
-
-        low, rows, gains = step(8.0, finish, chip, away, hid[j], whole_dy, outs=3)
+        low, own, give, gains = step(
+            4.8,
+            lambda a, b, h, *dy, j=j: norm_back_rows((a, b), (), dy, h, 2 * j + core, rank, gain_mlp),
+            chip,
+            away,
+            own_low[j],
+            *dy_pieces,
+            outs=4,
+        )
         branch_low.append(both(low))
-        out_rows.append(rows)
+        outs.append((own, core_move(give)))
         mlp_gains.append(gains)
 
-    def own_columns(blocks):
-        keeps, comes = [], []
-        for block in blocks:
-            keep, give = step(
-                1.5,
-                lambda b: (
-                    lax.dynamic_slice_in_dim(b, rank * narrow, narrow, 1),
-                    lax.dynamic_slice_in_dim(b, (rank ^ 1) * narrow, narrow, 1),
-                ),
-                block,
-                outs=2,
-            )
-            keeps.append(keep)
-            comes.append(core_move(give))
-
+    def own_columns(pairs):
         def merge(*values):
             pieces = []
-            for keep, came in zip(values[:chunks], values[chunks:]):
+            for keep, came in zip(values[::2], values[1::2]):
                 pieces += [jnp.where(core == 0, keep, came), jnp.where(core == 0, came, keep)]
             return jnp.concatenate(pieces, 0)
 
-        return step(2.0, merge, *keeps, *comes)
-
-    output = own_columns(out_rows)
+        return step(3.5, merge, *[v for pair in pairs for v in pair])
+
+    output = own_columns(outs)
 
     def joined(*values):
         return jnp.concatenate(values, 0)
-
-    def chosen(which):
-        return lambda own, came: low_add(
-            part(own, which, own.shape[0] // 2, 0), part(came, which, came.shape[0] // 2, 0)
-        )
-
-    def half_of(which):
-        return lambda own: part(own, which, own.shape[0] // 2, 0)
 
     def line_sum(own, mib):
         near = step(0.6 + 1.6 * mib, fast_add, own, z_move("in", own))
@@ -1153,102 +1350,80 @@
     def put(target, shape, spots, first, second, mib):
         if target is None:
             run = lambda a, b: pick_and_place(None, shape, outer, a, b, *spots)
-            return step(1.0 + 2.2 * mib, run, first, second, outs=2)
+            return step(2.2 + 1.4 * mib, run, first, second, outs=2)
         run = lambda a, b, t: pick_and_place(t, shape, outer, a, b, *spots)
-        return step(1.0 + 2.2 * mib, run, first, second, target, outs=2)
+        return step(2.2 + 1.4 * mib, run, first, second, target, outs=2)
 
     def set_down(target, shape, spots, value, mib):
         run = lambda v, t: place(t, shape, v, *spots)
-        return step(0.8 + 1.7 * mib, run, value, target)
+        return step(2.3 + 0.9 * mib, run, value, target)
 
     def put_only(target, shape, spots, first, second, mib):
         run = lambda a, b, *t: place_one(*(t or (None,)), shape, outer, a, b, *spots)
         rest = () if target is None else (target,)
-        return step(0.8 + 1.7 * mib, run, first, second, *rest)
-
-    def sum_middle(own, mib):
-        came = z_move("in", own)
-        send = step(0.8 * mib, chosen(1 - z_side), own, came)
-        keep = step(0.8 * mib, chosen(z_side), own, came)
-        keep = step(0.8 * mib, fast_add, keep, z_move("mid", send))
-        keep = step(0.8 * mib, fast_add, keep, y_move_at("middle", keep))
-        other = z_move("mid", keep)
-        return (z_move("out", keep), keep), (z_move("out", other), other)
-
-    def sum_ends(own, mib):
-        far = step(0.5 * mib, half_of(1 - z_side), own)
+        return step(2.3 + 0.9 * mib, run, first, second, *rest)
+
+    def sum_ends(far, near, mib):
         came = z_move("in", far)
-        came = z_move("mid", step(0.8 * mib, fast_add, far, came))
-        near = step(0.5 * mib, half_of(z_side), own)
-        came = z_move("out", step(0.8 * mib, fast_add, near, came))
-        root = step(0.8 * mib, fast_add, near, came)
-        root = step(0.8 * mib, fast_add, root, y_move_at("end", root))
+        came = z_move("mid", step(2.3 * mib, fast_add, far, came))
+        came = z_move("out", step(2.3 * mib, fast_add, near, came))
+        root = step(2.3 * mib, fast_add, near, came)
+        root = step(2.3 * mib, fast_add, root, y_move_at("end", root))
         first = z_move("in", root)
         second = z_move("mid", first)
         third = z_move("out", second)
         return (root, first), (third, second)
 
-    quarter = units // 4
-    whole_act = step(3.0, joined, *act)
-    whole_branch_low = step(3.0, joined, *branch_low)
-    down_grad = None
-    for k in range(4):
-        block = step(
-            5.0,
-            lambda a, b, k=k: dot(a[:, k * quarter : (k + 1) * quarter], b, 0, 0).astype(bf16),
-            whole_act,
-            whole_branch_low,
-        )
-        summed = (sum_middle if k % 2 else sum_ends)(block, 2.0)
+    down_grad, shape = None, (units, full_width)
+    for k in (0, 2):
+        which = jnp.stack([2 * k + 1 - z_side, 2 * k + z_side, 2 * k + 3 - y, 2 * k + 2 + y])
+        far, near, give, keep = step(
+            8.5,
+            lambda *v, which=which: down_grad_rows(*v, which),
+            *act,
+            *branch_low,
+            outs=4,
+        )
+        summed = sum_ends(far, near, 1.0)
         for side, pair in ((z_side, summed[0]), (1 - z_side, summed[1])):
-            spot = (2 * k + side, 0)
-            down_grad = put_only(down_grad, (units, full_width), spot, *pair, 1.0)
-
-    gate_low, up_low = [], []
+            down_grad = put_only(down_grad, shape, (2 * k + side, 0), *pair, 1.0)
+        own = step(2.3, fast_add, keep, y_move(give))
+        piece, down_grad = put(down_grad, shape, (2 * k + 2 + y, 0), *line_sum(own, 1.0), 1.0)
+        spot = (2 * k + 3 - y, 0)
+        down_grad = set_down(down_grad, shape, spot, y_move(piece), 1.0)
+
+    lows = []
     for j in range(chunks):
-        g, u = step(
-            12.0,
-            lambda low, gate, up: unfeed(low, w_down, gate, up),
-            branch_low[j],
-            gate[j],
-            up[j],
+        lows.append(
+            step(
+                12.0,
+                lambda low, gate, up: unfeed(low, w_down, gate, up, y),
+                branch_low[j],
+                gate[j],
+                up[j],
+                outs=4,
+            )
+        )
+
+    near = [y_move(low) for low in own_low]
+    beside = [core_move(n) for n in near]
+    wide = []
+    for which in range(2):
+        came = [y_move(low[which]) for low in lows]
+        pieces = step(
+            14.5,
+            wide_grad,
+            *hid_low,
+            near[0],
+            beside[0],
+            near[1],
+            beside[1],
+            *[low[2 + which] for low in lows],
+            *came,
             outs=2,
         )
-        gate_low.append(g)
-        up_low.append(u)
-
-    whole_hid = step(3.0, joined, *hid_low)
-    came = [y_move(low) for low in own_low]
-    beside = [core_move(c) for c in came]
-    neighbour_hid = step(
-        3.0, lambda a0, a1, b0, b1: joined(a0, b0, a1, b1), *came, *beside
-    )
-    mid = units // 2
-    piece_cols = mid // 2
-
-    wide = []
-    for lows in (gate_low, up_low):
-        result = None
-        for q in range(2):
-            def cut(g0, g1, q=q):
-                def columns(which):
-                    start = which * mid + q * piece_cols
-                    return joined(
-                        *[lax.dynamic_slice_in_dim(g, start, piece_cols, 1) for g in (g0, g1)]
-                    )
-
-                return columns(y), columns(1 - y)
-
-            keep, give = step(2.5, cut, *lows, outs=2)
-            own = step(
-                10.0,
-                lambda h, k, n, c: (dot(h, k, 0, 0) + dot(n, c, 0, 0)).astype(bf16),
-                whole_hid,
-                keep,
-                neighbour_hid,
-                y_move(give),
-            )
-            shape = (full_width, units)
+        result, shape = None, (full_width, units)
+        for q, own in enumerate(pieces):
             piece, result = put(result, shape, (0, 2 * y + q), *line_sum(own, 2.0), 2.0)
             result = set_down(result, shape, (0, 2 * (1 - y) + q), y_move(piece), 2.0)
         wide.append(result)
@@ -1258,24 +1433,24 @@
     for j in range(chunks):
         keep, give = step(
             14.0,
-            lambda g, u: unwide(g, u, w_gate, w_up),
-            gate_low[j],
-            up_low[j],
+            lambda *v: unwide(*v, w_gate, w_up, y),
+            *lows[j],
             outs=2,
         )
         chip, away = chip_sum(keep, give)
 
-        def unjoin(chip, away, dy, total, scale, j=j):
-            grad = own_rows(dy, j).astype(f32) + (chip.astype(f32) + away.astype(f32))
-            gained = gain_attn * grad
-            inner = jnp.sum(gained * total, 1, keepdims=True)
-            low = (scale * gained - total * scale**3 / full_width * inner).astype(bf16)
-            return low, grad, jnp.sum(grad * total * scale, 0)
-
-        low, grad, gains = step(
-            8.0, unjoin, chip, away, whole_dy, attn_total[j], attn_scale[j], outs=3
-        )
-        hidden_grad.append(grad)
+        low, own, give, gains = step(
+            5.5,
+            lambda a, b, c, d, *dy, j=j: norm_back_rows(
+                (a, b), (c, d), dy, None, 2 * j + core, rank, gain_attn
+            ),
+            *attn_sums[j],
+            chip,
+            away,
+            *dy_pieces,
+            outs=4,
+        )
+        hidden_grad.append((own, core_move(give)))
         attn_gains.append(gains)
         attn_low.append(both(low))
     grad_own = own_columns(hidden_grad)
@@ -1292,7 +1467,7 @@
     mixed_grad = step(6.0, unmix, whole_attn_low)
 
     query_gained, key_gained, value_grad_low, dots, head_gains = step(
-        21.0,
+        19.5,
         lambda q, k, v, m, qp, kp, s, cos, sin: unattend_heads(
             q, k, v, m, segments, qp, kp, s, full_width, gain_query, gain_key, cos, sin
         ),
@@ -1310,19 +1485,22 @@
     dots = small_sum(dots)
 
     def scaled_back(which, gained, projected):
-        run = lambda g, p, s, d: unscale(g, p, s, d, which, full_width)
-        return step(4.5, run, gained, projected, squares, dots)
-
-    query_low = scaled_back(0, query_gained, query_proj)
-    key_low = scaled_back(1, key_gained, key_proj)
+        run = lambda g, p, s, d: unscale(g, p, s, d, which, full_width, y)
+        return step(3.5, run, gained, projected, squares, dots, outs=2)
+
+    query_low, query_give = scaled_back(0, query_gained, query_proj)
+    key_low, key_give = scaled_back(1, key_gained, key_proj)
+    value_give = step(
+        1.0, lambda v: part(v, 1 - y, local_width // 2, 1), value_grad_low
+    )
 
     def pair_grad(left, right, shape):
         rows = shape[0] // 2
         give = step(
-            3.0, lambda a, b: dot(part(a, 1 - y, rows, 1), b, 0, 0).astype(bf16), left, right
+            4.8, lambda a, b: dot(part(a, 1 - y, rows, 1), b, 0, 0).astype(bf16), left, right
         )
         own = step(
-            3.5,
+            4.8,
             lambda a, b, c: (dot(part(a, y, rows, 1), b, 0, 0) + c.astype(f32)).astype(bf16),
             left,
             right,
@@ -1334,61 +1512,43 @@
     whole_mixed = step(1.5, joined, *mixed)
     out_grad = pair_grad(whole_mixed, whole_attn_low, (local_width, full_width))
 
-    x_own = step(2.5, lambda x: part(x, core, row_count // 2, 0), whole_x)
-    x_came = y_move(x_own)
-    neighbour_x = step(3.0, joined, x_came, core_move(x_came))
-
-    def core_first(value):
-        rows = row_count // 2
-        return joined(part(value, core, rows, 0), part(value, 1 - core, rows, 0))
-
-    def narrow_grad(low):
-        columns = local_width // 2
-        keep, give = step(
-            1.5, lambda v: (part(v, y, columns, 1), part(v, 1 - y, columns, 1)), low, outs=2
-        )
-        own = step(
-            5.0,
-            lambda x, k, n, c: (dot(x, k, 0, 0) + dot(n, core_first(c), 0, 0)).astype(bf16),
-            whole_x,
-            keep,
-            neighbour_x,
-            y_move(give),
-        )
+    came = [y_move(give) for give in (value_give, query_give, key_give)]
+    pieces = step(
+        11.0,
+        lambda x, n, v, q, k, cv, cq, ck: narrow_grads(x, n, (v, q, k), (cv, cq, ck), y),
+        whole_x,
+        neighbour_x,
+        value_grad_low,
+        query_low,
+        key_low,
+        *came,
+        outs=3,
+    )
+    narrow_results = []
+    for own in pieces:
         shape = (full_width, local_width)
         piece, result = put(None, shape, (0, y), *line_sum(own, 1.0), 1.0)
-        return set_down(result, shape, (0, 1 - y), y_move(piece), 1.0)
-
-    value_wgrad = narrow_grad(value_grad_low)
-    query_wgrad = narrow_grad(query_low)
-    key_wgrad = narrow_grad(key_low)
-
-    def column_part(which):
-        def run(query_low, key_low, value_low):
-            pieces = []
-            for x in (0, 1):
-                rows = (2 * x + which) * narrow
-                total = 0.0
-                for low, weight in ((query_low, w_query), (key_low, w_key), (value_low, w_value)):
-                    total = total + dot(
-                        low, lax.dynamic_slice_in_dim(weight, rows, narrow, 0), 1, 1
-                    )
-                pieces.append(total.astype(bf16))
-            return pieces
-
-        return run
-
-    lows = (query_low, key_low, value_grad_low)
-    give0, give1 = step(7.0, column_part(1 - core), *lows, outs=2)
-    keep0, keep1 = step(7.0, column_part(core), *lows, outs=2)
+        narrow_results.append(set_down(result, shape, (0, 1 - y), y_move(piece), 1.0))
+    value_wgrad, query_wgrad, key_wgrad = narrow_results
+
+    give, keep = step(
+        10.0,
+        lambda *v: input_columns(v, (w_query, w_key, w_value), core),
+        query_low,
+        key_low,
+        value_grad_low,
+        outs=2,
+    )
     x_here = rank // 2
 
-    def chip_columns(k0, k1, g0, g1):
-        k0, k1 = low_add(k0, g0), low_add(k1, g1)
-        first = x_here == 0
-        return jnp.where(first, k0, k1), jnp.where(first, k1, k0)
-
-    here, there = step(3.0, chip_columns, keep0, keep1, core_move(give0), core_move(give1), outs=2)
+    def chip_columns(keep, came):
+        total = low_add(keep, came)
+        return (
+            lax.dynamic_index_in_dim(total, x_here, 0, False),
+            lax.dynamic_index_in_dim(total, 1 - x_here, 0, False),
+        )
+
+    here, there = step(3.5, chip_columns, keep, core_move(give), outs=2)
     input_grad = step(
         2.0,
         lambda a, b, c: (a.astype(f32) + b.astype(f32) + c).astype(bf16),
@@ -1398,14 +1558,14 @@
     )
 
     wide_gains = step(
-        1.0, lambda a, b, c, d: jnp.stack([a + b, c + d]), *mlp_gains, *attn_gains
+        0.3, lambda a, b, c, d: joined(a + b, c + d), *mlp_gains, *attn_gains
     )
 
     def masked(a, b):
         mine = jnp.arange(full_width) // (full_width // 2) == rank // 2
         return jnp.where(mine, a + b, 0.0)
 
-    wide_gains = step(1.0, masked, wide_gains, core_move(wide_gains))
+    wide_gains = step(0.3, masked, wide_gains, core_move(wide_gains))
     gains = step(
         1.0,
         lambda a, b, h: jnp.concatenate([(a + b).reshape(-1), h.reshape(-1)]),
@@ -1413,10 +1573,10 @@
         x_move(wide_gains),
         head_gains,
     )
-    gains = step(0.6, lambda a, b: a + b, gains, y_move(gains))
-    gains = step(0.6, lambda a, b: a + b, gains, z_move("in", gains))
-    gains = step(0.6, lambda a, b: a + b, gains, z_move("mid", gains))
-    gains = step(0.6, lambda a, b: jnp.where(outer, a, b), z_move("out", gains), gains)
+    gains = step(0.2, lambda a, b: a + b, gains, y_move(gains))
+    gains = step(0.2, lambda a, b: a + b, gains, z_move("in", gains))
+    gains = step(0.2, lambda a, b: a + b, gains, z_move("mid", gains))
+    gains = step(0.2, lambda a, b: jnp.where(outer, a, b), z_move("out", gains), gains)
 
     plan.run()
     results = (

time: 1090 us -> 911 us (0.84)
  waiting for transfers between devices: 379 us -> 253 us
  Pallas kernels: 277 us -> 375 us
  matrix products: 104 us -> 28.2 us
  other arithmetic: 94.9 us -> 33.8 us
  local copies, waits for them, and re-layouts: 56.8 us -> 40.1 us
    ppermute x73 -> x71, waiting for transfers between devices: 320 us -> 183 us  [over_dp(): return lax.ppermute(value, 'dp', pairs)]
    pallas_call x47 -> x61, Pallas kernels: 164 us -> 285 us  [matmul_call(): pl.pallas_call(kernel, out_shape=[jax.ShapeDtypeStruct(s, d) for s, d, _,...]
    dot_general x37 -> x7, matrix products: 104 us -> 28.2 us  [dot(): lax.dot_general(left, right, (((left_axis,), (right_axis,)), ((), ())), p...]
    concatenate x15 -> x3, other arithmetic: 24.6 us -> 1.65 us  [joined(): return jnp.concatenate(values, 0)]
    pallas_call x8 -> x4, Pallas kernels: 29.3 us -> 12.3 us  [place_one(): pl.pallas_call(kernel, out_shape=jax.ShapeDtypeStruct(shape, f32), grid_s...]
    convert_element_type x6 -> x0, other arithmetic: 15.2 us -> none  [the longest x2 7.52 us: join(): return (total, scale, hidden, hidden.astype(bf16))]
    ppermute x12 -> x13, waiting for transfers between devices: 52 us -> 66.4 us  [to_x(): return lax.ppermute(value, 'tensor', SWAP_X)]
    reduce_sum x6 -> x0, other arithmetic: 13 us -> none  [the longest x2 5.58 us: finish(): jnp.sum(dy_rows * normed, 0)]
  transfers between devices with their start and end apart: 113 -> 112, of which waited for: 37 -> 34; matrix products, arithmetic and copies ran while one was open for 18% -> 8% of each run, Pallas kernels for 25% -> 41%
where the time goes in v2:
time: 911 us; the launch traced here: 899 us
  Pallas kernels  375 us (41%)
  waiting for transfers between devices  253 us (28%)
  starting transfers between devices  168 us (18%)
  local copies, waits for them, and re-layouts  40.1 us (4%)
  other arithmetic  33.8 us (4%)
  matrix products  28.2 us (3%)
    pallas_call x61, Pallas kernels, matmul_call(): pl.pallas_call(kernel, out_shape=[jax.ShapeDtypeStruct(s, d) for s, d, _,...  285 us
    ppermute x71, waiting for transfers between devices, over_dp(): return lax.ppermute(value, 'dp', pairs)  183 us
    ppermute x71, starting transfers between devices, over_dp(): return lax.ppermute(value, 'dp', pairs)  146 us
    ppermute x13, waiting for transfers between devices, to_x(): return lax.ppermute(value, 'tensor', SWAP_X)  66.4 us
    pallas_call x10, Pallas kernels, pick_and_place(): pl.pallas_call(kernel, out_shape=[jax.ShapeDtypeStruct(first.shape, bf16)...  43 us
    unnamed x222, local copies, waits for them, and re-layouts  33.2 us
    pallas_call x10, Pallas kernels, place(): pl.pallas_call(kernel, out_shape=jax.ShapeDtypeStruct(shape, f32), grid_s...  30.5 us
    dot_general x7, matrix products, dot(): lax.dot_general(left, right, (((left_axis,), (right_axis,)), ((), ())), p...  28.2 us
  transfers between devices with their start and end apart: 112, of which 34 were waited for; matrix products, arithmetic and copies ran while one was open for 8% of the time, Pallas kernels for 41%

profile of v2, /device:TPU:0, one launch (start us, length us, event | category | flops | bytes accessed | tf_op | source)
XLA Modules:
  0.0 899.5 jit_solution(17432418908317503484)
XLA Ops:
  5.2 21.8 %collective-permute-done.2.refs_2_ = bf16[1024,512]{1,0:T(8,128)(2,1)S(1)} collective-permute-done((bf16[1024,512]{1,0:T(8,128)(2,1)}, bf16[1024,512]{1,0:T(8,128)(2,1)S(1)}, u32[]{:S(2)}, u32[]{:S(2)}) %collective-permute-start.2) | collective-permute-done | bytes 1048608 | tf_op jit(solution)/shard_map/ppermute | solution.py:356
  36.1 11.2 %shard_map.237 = (f32[1024,512]{1,0:T(8,128)}, f32[1024,512]{1,0:T(8,128)}, bf16[1024,512]{1,0:T(8,128)(2,1)}, f32[2,1024]{1,0:T(2,128)}) custom-call(bf16[1024,2048]{1,0:T(8,128)(2,1)} %copy-done.2, bf16[2048,512]{1,0:T(8,128)(2,1)} %w0.1, bf16[2048,512]{1,0:T(8,128)(2,1)} %w1.1, bf16[2048,512]{1,0:T(8,128)(2,1)} %w2.1), custom_call_target="tpu_custom_call" | custom-call | flops 6442450944 | bytes 15736832 | tf_op jit(solution)/shard_map/pallas_call | solution.py:452
  79.1 16.5 %collective-permute-done.12.refs_5_.refs_6_ = bf16[1024,512]{1,0:T(8,128)(2,1)S(1)} collective-permute-done((bf16[1024,512]{1,0:T(8,128)(2,1)S(1)}, bf16[1024,512]{1,0:T(8,128)(2,1)S(1)}, u32[]{:S(2)}, u32[]{:S(2)}) %collective-permute-start.12) | collective-permute-done | bytes 1048608 | tf_op jit(solution)/shard_map/ppermute | solution.py:356
  105.3 21.5 %collective-permute-done.10.away_ref.refs_1_ = bf16[256,2048]{1,0:T(8,128)(2,1)S(1)} collective-permute-done((bf16[256,2048]{1,0:T(8,128)(2,1)S(1)}, bf16[256,2048]{1,0:T(8,128)(2,1)S(1)}, u32[]{:S(2)}, u32[]{:S(2)}) %collective-permute-start.10) | collective-permute-done | bytes 1048608 | tf_op jit(solution)/shard_map/ppermute | solution.py:356
  135.7 14.2 %shard_map.244 = (bf16[512,2048]{1,0:T(8,128)(2,1)}, bf16[512,2048]{1,0:T(8,128)(2,1)}, bf16[512,2048]{1,0:T(8,128)(2,1)}) custom-call(bf16[512,2048]{1,0:T(8,128)(2,1)} %pad_maximum_fusion.1.low_ref.h0, bf16[2048,2048]{1,0:T(8,128)(2,1)} %keep_gw.3, bf16[2048,2048]{1,0:T(8,128)(2,1)} %keep_uw.3), custom_call_target="tpu_custom_call" | custom-call | flops 8589934592 | bytes 25165824 | tf_op jit(solution)/shard_map/pallas_call | solution.py:452
  149.9 8.5 convolution_convert_fusion.1
  170.9 13.8 %shard_map.247 = (bf16[512,2048]{1,0:T(8,128)(2,1)}, bf16[512,2048]{1,0:T(8,128)(2,1)}, bf16[512,2048]{1,0:T(8,128)(2,1)}) custom-call(bf16[512,2048]{1,0:T(8,128)(2,1)} %pad_maximum_fusion.2.low_ref.h1, bf16[2048,2048]{1,0:T(8,128)(2,1)} %keep_gw.3, bf16[2048,2048]{1,0:T(8,128)(2,1)} %keep_uw.3), custom_call_target="tpu_custom_call" | custom-call | flops 8589934592 | bytes 25165824 | tf_op jit(solution)/shard_map/pallas_call | solution.py:452
  184.7 8.5 convolution_convert_fusion
  208.7 11.5 %shard_map.250 = (bf16[512,1024]{1,0:T(8,128)(2,1)}, bf16[512,1024]{1,0:T(8,128)(2,1)}, bf16[512,1024]{1,0:T(8,128)(2,1)}, bf16[512,1024]{1,0:T(8,128)(2,1)}) custom-call(s32[1]{0:T(128)} %bitcast._.y_ref, bf16[512,2048]{1,0:T(8,128)(2,1)} %pad_maximum_fusion.3.low_ref.b0, bf16[2048,2048]{1,0:T(8,128)(2,1)} %down_w.3, ...), custom_call_target="tpu_custom_call" | custom-call | flops 4294967296 | bytes 18874368 | tf_op jit(solution)/shard_map/pallas_call | solution.py:452
  220.2 14.3 %shard_map.251 = (bf16[256,2048]{1,0:T(8,128)(2,1)}, bf16[256,2048]{1,0:T(8,128)(2,1)}) custom-call(s32[1]{0:T(128)} %bitcast._.y_ref, bf16[512,1024]{1,0:T(8,128)(2,1)} %get-tuple-element.895.give_g, bf16[512,1024]{1,0:T(8,128)(2,1)} %get-tuple-element.838.give_u, bf16[512,1024]{1,0:T(8,128)(2,1)} %get-tuple-element.965.keep_g.o0, ...), custom_call_target="tpu_custom_call" | custom-call | flops 8589934592 | bytes 39845888 | tf_op jit(solution)/shard_map/pallas_call | solution.py:452
  250.0 11.3 %shard_map.254 = (bf16[512,1024]{1,0:T(8,128)(2,1)}, bf16[512,1024]{1,0:T(8,128)(2,1)}, bf16[512,1024]{1,0:T(8,128)(2,1)}, bf16[512,1024]{1,0:T(8,128)(2,1)}) custom-call(s32[1]{0:T(128)} %bitcast._.y_ref, bf16[512,2048]{1,0:T(8,128)(2,1)} %pad_maximum_fusion.4.low_ref.b1, bf16[2048,2048]{1,0:T(8,128)(2,1)} %down_w.3, ...), custom_call_target="tpu_custom_call" | custom-call | flops 4294967296 | bytes 18874368 | tf_op jit(solution)/shard_map/pallas_call | solution.py:452
  267.2 10.7 %shard_map.255 = (bf16[256,2048]{1,0:T(8,128)(2,1)}, bf16[256,2048]{1,0:T(8,128)(2,1)}, bf16[256,2048]{1,0:T(8,128)(2,1)}, bf16[256,2048]{1,0:T(8,128)(2,1)}) custom-call(s32[4]{0:T(128)} %get-tuple-element.1435._, bf16[512,2048]{1,0:T(8,128)(2,1)} %get-tuple-element.897.a0, bf16[512,2048]{1,0:T(8,128)(2,1)} %get-tuple-element.898.a1, ...), custom_call_target="tpu_custom_call" | custom-call | flops 8589934592 | bytes 12582912 | tf_op jit(solution)/shard_map/pallas_call | solution.py:452
  282.2 14.1 %shard_map.256 = (bf16[256,2048]{1,0:T(8,128)(2,1)}, bf16[256,2048]{1,0:T(8,128)(2,1)}) custom-call(s32[1]{0:T(128)} %bitcast._.y_ref, bf16[512,1024]{1,0:T(8,128)(2,1)} %get-tuple-element.929.give_g, bf16[512,1024]{1,0:T(8,128)(2,1)} %get-tuple-element.890.give_u, bf16[512,1024]{1,0:T(8,128)(2,1)} %get-tuple-element.966.keep_g.o1, ...), custom_call_target="tpu_custom_call" | custom-call | flops 8589934592 | bytes 39845888 | tf_op jit(solution)/shard_map/pallas_call | solution.py:452
  297.8 10.9 %shard_map.257 = (bf16[256,2048]{1,0:T(8,128)(2,1)}, bf16[256,2048]{1,0:T(8,128)(2,1)}, bf16[256,2048]{1,0:T(8,128)(2,1)}, bf16[256,2048]{1,0:T(8,128)(2,1)}) custom-call(s32[4]{0:T(128)} %get-tuple-element.1436._, bf16[512,2048]{1,0:T(8,128)(2,1)} %get-tuple-element.897.a0, bf16[512,2048]{1,0:T(8,128)(2,1)} %get-tuple-element.898.a1, ...), custom_call_target="tpu_custom_call" | custom-call | flops 8589934592 | bytes 12582912 | tf_op jit(solution)/shard_map/pallas_call | solution.py:452
  314.5 13.7 %shard_map.259 = (bf16[2048,512]{1,0:T(8,128)(2,1)}, bf16[2048,512]{1,0:T(8,128)(2,1)}) custom-call(bf16[512,2048]{1,0:T(8,128)(2,1)} %pad_maximum_fusion.1.low_ref.h0, bf16[512,2048]{1,0:T(8,128)(2,1)} %pad_maximum_fusion.2.low_ref.h1, bf16[256,2048]{1,0:T(8,128)(2,1)} %collective-permute-done.16.n0, bf16[256,2048]{1,0:T(8,128)(2,1)} %collective-permute-done.22.x0, ...), custom_call_target="tpu_custom_call" | custom-call | flops 8589934592 | bytes 16777216 | tf_op jit(solution)/shard_map/pallas_call | solution.py:452
  353.3 13.5 %shard_map.264 = (bf16[2048,512]{1,0:T(8,128)(2,1)}, bf16[2048,512]{1,0:T(8,128)(2,1)}) custom-call(bf16[512,2048]{1,0:T(8,128)(2,1)} %pad_maximum_fusion.1.low_ref.h0, bf16[512,2048]{1,0:T(8,128)(2,1)} %pad_maximum_fusion.2.low_ref.h1, bf16[256,2048]{1,0:T(8,128)(2,1)} %collective-permute-done.16.n0, bf16[256,2048]{1,0:T(8,128)(2,1)} %collective-permute-done.22.x0, ...), custom_call_target="tpu_custom_call" | custom-call | flops 8589934592 | bytes 16777216 | tf_op jit(solution)/shard_map/pallas_call | solution.py:452
  366.8 9.1 %collective-permute-done.43.right_ref = bf16[256,2048]{1,0:T(8,128)(2,1)} collective-permute-done((bf16[256,2048]{1,0:T(8,128)(2,1)}, bf16[256,2048]{1,0:T(8,128)(2,1)}, u32[]{:S(2)}, u32[]{:S(2)}) %collective-permute-start.43) | collective-permute-done | bytes 1048608 | tf_op jit(solution)/shard_map/ppermute | solution.py:348
  414.9 17.0 %collective-permute-done.50.right_ref = bf16[256,2048]{1,0:T(8,128)(2,1)S(1)} collective-permute-done((bf16[256,2048]{1,0:T(8,128)(2,1)}, bf16[256,2048]{1,0:T(8,128)(2,1)S(1)}, u32[]{:S(2)}, u32[]{:S(2)}) %collective-permute-start.50) | collective-permute-done | bytes 1048608 | tf_op jit(solution)/shard_map/ppermute | solution.py:348
  443.6 19.5 %shard_map.269 = (f32[1024,512]{1,0:T(8,128)}, f32[1024,512]{1,0:T(8,128)}, bf16[1024,512]{1,0:T(8,128)(2,1)}, f32[2,1024]{1,0:T(2,128)}, f32[2,512]{1,0:T(2,128)}) custom-call(bf16[1024,512]{1,0:T(8,128)(2,1)} %copy-done.75, bf16[1024,512]{1,0:T(8,128)(2,1)} %copy-done.76, bf16[1024,512]{1,0:T(8,128)(2,1)} %get-tuple-element.1005.v_ref, ...), custom_call_target="tpu_custom_call" | custom-call | flops 5368709120 | bytes 14708736 | tf_op jit(solution)/shard_map/pallas_call | solution.py:452
  499.7 13.4 %collective-permute-done.61.right_ref = bf16[256,2048]{1,0:T(8,128)(2,1)S(1)} collective-permute-done((bf16[256,2048]{1,0:T(8,128)(2,1)S(1)}, bf16[256,2048]{1,0:T(8,128)(2,1)S(1)}, u32[]{:S(2)}, u32[]{:S(2)}) %collective-permute-start.61) | collective-permute-done | bytes 1048608 | tf_op jit(solution)/shard_map/ppermute | solution.py:348
  546.6 11.7 %shard_map.279 = (bf16[2,1024,512]{2,1,0:T(8,128)(2,1)}, bf16[2,1024,512]{2,1,0:T(8,128)(2,1)}) custom-call(s32[1]{0:T(128)} %bitcast.7._, bf16[1024,512]{1,0:T(8,128)(2,1)} %copy-done.89, bf16[1024,512]{1,0:T(8,128)(2,1)} %copy-done.90, bf16[1024,512]{1,0:T(8,128)(2,1)} %get-tuple-element.1228.a2.refs_0_, bf16[2048,512]{1,0:T(8,128)(2,1)} %w0.1, ...), custom_call_target="tpu_custom_call" | custom-call | flops 6442450944 | bytes 13631488 | tf_op jit(solution)/shard_map/pallas_call | solution.py:452
  566.6 10.2 %collective-permute-start.74 = (bf16[256,2048]{1,0:T(8,128)(2,1)}, bf16[256,2048]{1,0:T(8,128)(2,1)}, u32[]{:S(2)}, u32[]{:S(2)}) collective-permute-start(bf16[256,2048]{1,0:T(8,128)(2,1)} %shard_map.273.left_ref), channel_id=1, source_target_pairs={{0,8},{4,12},{24,16},{28,20},{1,9},{5,13},{25,17},{29,21},{2,10},{... | collective-permute-start | bytes 3145736 | tf_op jit(solution)/shard_map/ppermute | solution.py:348
  583.2 8.9 collective-permute-done.69.block_ref
  651.9 12.5 %collective-permute-start.87 = (bf16[256,2048]{1,0:T(8,128)(2,1)S(1)}, bf16[256,2048]{1,0:T(8,128)(2,1)}, u32[]{:S(2)}, u32[]{:S(2)}) collective-permute-start(bf16[256,2048]{1,0:T(8,128)(2,1)S(1)} %shard_map.277.first_ref), channel_id=1, source_target_pairs={{0,8},{4,12},{24,16},{28,20},{1,9},{5,13},{25,17},{29,21},{2,10},{... | collective-permute-start | bytes 3145736 | tf_op jit(solution)/shard_map/ppermute | solution.py:348
  674.5 10.7 %shard_map.289 = (bf16[2048,256]{1,0:T(8,128)(2,1)}, bf16[2048,256]{1,0:T(8,128)(2,1)}, bf16[2048,256]{1,0:T(8,128)(2,1)}) custom-call(s32[1]{0:T(128)} %bitcast._.y_ref, bf16[1024,2048]{1,0:T(8,128)(2,1)} %copy-done.2, bf16[1024,2048]{1,0:T(8,128)(2,1)} %copy-done.38, bf16[1024,512]{1,0:T(8,128)(2,1)} %get-tuple-element.1228.a2.refs_0_, ...), custom_call_target="tpu_custom_call" | custom-call | flops 6442450944 | bytes 16252928 | tf_op jit(solution)/shard_map/pallas_call | solution.py:452
  720.3 15.6 %collective-permute-done.91.first_ref = bf16[256,2048]{1,0:T(8,128)(2,1)S(1)} collective-permute-done((bf16[256,2048]{1,0:T(8,128)(2,1)}, bf16[256,2048]{1,0:T(8,128)(2,1)S(1)}, u32[]{:S(2)}, u32[]{:S(2)}) %collective-permute-start.91) | collective-permute-done | bytes 1048608 | tf_op jit(solution)/shard_map/ppermute | solution.py:348
  794.2 15.5 %collective-permute-done.99.block_ref = bf16[256,2048]{1,0:T(8,128)(2,1)} collective-permute-done((bf16[256,2048]{1,0:T(8,128)(2,1)}, bf16[256,2048]{1,0:T(8,128)(2,1)}, u32[]{:S(2)}, u32[]{:S(2)}) %collective-permute-start.99) | collective-permute-done | bytes 1048608 | tf_op jit(solution)/shard_map/ppermute | solution.py:348
  818.4 14.1 %collective-permute-done.105.first_ref = bf16[2048,256]{1,0:T(8,128)(2,1)} collective-permute-done((bf16[2048,256]{1,0:T(8,128)(2,1)}, bf16[2048,256]{1,0:T(8,128)(2,1)}, u32[]{:S(2)}, u32[]{:S(2)}) %collective-permute-start.105) | collective-permute-done | bytes 1048608 | tf_op jit(solution)/shard_map/ppermute | solution.py:348
  844.5 10.5 %collective-permute-done.104.first_ref = bf16[2048,256]{1,0:T(8,128)(2,1)} collective-permute-done((bf16[2048,256]{1,0:T(8,128)(2,1)S(1)}, bf16[2048,256]{1,0:T(8,128)(2,1)}, u32[]{:S(2)}, u32[]{:S(2)}) %collective-permute-start.104) | collective-permute-done | bytes 1048608 | tf_op jit(solution)/shard_map/ppermute | solution.py:348
  861.4 6.8 collective-permute-done.109.first_ref
  874.7 7.1 collective-permute-done.108.block_ref
  883.8 12.4 %collective-permute-done.111.block_ref = bf16[256,2048]{1,0:T(8,128)(2,1)S(1)} collective-permute-done((bf16[256,2048]{1,0:T(8,128)(2,1)}, bf16[256,2048]{1,0:T(8,128)(2,1)S(1)}, u32[]{:S(2)}, u32[]{:S(2)}) %collective-permute-start.111) | collective-permute-done | bytes 1048608 | tf_op jit(solution)/shard_map/ppermute | solution.py:348
  (582 shorter events, 486.0 us)
Async XLA Ops:
  242.1 54.2 %collective-permute-start.33 = (bf16[512,1024]{1,0:T(8,128)(2,1)}, bf16[512,1024]{1,0:T(8,128)(2,1)S(1)}, u32[]{:S(2)}, u32[]{:S(2)}) collective-permute-start(bf16[512,1024]{1,0:T(8,128)(2,1)} %get-tuple-element.895.give_g), channel_id=1, source_target_pairs={{0,4},{4,0},{8,12},{12,8},{16,20},{20,16},{24,28},{28,24},{1,5},{5... | collective-permute-start | bytes 3145736 | tf_op jit(solution)/shard_map/ppermute | solution.py:348
  344.0 49.8 %collective-permute-start.35 = (bf16[2048,512]{1,0:T(8,128)(2,1)}, bf16[2048,512]{1,0:T(8,128)(2,1)}, u32[]{:S(2)}, u32[]{:S(2)}) collective-permute-start(bf16[2048,512]{1,0:T(8,128)(2,1)} %get-tuple-element.992.left_ref), channel_id=1, source_target_pairs={{0,8},{4,12},{24,16},{28,20},{1,9},{5,13},{25,17},{29,21},{2,10},{... | collective-permute-start | bytes 6291464 | tf_op jit(solution)/shard_map/ppermute | solution.py:348
  386.5 45.5 %collective-permute-start.50 = (bf16[256,2048]{1,0:T(8,128)(2,1)}, bf16[256,2048]{1,0:T(8,128)(2,1)S(1)}, u32[]{:S(2)}, u32[]{:S(2)}) collective-permute-start(bf16[256,2048]{1,0:T(8,128)(2,1)} %get-tuple-element.1024), channel_id=1, source_target_pairs={{0,4},{4,0},{8,12},{12,8},{16,20},{20,16},{24,28},{28,24},{1,5},{5... | collective-permute-start | bytes 3145736 | tf_op jit(solution)/shard_map/ppermute | solution.py:348
  387.7 50.2 %collective-permute-start.48 = (bf16[2048,512]{1,0:T(8,128)(2,1)}, bf16[2048,512]{1,0:T(8,128)(2,1)}, u32[]{:S(2)}, u32[]{:S(2)}) collective-permute-start(bf16[2048,512]{1,0:T(8,128)(2,1)} %get-tuple-element.1015.left_ref), channel_id=1, source_target_pairs={{0,8},{4,12},{24,16},{28,20},{1,9},{5,13},{25,17},{29,21},{2,10},{... | collective-permute-start | bytes 6291464 | tf_op jit(solution)/shard_map/ppermute | solution.py:348
  397.2 69.4 %collective-permute-start.51 = (bf16[2048,512]{1,0:T(8,128)(2,1)}, bf16[2048,512]{1,0:T(8,128)(2,1)}, u32[]{:S(2)}, u32[]{:S(2)}) collective-permute-start(bf16[2048,512]{1,0:T(8,128)(2,1)} %shard_map.268.left_ref), channel_id=1, source_target_pairs={{8,16},{12,20},{16,8},{20,12},{9,17},{13,21},{17,9},{21,13},{10,18... | collective-permute-start | bytes 6291464 | tf_op jit(solution)/shard_map/ppermute | solution.py:348
  410.4 59.8 %collective-permute-start.53 = (bf16[256,2048]{1,0:T(8,128)(2,1)}, bf16[256,2048]{1,0:T(8,128)(2,1)}, u32[]{:S(2)}, u32[]{:S(2)}) collective-permute-start(bf16[256,2048]{1,0:T(8,128)(2,1)} %shard_map.267), channel_id=1, source_target_pairs={{8,0},{12,4},{16,24},{20,28},{9,1},{13,5},{17,25},{21,29},{10,2},{... | collective-permute-start | bytes 3145736 | tf_op jit(solution)/shard_map/ppermute | solution.py:348
  411.7 61.4 %collective-permute-start.54 = (bf16[256,2048]{1,0:T(8,128)(2,1)}, bf16[256,2048]{1,0:T(8,128)(2,1)}, u32[]{:S(2)}, u32[]{:S(2)}) collective-permute-start(bf16[256,2048]{1,0:T(8,128)(2,1)} %shard_map.265.left_ref), channel_id=1, source_target_pairs={{0,4},{4,0},{24,28},{28,24},{1,5},{5,1},{25,29},{29,25},{2,6},{6,2... | collective-permute-start | bytes 3145736 | tf_op jit(solution)/shard_map/ppermute | solution.py:348
  431.9 45.1 %collective-permute-start.56 = (f32[256,512]{1,0:T(8,128)}, f32[256,512]{1,0:T(8,128)S(1)}, u32[]{:S(2)}, u32[]{:S(2)}) collective-permute-start(f32[256,512]{1,0:T(8,128)} %get-tuple-element.1053), channel_id=1, source_target_pairs={{0,1},{1,0},{2,3},{3,2},{4,5},{5,4},{6,7},{7,6},{8,9},{9,8},{10,11... | collective-permute-start | bytes 1572872 | tf_op jit(solution)/shard_map/ppermute | solution.py:352
  437.9 57.5 %collective-permute-start.57 = (bf16[2048,512]{1,0:T(8,128)(2,1)}, bf16[2048,512]{1,0:T(8,128)(2,1)}, u32[]{:S(2)}, u32[]{:S(2)}) collective-permute-start(bf16[2048,512]{1,0:T(8,128)(2,1)} %get-tuple-element.1082.left_ref), channel_id=1, source_target_pairs={{0,8},{4,12},{24,16},{28,20},{1,9},{5,13},{25,17},{29,21},{2,10},{... | collective-permute-start | bytes 6291464 | tf_op jit(solution)/shard_map/ppermute | solution.py:348
  473.1 49.1 %collective-permute-start.49 = (bf16[2048,512]{1,0:T(8,128)(2,1)S(1)}, bf16[2048,512]{1,0:T(8,128)(2,1)}, u32[]{:S(2)}, u32[]{:S(2)}) collective-permute-start(bf16[2048,512]{1,0:T(8,128)(2,1)S(1)} %shard_map.270.left_ref), channel_id=1, source_target_pairs={{8,16},{12,20},{16,8},{20,12},{9,17},{13,21},{17,9},{21,13},{10,18... | collective-permute-start | bytes 6291464 | tf_op jit(solution)/shard_map/ppermute | solution.py:348
  477.1 49.7 %collective-permute-start.62 = (bf16[2048,512]{1,0:T(8,128)(2,1)}, bf16[2048,512]{1,0:T(8,128)(2,1)}, u32[]{:S(2)}, u32[]{:S(2)}) collective-permute-start(bf16[2048,512]{1,0:T(8,128)(2,1)} %shard_map.271.second_ref), channel_id=1, source_target_pairs={{8,0},{12,4},{16,24},{20,28},{9,1},{13,5},{17,25},{21,29},{10,2},{... | collective-permute-start | bytes 6291464 | tf_op jit(solution)/shard_map/ppermute | solution.py:348
  487.8 58.0 %collective-permute-start.66 = (bf16[2048,512]{1,0:T(8,128)(2,1)}, bf16[2048,512]{1,0:T(8,128)(2,1)}, u32[]{:S(2)}, u32[]{:S(2)}) collective-permute-start(bf16[2048,512]{1,0:T(8,128)(2,1)} %get-tuple-element.1129.left_ref), channel_id=1, source_target_pairs={{0,8},{4,12},{24,16},{28,20},{1,9},{5,13},{25,17},{29,21},{2,10},{... | collective-permute-start | bytes 6291464 | tf_op jit(solution)/shard_map/ppermute | solution.py:348
  495.4 40.2 %collective-permute-start.63 = (bf16[256,2048]{1,0:T(8,128)(2,1)}, bf16[256,2048]{1,0:T(8,128)(2,1)}, u32[]{:S(2)}, u32[]{:S(2)}) collective-permute-start(bf16[256,2048]{1,0:T(8,128)(2,1)} %convolution_convert_fusion.4), channel_id=1, source_target_pairs={{0,4},{4,0},{8,12},{12,8},{16,20},{20,16},{24,28},{28,24},{1,5},{5... | collective-permute-start | bytes 3145736 | tf_op jit(solution)/shard_map/ppermute | solution.py:348
  514.0 46.2 %collective-permute-start.65 = (bf16[2048,512]{1,0:T(8,128)(2,1)}, bf16[2048,512]{1,0:T(8,128)(2,1)}, u32[]{:S(2)}, u32[]{:S(2)}) collective-permute-start(bf16[2048,512]{1,0:T(8,128)(2,1)} %shard_map.274.left_ref), channel_id=1, source_target_pairs={{8,16},{12,20},{16,8},{20,12},{9,17},{13,21},{17,9},{21,13},{10,18... | collective-permute-start | bytes 6291464 | tf_op jit(solution)/shard_map/ppermute | solution.py:348
  526.8 50.0 %collective-permute-start.64 = (bf16[2048,512]{1,0:T(8,128)(2,1)}, bf16[2048,512]{1,0:T(8,128)(2,1)}, u32[]{:S(2)}, u32[]{:S(2)}) collective-permute-start(bf16[2048,512]{1,0:T(8,128)(2,1)} %shard_map.276.second_ref), channel_id=1, source_target_pairs={{8,0},{12,4},{16,24},{20,28},{9,1},{13,5},{17,25},{21,29},{10,2},{... | collective-permute-start | bytes 6291464 | tf_op jit(solution)/shard_map/ppermute | solution.py:348
  545.8 46.4 %collective-permute-start.69 = (bf16[2048,512]{1,0:T(8,128)(2,1)}, bf16[2048,512]{1,0:T(8,128)(2,1)}, u32[]{:S(2)}, u32[]{:S(2)}) collective-permute-start(bf16[2048,512]{1,0:T(8,128)(2,1)} %get-tuple-element.1108), channel_id=1, source_target_pairs={{0,4},{4,0},{8,12},{12,8},{16,20},{20,16},{24,28},{28,24},{1,5},{5... | collective-permute-start | bytes 6291464 | tf_op jit(solution)/shard_map/ppermute | solution.py:348
  560.1 50.6 %collective-permute-start.73 = (bf16[2,1024,512]{2,1,0:T(8,128)(2,1)}, bf16[2,1024,512]{2,1,0:T(8,128)(2,1)}, u32[]{:S(2)}, u32[]{:S(2)}) collective-permute-start(bf16[2,1024,512]{2,1,0:T(8,128)(2,1)} %get-tuple-element.1164), channel_id=1, source_target_pairs={{0,1},{1,0},{2,3},{3,2},{4,5},{5,4},{6,7},{7,6},{8,9},{9,8},{10,11... | collective-permute-start | bytes 6291464 | tf_op jit(solution)/shard_map/ppermute | solution.py:352
  560.2 55.8 %collective-permute-start.72 = (bf16[2048,512]{1,0:T(8,128)(2,1)S(1)}, bf16[2048,512]{1,0:T(8,128)(2,1)}, u32[]{:S(2)}, u32[]{:S(2)}) collective-permute-start(bf16[2048,512]{1,0:T(8,128)(2,1)S(1)} %shard_map.280.left_ref), channel_id=1, source_target_pairs={{8,16},{12,20},{16,8},{20,12},{9,17},{13,21},{17,9},{21,13},{10,18... | collective-permute-start | bytes 6291464 | tf_op jit(solution)/shard_map/ppermute | solution.py:348
  576.8 57.4 %collective-permute-start.77 = (bf16[2048,512]{1,0:T(8,128)(2,1)}, bf16[2048,512]{1,0:T(8,128)(2,1)}, u32[]{:S(2)}, u32[]{:S(2)}) collective-permute-start(bf16[2048,512]{1,0:T(8,128)(2,1)} %shard_map.281.second_ref), channel_id=1, source_target_pairs={{8,0},{12,4},{16,24},{20,28},{9,1},{13,5},{17,25},{21,29},{10,2},{... | collective-permute-start | bytes 6291464 | tf_op jit(solution)/shard_map/ppermute | solution.py:348
  603.1 48.8 %collective-permute-start.82 = (bf16[2048,512]{1,0:T(8,128)(2,1)}, bf16[2048,512]{1,0:T(8,128)(2,1)}, u32[]{:S(2)}, u32[]{:S(2)}) collective-permute-start(bf16[2048,512]{1,0:T(8,128)(2,1)} %get-tuple-element.1216), channel_id=1, source_target_pairs={{0,4},{4,0},{8,12},{12,8},{16,20},{20,16},{24,28},{28,24},{1,5},{5... | collective-permute-start | bytes 6291464 | tf_op jit(solution)/shard_map/ppermute | solution.py:348
  629.4 38.9 %collective-permute-start.76 = (bf16[256,2048]{1,0:T(8,128)(2,1)}, bf16[256,2048]{1,0:T(8,128)(2,1)}, u32[]{:S(2)}, u32[]{:S(2)}) collective-permute-start(bf16[256,2048]{1,0:T(8,128)(2,1)} %shard_map.282.first_ref), channel_id=1, source_target_pairs={{0,8},{4,12},{24,16},{28,20},{1,9},{5,13},{25,17},{29,21},{2,10},{... | collective-permute-start | bytes 3145736 | tf_op jit(solution)/shard_map/ppermute | solution.py:348
  634.2 54.2 %collective-permute-start.84 = (bf16[2048,512]{1,0:T(8,128)(2,1)S(1)}, bf16[2048,512]{1,0:T(8,128)(2,1)}, u32[]{:S(2)}, u32[]{:S(2)}) collective-permute-start(bf16[2048,512]{1,0:T(8,128)(2,1)S(1)} %shard_map.286.second_ref), channel_id=1, source_target_pairs={{8,0},{12,4},{16,24},{20,28},{9,1},{13,5},{17,25},{21,29},{10,2},{... | collective-permute-start | bytes 6291464 | tf_op jit(solution)/shard_map/ppermute | solution.py:348
  644.7 40.6 %collective-permute-start.85 = (bf16[256,2048]{1,0:T(8,128)(2,1)}, bf16[256,2048]{1,0:T(8,128)(2,1)S(1)}, u32[]{:S(2)}, u32[]{:S(2)}) collective-permute-start(bf16[256,2048]{1,0:T(8,128)(2,1)} %copy-done.31), channel_id=1, source_target_pairs={{8,16},{12,20},{16,8},{20,12},{9,17},{13,21},{17,9},{21,13},{10,18... | collective-permute-start | bytes 3145736 | tf_op jit(solution)/shard_map/ppermute | solution.py:348
  651.9 45.8 %collective-permute-start.87 = (bf16[256,2048]{1,0:T(8,128)(2,1)S(1)}, bf16[256,2048]{1,0:T(8,128)(2,1)}, u32[]{:S(2)}, u32[]{:S(2)}) collective-permute-start(bf16[256,2048]{1,0:T(8,128)(2,1)S(1)} %shard_map.277.first_ref), channel_id=1, source_target_pairs={{0,8},{4,12},{24,16},{28,20},{1,9},{5,13},{25,17},{29,21},{2,10},{... | collective-permute-start | bytes 3145736 | tf_op jit(solution)/shard_map/ppermute | solution.py:348
  668.3 50.7 %collective-permute-start.90 = (bf16[2048,512]{1,0:T(8,128)(2,1)}, bf16[2048,512]{1,0:T(8,128)(2,1)}, u32[]{:S(2)}, u32[]{:S(2)}) collective-permute-start(bf16[2048,512]{1,0:T(8,128)(2,1)} %get-tuple-element.1280), channel_id=1, source_target_pairs={{0,4},{4,0},{8,12},{12,8},{16,20},{20,16},{24,28},{28,24},{1,5},{5... | collective-permute-start | bytes 6291464 | tf_op jit(solution)/shard_map/ppermute | solution.py:348
  697.8 67.1 %collective-permute-start.95 = (bf16[2048,512]{1,0:T(8,128)(2,1)}, bf16[2048,512]{1,0:T(8,128)(2,1)}, u32[]{:S(2)}, u32[]{:S(2)}) collective-permute-start(bf16[2048,512]{1,0:T(8,128)(2,1)} %get-tuple-element.1269), channel_id=1, source_target_pairs={{0,4},{4,0},{8,12},{12,8},{16,20},{20,16},{24,28},{28,24},{1,5},{5... | collective-permute-start | bytes 6291464 | tf_op jit(solution)/shard_map/ppermute | solution.py:348
  713.6 40.3 %collective-permute-start.94 = (bf16[2048,256]{1,0:T(8,128)(2,1)S(1)}, bf16[2048,256]{1,0:T(8,128)(2,1)}, u32[]{:S(2)}, u32[]{:S(2)}) collective-permute-start(bf16[2048,256]{1,0:T(8,128)(2,1)S(1)} %copy-done.57), channel_id=1, source_target_pairs={{0,8},{4,12},{24,16},{28,20},{1,9},{5,13},{25,17},{29,21},{2,10},{... | collective-permute-start | bytes 3145736 | tf_op jit(solution)/shard_map/ppermute | solution.py:348
  717.4 39.5 %collective-permute-start.93 = (bf16[2048,256]{1,0:T(8,128)(2,1)S(1)}, bf16[2048,256]{1,0:T(8,128)(2,1)}, u32[]{:S(2)}, u32[]{:S(2)}) collective-permute-start(bf16[2048,256]{1,0:T(8,128)(2,1)S(1)} %shard_map.291.left_ref), channel_id=1, source_target_pairs={{8,16},{12,20},{16,8},{20,12},{9,17},{13,21},{17,9},{21,13},{10,18... | collective-permute-start | bytes 3145736 | tf_op jit(solution)/shard_map/ppermute | solution.py:348
  719.0 41.8 %collective-permute-start.89 = (bf16[256,2048]{1,0:T(8,128)(2,1)}, bf16[256,2048]{1,0:T(8,128)(2,1)}, u32[]{:S(2)}, u32[]{:S(2)}) collective-permute-start(bf16[256,2048]{1,0:T(8,128)(2,1)} %shard_map.290.second_ref), channel_id=1, source_target_pairs={{8,0},{12,4},{16,24},{20,28},{9,1},{13,5},{17,25},{21,29},{10,2},{... | collective-permute-start | bytes 3145736 | tf_op jit(solution)/shard_map/ppermute | solution.py:348
  773.8 41.8 %collective-permute-start.98 = (bf16[2048,256]{1,0:T(8,128)(2,1)S(1)}, bf16[2048,256]{1,0:T(8,128)(2,1)}, u32[]{:S(2)}, u32[]{:S(2)}) collective-permute-start(bf16[2048,256]{1,0:T(8,128)(2,1)S(1)} %shard_map.295.left_ref), channel_id=1, source_target_pairs={{8,16},{12,20},{16,8},{20,12},{9,17},{13,21},{17,9},{21,13},{10,18... | collective-permute-start | bytes 3145736 | tf_op jit(solution)/shard_map/ppermute | solution.py:348
  792.3 40.2 %collective-permute-start.105 = (bf16[2048,256]{1,0:T(8,128)(2,1)}, bf16[2048,256]{1,0:T(8,128)(2,1)}, u32[]{:S(2)}, u32[]{:S(2)}) collective-permute-start(bf16[2048,256]{1,0:T(8,128)(2,1)} %shard_map.296.second_ref), channel_id=1, source_target_pairs={{8,0},{12,4},{16,24},{20,28},{9,1},{13,5},{17,25},{21,29},{10,2},{... | collective-permute-start | bytes 3145736 | tf_op jit(solution)/shard_map/ppermute | solution.py:348
  793.8 47.7 %collective-permute-start.106 = (bf16[2048,256]{1,0:T(8,128)(2,1)}, bf16[2048,256]{1,0:T(8,128)(2,1)}, u32[]{:S(2)}, u32[]{:S(2)}) collective-permute-start(bf16[2048,256]{1,0:T(8,128)(2,1)} %get-tuple-element.1332), channel_id=1, source_target_pairs={{0,4},{4,0},{8,12},{12,8},{16,20},{20,16},{24,28},{28,24},{1,5},{5... | collective-permute-start | bytes 3145736 | tf_op jit(solution)/shard_map/ppermute | solution.py:348
  (190 other events, 2476.0 us)
